TPU v7x, 256 devices: a whole 4x4x8 slice. The times are simulated.
256 devices in a mesh: tm: 32 (over x, z_hi, core), space: 8 (over y, z_lo).
Axes of the slice: x: 4, y: 4, z: 8 (z_hi: 4, z_lo: 2; z = z_hi * 2 + z_lo), core: 2. Of those that a mesh axis runs over, the one named last changes fastest.
Arguments:
- primal: float32 [256, 5, 64, 16, 128], P('tm', None, 'space'), may hold values from -2 to 2
- source: float32 [256, 5, 64, 16, 128], P('tm', None, 'space'), may hold values from -4 to 4
- guess: float32 [32, 5, 64, 16, 128], P('tm', None, 'space'), may hold values from -6 to 6
- mixing: float32 [5, 5], replicated, may hold values from -1 to 1.2
Outputs:
- fine_states: float32 [256, 5, 64, 16, 128], P('tm', None, 'space')
- coarse_residual: float32 [32, 5, 64, 16, 128], P('tm', None, 'space')
All inputs are finite; a program needn't handle non-finite values.
Results may differ from a plain program's by a relative error of at most 0.00026.
Values sent between devices are 32-bit elements; how exact they have to be, the bound alone decides.
No kernel may reach another device: no remote copies, remote signals or barrier semaphores. Data moves between devices by JAX's collectives and lax.ppermute only.
A program may use at most 64 MiB of HBM per device.

v0:
```python
import jax
import jax.numpy as jnp
from jax import lax
from jax.sharding import PartitionSpec as P

STEPS = 8


DIFFUSION = 0.1
RATE = 0.25
COARSE_STEP = 0.75


def padded_2(block, sides, width):
    for axis, dim in sides:
        count = lax.axis_size(axis)
        forward = [(i, i + 1) for i in range(count - 1)]
        forward.append((count - 1, 0))
        backward = [(target, source) for source, target in forward]
        low = lax.ppermute(
            lax.slice_in_dim(block, block.shape[dim] - width, None, axis=dim), axis, forward
        )
        high = lax.ppermute(lax.slice_in_dim(block, 0, width, axis=dim), axis, backward)
        block = jnp.concatenate([low, block, high], axis=dim)
    return block


def from_behind(array, axis, by):
    count = lax.axis_size(axis)
    pairs = [(i, i + by) for i in range(count) if 0 <= i + by < count]
    return lax.ppermute(array, axis, pairs)


def apply_mix(mixing, field):
    return jnp.einsum("ij,...jxyz->...ixyz", mixing, field, precision=lax.Precision.HIGHEST)


def slopes(mixing, state):
    tilted = jnp.tanh(apply_mix(mixing, state))
    return 1.0 - tilted * tilted


def laplace(field, across):
    widths = [(0, 0)] * (field.ndim - 2) + [(1, 1), (0, 0)]
    padded = jnp.pad(field, widths)
    total = across + padded[..., 2:, :] + padded[..., :-2, :]
    total = total + jnp.roll(field, 1, -1) + jnp.roll(field, -1, -1)
    return total - 6.0 * field


def stencil_step(mixing, slope, field, across):
    return (
        field
        + DIFFUSION * laplace(field, across)
        + RATE * (slope * apply_mix(mixing, field) - field)
    )


def march_near(mixing, slope_table, source, start, count):
    field = start
    marched = []
    for column in range(count):
        padded = padded_2(field, (("space", 1),), 1)
        across = padded[:, 2:] + padded[:, :-2]
        field = stencil_step(mixing, slope_table[column], field, across)
        if column + 1 < STEPS:
            field = field + source[column + 1]
        marched.append(field)
    return marched


def receive_end(ended):
    return from_behind(ended, "tm", 1)


def per_device(primal, source, guess, mixing):
    position = lax.axis_index("tm")
    leading = position == 0
    slope_table = slopes(mixing, primal)

    def march(start, count):
        return march_near(mixing, slope_table, source, start, count)

    start = guess[0]
    ended = march(start, STEPS)[-1]
    relaxed = jnp.where(leading, start, receive_end(ended) + source[0])
    ended_again = march(relaxed, STEPS)[-1]
    residual = jnp.where(leading, source[0], receive_end(ended_again) + source[0] - relaxed)
    coarse_slope = slope_table[0]

    def coarse_turn(turn, error):
        moved = error + COARSE_STEP * (coarse_slope * apply_mix(mixing, error) - error)
        arrived = from_behind(moved, "tm", 1)
        return jnp.where(position == turn, arrived + residual, error)

    initial = jnp.where(leading, residual, jnp.zeros_like(residual))
    error = lax.fori_loop(1, lax.axis_size("tm"), coarse_turn, initial)
    corrected = relaxed + error
    finals = march(corrected, STEPS - 1)
    fine_states = jnp.stack([corrected] + finals, axis=0)
    return (fine_states, residual[None])


def solution(mesh):
    placed = (
        P("tm", None, "space", None, None),
        P("tm", None, "space", None, None),
        P("tm", None, "space", None, None),
        P(),
    )
    return jax.shard_map(
        per_device,
        mesh=mesh,
        in_specs=placed,
        out_specs=(P("tm", None, "space", None, None), P("tm", None, "space", None, None)),
        check_vma=False,
    )
```

profile of v0, /device:TPU:6, one launch (start us, length us, event | category | flops | bytes accessed | tf_op | source)
XLA Modules:
  0.0 782.0 jit_solution(15624162312508072852)
XLA Ops:
  85.2 17.6 %collective-permute-done.17 = f32[5,8,16,128]{3,0,2,1:T(8,128)} collective-permute-done((f32[5,8,16,128]{3,0,2,1:T(8,128)}, f32[5,8,16,128]{3,0,2,1:T(8,128)}, u32[]{:S(2)}, u32[]{:S(2)}) %collective-permute-start.17) | collective-permute-done | bytes 327712 | tf_op jit(solution)/shard_map/ppermute | solution.py:31
  180.9 15.0 %collective-permute-done.34 = f32[5,8,16,128]{3,0,2,1:T(8,128)S(1)} collective-permute-done((f32[5,8,16,128]{3,0,2,1:T(8,128)S(1)}, f32[5,8,16,128]{3,0,2,1:T(8,128)S(1)}, u32[]{:S(2)}, u32[]{:S(2)}) %collective-permute-start.34) | collective-permute-done | bytes 327712 | tf_op jit(solution)/shard_map/ppermute | solution.py:31
  196.2 508.3 %while.13 = (s32[]{:T(128)}, f32[5,8,16,128]{3,0,2,1:T(8,128)S(1)}, s32[]{:T(128)}, f32[5,5]{1,0:T(8,128)S(1)}, f32[5,8,16,128]{3,0,2,1:T(8,128)S(1)}, /*index=5*/f32[5,8,16,128]{3,0,2,1:T(8,128)S(1)}, s32[]{:T(128)}) while((s32[]{:T(128)}, f32[5,8,16,128]{3,0,2,1:T(8,128)S(1)}, s32[]{:T(128)}, f32[5,5]{1,0:T(8,128)S(1)}, ...), condition=%wide.region_1.2_spmd, body=%wide.region_0.1_spmd.sunk | while | flops 5406723 | bytes 3604707 | solution.py:97
  198.7 15.5 %collective-permute-done = f32[5,8,16,128]{3,0,2,1:T(8,128)S(1)} collective-permute-done((f32[5,8,16,128]{3,0,2,1:T(8,128)S(1)}, f32[5,8,16,128]{3,0,2,1:T(8,128)S(1)}, u32[]{:S(2)}, u32[]{:S(2)}) %collective-permute-start) | collective-permute-done | bytes 327712 | tf_op jit(solution)/shard_map/while/body/eval_jaxpr/ppermute | solution.py:31
  217.0 17.2 %collective-permute-done = f32[5,8,16,128]{3,0,2,1:T(8,128)S(1)} collective-permute-done((f32[5,8,16,128]{3,0,2,1:T(8,128)S(1)}, f32[5,8,16,128]{3,0,2,1:T(8,128)S(1)}, u32[]{:S(2)}, u32[]{:S(2)}) %collective-permute-start) | collective-permute-done | bytes 327712 | tf_op jit(solution)/shard_map/while/body/eval_jaxpr/ppermute | solution.py:31
  236.9 11.7 %collective-permute-done = f32[5,8,16,128]{3,0,2,1:T(8,128)S(1)} collective-permute-done((f32[5,8,16,128]{3,0,2,1:T(8,128)S(1)}, f32[5,8,16,128]{3,0,2,1:T(8,128)S(1)}, u32[]{:S(2)}, u32[]{:S(2)}) %collective-permute-start) | collective-permute-done | bytes 327712 | tf_op jit(solution)/shard_map/while/body/eval_jaxpr/ppermute | solution.py:31
  251.4 11.7 %collective-permute-done = f32[5,8,16,128]{3,0,2,1:T(8,128)S(1)} collective-permute-done((f32[5,8,16,128]{3,0,2,1:T(8,128)S(1)}, f32[5,8,16,128]{3,0,2,1:T(8,128)S(1)}, u32[]{:S(2)}, u32[]{:S(2)}) %collective-permute-start) | collective-permute-done | bytes 327712 | tf_op jit(solution)/shard_map/while/body/eval_jaxpr/ppermute | solution.py:31
  280.1 11.6 %collective-permute-done = f32[5,8,16,128]{3,0,2,1:T(8,128)S(1)} collective-permute-done((f32[5,8,16,128]{3,0,2,1:T(8,128)S(1)}, f32[5,8,16,128]{3,0,2,1:T(8,128)S(1)}, u32[]{:S(2)}, u32[]{:S(2)}) %collective-permute-start) | collective-permute-done | bytes 327712 | tf_op jit(solution)/shard_map/while/body/eval_jaxpr/ppermute | solution.py:31
  294.5 12.1 %collective-permute-done = f32[5,8,16,128]{3,0,2,1:T(8,128)S(1)} collective-permute-done((f32[5,8,16,128]{3,0,2,1:T(8,128)S(1)}, f32[5,8,16,128]{3,0,2,1:T(8,128)S(1)}, u32[]{:S(2)}, u32[]{:S(2)}) %collective-permute-start) | collective-permute-done | bytes 327712 | tf_op jit(solution)/shard_map/while/body/eval_jaxpr/ppermute | solution.py:31
  309.3 16.5 %collective-permute-done = f32[5,8,16,128]{3,0,2,1:T(8,128)S(1)} collective-permute-done((f32[5,8,16,128]{3,0,2,1:T(8,128)S(1)}, f32[5,8,16,128]{3,0,2,1:T(8,128)S(1)}, u32[]{:S(2)}, u32[]{:S(2)}) %collective-permute-start) | collective-permute-done | bytes 327712 | tf_op jit(solution)/shard_map/while/body/eval_jaxpr/ppermute | solution.py:31
  328.6 14.0 %collective-permute-done = f32[5,8,16,128]{3,0,2,1:T(8,128)S(1)} collective-permute-done((f32[5,8,16,128]{3,0,2,1:T(8,128)S(1)}, f32[5,8,16,128]{3,0,2,1:T(8,128)S(1)}, u32[]{:S(2)}, u32[]{:S(2)}) %collective-permute-start) | collective-permute-done | bytes 327712 | tf_op jit(solution)/shard_map/while/body/eval_jaxpr/ppermute | solution.py:31
  359.7 12.6 %collective-permute-done = f32[5,8,16,128]{3,0,2,1:T(8,128)S(1)} collective-permute-done((f32[5,8,16,128]{3,0,2,1:T(8,128)S(1)}, f32[5,8,16,128]{3,0,2,1:T(8,128)S(1)}, u32[]{:S(2)}, u32[]{:S(2)}) %collective-permute-start) | collective-permute-done | bytes 327712 | tf_op jit(solution)/shard_map/while/body/eval_jaxpr/ppermute | solution.py:31
  375.1 12.8 %collective-permute-done = f32[5,8,16,128]{3,0,2,1:T(8,128)S(1)} collective-permute-done((f32[5,8,16,128]{3,0,2,1:T(8,128)S(1)}, f32[5,8,16,128]{3,0,2,1:T(8,128)S(1)}, u32[]{:S(2)}, u32[]{:S(2)}) %collective-permute-start) | collective-permute-done | bytes 327712 | tf_op jit(solution)/shard_map/while/body/eval_jaxpr/ppermute | solution.py:31
  390.7 15.1 %collective-permute-done = f32[5,8,16,128]{3,0,2,1:T(8,128)S(1)} collective-permute-done((f32[5,8,16,128]{3,0,2,1:T(8,128)S(1)}, f32[5,8,16,128]{3,0,2,1:T(8,128)S(1)}, u32[]{:S(2)}, u32[]{:S(2)}) %collective-permute-start) | collective-permute-done | bytes 327712 | tf_op jit(solution)/shard_map/while/body/eval_jaxpr/ppermute | solution.py:31
  408.5 13.6 %collective-permute-done = f32[5,8,16,128]{3,0,2,1:T(8,128)S(1)} collective-permute-done((f32[5,8,16,128]{3,0,2,1:T(8,128)S(1)}, f32[5,8,16,128]{3,0,2,1:T(8,128)S(1)}, u32[]{:S(2)}, u32[]{:S(2)}) %collective-permute-start) | collective-permute-done | bytes 327712 | tf_op jit(solution)/shard_map/while/body/eval_jaxpr/ppermute | solution.py:31
  424.8 12.8 %collective-permute-done = f32[5,8,16,128]{3,0,2,1:T(8,128)S(1)} collective-permute-done((f32[5,8,16,128]{3,0,2,1:T(8,128)S(1)}, f32[5,8,16,128]{3,0,2,1:T(8,128)S(1)}, u32[]{:S(2)}, u32[]{:S(2)}) %collective-permute-start) | collective-permute-done | bytes 327712 | tf_op jit(solution)/shard_map/while/body/eval_jaxpr/ppermute | solution.py:31
  440.4 15.1 %collective-permute-done = f32[5,8,16,128]{3,0,2,1:T(8,128)S(1)} collective-permute-done((f32[5,8,16,128]{3,0,2,1:T(8,128)S(1)}, f32[5,8,16,128]{3,0,2,1:T(8,128)S(1)}, u32[]{:S(2)}, u32[]{:S(2)}) %collective-permute-start) | collective-permute-done | bytes 327712 | tf_op jit(solution)/shard_map/while/body/eval_jaxpr/ppermute | solution.py:31
  458.2 13.6 %collective-permute-done = f32[5,8,16,128]{3,0,2,1:T(8,128)S(1)} collective-permute-done((f32[5,8,16,128]{3,0,2,1:T(8,128)S(1)}, f32[5,8,16,128]{3,0,2,1:T(8,128)S(1)}, u32[]{:S(2)}, u32[]{:S(2)}) %collective-permute-start) | collective-permute-done | bytes 327712 | tf_op jit(solution)/shard_map/while/body/eval_jaxpr/ppermute | solution.py:31
  474.6 12.8 %collective-permute-done = f32[5,8,16,128]{3,0,2,1:T(8,128)S(1)} collective-permute-done((f32[5,8,16,128]{3,0,2,1:T(8,128)S(1)}, f32[5,8,16,128]{3,0,2,1:T(8,128)S(1)}, u32[]{:S(2)}, u32[]{:S(2)}) %collective-permute-start) | collective-permute-done | bytes 327712 | tf_op jit(solution)/shard_map/while/body/eval_jaxpr/ppermute | solution.py:31
  490.2 15.1 %collective-permute-done = f32[5,8,16,128]{3,0,2,1:T(8,128)S(1)} collective-permute-done((f32[5,8,16,128]{3,0,2,1:T(8,128)S(1)}, f32[5,8,16,128]{3,0,2,1:T(8,128)S(1)}, u32[]{:S(2)}, u32[]{:S(2)}) %collective-permute-start) | collective-permute-done | bytes 327712 | tf_op jit(solution)/shard_map/while/body/eval_jaxpr/ppermute | solution.py:31
  508.0 13.6 %collective-permute-done = f32[5,8,16,128]{3,0,2,1:T(8,128)S(1)} collective-permute-done((f32[5,8,16,128]{3,0,2,1:T(8,128)S(1)}, f32[5,8,16,128]{3,0,2,1:T(8,128)S(1)}, u32[]{:S(2)}, u32[]{:S(2)}) %collective-permute-start) | collective-permute-done | bytes 327712 | tf_op jit(solution)/shard_map/while/body/eval_jaxpr/ppermute | solution.py:31
  524.3 12.8 %collective-permute-done = f32[5,8,16,128]{3,0,2,1:T(8,128)S(1)} collective-permute-done((f32[5,8,16,128]{3,0,2,1:T(8,128)S(1)}, f32[5,8,16,128]{3,0,2,1:T(8,128)S(1)}, u32[]{:S(2)}, u32[]{:S(2)}) %collective-permute-start) | collective-permute-done | bytes 327712 | tf_op jit(solution)/shard_map/while/body/eval_jaxpr/ppermute | solution.py:31
  539.9 15.1 %collective-permute-done = f32[5,8,16,128]{3,0,2,1:T(8,128)S(1)} collective-permute-done((f32[5,8,16,128]{3,0,2,1:T(8,128)S(1)}, f32[5,8,16,128]{3,0,2,1:T(8,128)S(1)}, u32[]{:S(2)}, u32[]{:S(2)}) %collective-permute-start) | collective-permute-done | bytes 327712 | tf_op jit(solution)/shard_map/while/body/eval_jaxpr/ppermute | solution.py:31
  557.7 13.6 %collective-permute-done = f32[5,8,16,128]{3,0,2,1:T(8,128)S(1)} collective-permute-done((f32[5,8,16,128]{3,0,2,1:T(8,128)S(1)}, f32[5,8,16,128]{3,0,2,1:T(8,128)S(1)}, u32[]{:S(2)}, u32[]{:S(2)}) %collective-permute-start) | collective-permute-done | bytes 327712 | tf_op jit(solution)/shard_map/while/body/eval_jaxpr/ppermute | solution.py:31
  574.1 12.8 %collective-permute-done = f32[5,8,16,128]{3,0,2,1:T(8,128)S(1)} collective-permute-done((f32[5,8,16,128]{3,0,2,1:T(8,128)S(1)}, f32[5,8,16,128]{3,0,2,1:T(8,128)S(1)}, u32[]{:S(2)}, u32[]{:S(2)}) %collective-permute-start) | collective-permute-done | bytes 327712 | tf_op jit(solution)/shard_map/while/body/eval_jaxpr/ppermute | solution.py:31
  589.7 15.1 %collective-permute-done = f32[5,8,16,128]{3,0,2,1:T(8,128)S(1)} collective-permute-done((f32[5,8,16,128]{3,0,2,1:T(8,128)S(1)}, f32[5,8,16,128]{3,0,2,1:T(8,128)S(1)}, u32[]{:S(2)}, u32[]{:S(2)}) %collective-permute-start) | collective-permute-done | bytes 327712 | tf_op jit(solution)/shard_map/while/body/eval_jaxpr/ppermute | solution.py:31
  607.5 13.6 %collective-permute-done = f32[5,8,16,128]{3,0,2,1:T(8,128)S(1)} collective-permute-done((f32[5,8,16,128]{3,0,2,1:T(8,128)S(1)}, f32[5,8,16,128]{3,0,2,1:T(8,128)S(1)}, u32[]{:S(2)}, u32[]{:S(2)}) %collective-permute-start) | collective-permute-done | bytes 327712 | tf_op jit(solution)/shard_map/while/body/eval_jaxpr/ppermute | solution.py:31
  623.8 12.8 %collective-permute-done = f32[5,8,16,128]{3,0,2,1:T(8,128)S(1)} collective-permute-done((f32[5,8,16,128]{3,0,2,1:T(8,128)S(1)}, f32[5,8,16,128]{3,0,2,1:T(8,128)S(1)}, u32[]{:S(2)}, u32[]{:S(2)}) %collective-permute-start) | collective-permute-done | bytes 327712 | tf_op jit(solution)/shard_map/while/body/eval_jaxpr/ppermute | solution.py:31
  639.4 15.1 %collective-permute-done = f32[5,8,16,128]{3,0,2,1:T(8,128)S(1)} collective-permute-done((f32[5,8,16,128]{3,0,2,1:T(8,128)S(1)}, f32[5,8,16,128]{3,0,2,1:T(8,128)S(1)}, u32[]{:S(2)}, u32[]{:S(2)}) %collective-permute-start) | collective-permute-done | bytes 327712 | tf_op jit(solution)/shard_map/while/body/eval_jaxpr/ppermute | solution.py:31
  657.2 13.6 %collective-permute-done = f32[5,8,16,128]{3,0,2,1:T(8,128)S(1)} collective-permute-done((f32[5,8,16,128]{3,0,2,1:T(8,128)S(1)}, f32[5,8,16,128]{3,0,2,1:T(8,128)S(1)}, u32[]{:S(2)}, u32[]{:S(2)}) %collective-permute-start) | collective-permute-done | bytes 327712 | tf_op jit(solution)/shard_map/while/body/eval_jaxpr/ppermute | solution.py:31
  673.6 12.8 %collective-permute-done = f32[5,8,16,128]{3,0,2,1:T(8,128)S(1)} collective-permute-done((f32[5,8,16,128]{3,0,2,1:T(8,128)S(1)}, f32[5,8,16,128]{3,0,2,1:T(8,128)S(1)}, u32[]{:S(2)}, u32[]{:S(2)}) %collective-permute-start) | collective-permute-done | bytes 327712 | tf_op jit(solution)/shard_map/while/body/eval_jaxpr/ppermute | solution.py:31
  689.2 15.1 %collective-permute-done = f32[5,8,16,128]{3,0,2,1:T(8,128)S(1)} collective-permute-done((f32[5,8,16,128]{3,0,2,1:T(8,128)S(1)}, f32[5,8,16,128]{3,0,2,1:T(8,128)S(1)}, u32[]{:S(2)}, u32[]{:S(2)}) %collective-permute-start) | collective-permute-done | bytes 327712 | tf_op jit(solution)/shard_map/while/body/eval_jaxpr/ppermute | solution.py:31
  (322 shorter events, 347.0 us)
Async XLA Ops:
  83.3 19.5 %collective-permute-start.17 = (f32[5,8,16,128]{3,0,2,1:T(8,128)}, f32[5,8,16,128]{3,0,2,1:T(8,128)}, u32[]{:S(2)}, u32[]{:S(2)}) collective-permute-start(f32[5,8,16,128]{3,0,2,1:T(8,128)} %fusion.41), channel_id=1, source_target_pairs={{0,8},{8,16},{16,24},{24,32},{32,40},{40,48},{48,56},{56,64},{64,7... | collective-permute-start | bytes 983048 | tf_op jit(solution)/shard_map/ppermute | solution.py:31
  177.9 18.0 %collective-permute-start.34 = (f32[5,8,16,128]{3,0,2,1:T(8,128)S(1)}, f32[5,8,16,128]{3,0,2,1:T(8,128)S(1)}, u32[]{:S(2)}, u32[]{:S(2)}) collective-permute-start(f32[5,8,16,128]{3,0,2,1:T(8,128)S(1)} %fusion.78), channel_id=1, source_target_pairs={{0,8},{8,16},{16,24},{24,32},{32,40},{40,48},{48,56},{56,64},{64,7... | collective-permute-start | bytes 983048 | tf_op jit(solution)/shard_map/ppermute | solution.py:31
  196.8 17.5 %collective-permute-start = (f32[5,8,16,128]{3,0,2,1:T(8,128)S(1)}, f32[5,8,16,128]{3,0,2,1:T(8,128)S(1)}, u32[]{:S(2)}, u32[]{:S(2)}) collective-permute-start(f32[5,8,16,128]{3,0,2,1:T(8,128)S(1)} %fusion.435), channel_id=1, source_target_pairs={{0,8},{8,16},{16,24},{24,32},{32,40},{40,48},{48,56},{56,64},{64,7... | collective-permute-start | bytes 983048 | tf_op jit(solution)/shard_map/while/body/eval_jaxpr/ppermute | solution.py:31
  215.0 19.1 %collective-permute-start = (f32[5,8,16,128]{3,0,2,1:T(8,128)S(1)}, f32[5,8,16,128]{3,0,2,1:T(8,128)S(1)}, u32[]{:S(2)}, u32[]{:S(2)}) collective-permute-start(f32[5,8,16,128]{3,0,2,1:T(8,128)S(1)} %fusion.435), channel_id=1, source_target_pairs={{0,8},{8,16},{16,24},{24,32},{32,40},{40,48},{48,56},{56,64},{64,7... | collective-permute-start | bytes 983048 | tf_op jit(solution)/shard_map/while/body/eval_jaxpr/ppermute | solution.py:31
  235.0 13.6 %collective-permute-start = (f32[5,8,16,128]{3,0,2,1:T(8,128)S(1)}, f32[5,8,16,128]{3,0,2,1:T(8,128)S(1)}, u32[]{:S(2)}, u32[]{:S(2)}) collective-permute-start(f32[5,8,16,128]{3,0,2,1:T(8,128)S(1)} %fusion.435), channel_id=1, source_target_pairs={{0,8},{8,16},{16,24},{24,32},{32,40},{40,48},{48,56},{56,64},{64,7... | collective-permute-start | bytes 983048 | tf_op jit(solution)/shard_map/while/body/eval_jaxpr/ppermute | solution.py:31
  249.4 13.6 %collective-permute-start = (f32[5,8,16,128]{3,0,2,1:T(8,128)S(1)}, f32[5,8,16,128]{3,0,2,1:T(8,128)S(1)}, u32[]{:S(2)}, u32[]{:S(2)}) collective-permute-start(f32[5,8,16,128]{3,0,2,1:T(8,128)S(1)} %fusion.435), channel_id=1, source_target_pairs={{0,8},{8,16},{16,24},{24,32},{32,40},{40,48},{48,56},{56,64},{64,7... | collective-permute-start | bytes 983048 | tf_op jit(solution)/shard_map/while/body/eval_jaxpr/ppermute | solution.py:31
  263.9 13.5 %collective-permute-start = (f32[5,8,16,128]{3,0,2,1:T(8,128)S(1)}, f32[5,8,16,128]{3,0,2,1:T(8,128)S(1)}, u32[]{:S(2)}, u32[]{:S(2)}) collective-permute-start(f32[5,8,16,128]{3,0,2,1:T(8,128)S(1)} %fusion.435), channel_id=1, source_target_pairs={{0,8},{8,16},{16,24},{24,32},{32,40},{40,48},{48,56},{56,64},{64,7... | collective-permute-start | bytes 983048 | tf_op jit(solution)/shard_map/while/body/eval_jaxpr/ppermute | solution.py:31
  278.2 13.5 %collective-permute-start = (f32[5,8,16,128]{3,0,2,1:T(8,128)S(1)}, f32[5,8,16,128]{3,0,2,1:T(8,128)S(1)}, u32[]{:S(2)}, u32[]{:S(2)}) collective-permute-start(f32[5,8,16,128]{3,0,2,1:T(8,128)S(1)} %fusion.435), channel_id=1, source_target_pairs={{0,8},{8,16},{16,24},{24,32},{32,40},{40,48},{48,56},{56,64},{64,7... | collective-permute-start | bytes 983048 | tf_op jit(solution)/shard_map/while/body/eval_jaxpr/ppermute | solution.py:31
  292.5 14.1 %collective-permute-start = (f32[5,8,16,128]{3,0,2,1:T(8,128)S(1)}, f32[5,8,16,128]{3,0,2,1:T(8,128)S(1)}, u32[]{:S(2)}, u32[]{:S(2)}) collective-permute-start(f32[5,8,16,128]{3,0,2,1:T(8,128)S(1)} %fusion.435), channel_id=1, source_target_pairs={{0,8},{8,16},{16,24},{24,32},{32,40},{40,48},{48,56},{56,64},{64,7... | collective-permute-start | bytes 983048 | tf_op jit(solution)/shard_map/while/body/eval_jaxpr/ppermute | solution.py:31
  307.4 18.5 %collective-permute-start = (f32[5,8,16,128]{3,0,2,1:T(8,128)S(1)}, f32[5,8,16,128]{3,0,2,1:T(8,128)S(1)}, u32[]{:S(2)}, u32[]{:S(2)}) collective-permute-start(f32[5,8,16,128]{3,0,2,1:T(8,128)S(1)} %fusion.435), channel_id=1, source_target_pairs={{0,8},{8,16},{16,24},{24,32},{32,40},{40,48},{48,56},{56,64},{64,7... | collective-permute-start | bytes 983048 | tf_op jit(solution)/shard_map/while/body/eval_jaxpr/ppermute | solution.py:31
  326.7 15.9 %collective-permute-start = (f32[5,8,16,128]{3,0,2,1:T(8,128)S(1)}, f32[5,8,16,128]{3,0,2,1:T(8,128)S(1)}, u32[]{:S(2)}, u32[]{:S(2)}) collective-permute-start(f32[5,8,16,128]{3,0,2,1:T(8,128)S(1)} %fusion.435), channel_id=1, source_target_pairs={{0,8},{8,16},{16,24},{24,32},{32,40},{40,48},{48,56},{56,64},{64,7... | collective-permute-start | bytes 983048 | tf_op jit(solution)/shard_map/while/body/eval_jaxpr/ppermute | solution.py:31
  357.8 14.5 %collective-permute-start = (f32[5,8,16,128]{3,0,2,1:T(8,128)S(1)}, f32[5,8,16,128]{3,0,2,1:T(8,128)S(1)}, u32[]{:S(2)}, u32[]{:S(2)}) collective-permute-start(f32[5,8,16,128]{3,0,2,1:T(8,128)S(1)} %fusion.435), channel_id=1, source_target_pairs={{0,8},{8,16},{16,24},{24,32},{32,40},{40,48},{48,56},{56,64},{64,7... | collective-permute-start | bytes 983048 | tf_op jit(solution)/shard_map/while/body/eval_jaxpr/ppermute | solution.py:31
  373.1 14.8 %collective-permute-start = (f32[5,8,16,128]{3,0,2,1:T(8,128)S(1)}, f32[5,8,16,128]{3,0,2,1:T(8,128)S(1)}, u32[]{:S(2)}, u32[]{:S(2)}) collective-permute-start(f32[5,8,16,128]{3,0,2,1:T(8,128)S(1)} %fusion.435), channel_id=1, source_target_pairs={{0,8},{8,16},{16,24},{24,32},{32,40},{40,48},{48,56},{56,64},{64,7... | collective-permute-start | bytes 983048 | tf_op jit(solution)/shard_map/while/body/eval_jaxpr/ppermute | solution.py:31
  388.7 17.0 %collective-permute-start = (f32[5,8,16,128]{3,0,2,1:T(8,128)S(1)}, f32[5,8,16,128]{3,0,2,1:T(8,128)S(1)}, u32[]{:S(2)}, u32[]{:S(2)}) collective-permute-start(f32[5,8,16,128]{3,0,2,1:T(8,128)S(1)} %fusion.435), channel_id=1, source_target_pairs={{0,8},{8,16},{16,24},{24,32},{32,40},{40,48},{48,56},{56,64},{64,7... | collective-permute-start | bytes 983048 | tf_op jit(solution)/shard_map/while/body/eval_jaxpr/ppermute | solution.py:31
  406.6 15.5 %collective-permute-start = (f32[5,8,16,128]{3,0,2,1:T(8,128)S(1)}, f32[5,8,16,128]{3,0,2,1:T(8,128)S(1)}, u32[]{:S(2)}, u32[]{:S(2)}) collective-permute-start(f32[5,8,16,128]{3,0,2,1:T(8,128)S(1)} %fusion.435), channel_id=1, source_target_pairs={{0,8},{8,16},{16,24},{24,32},{32,40},{40,48},{48,56},{56,64},{64,7... | collective-permute-start | bytes 983048 | tf_op jit(solution)/shard_map/while/body/eval_jaxpr/ppermute | solution.py:31
  422.9 14.8 %collective-permute-start = (f32[5,8,16,128]{3,0,2,1:T(8,128)S(1)}, f32[5,8,16,128]{3,0,2,1:T(8,128)S(1)}, u32[]{:S(2)}, u32[]{:S(2)}) collective-permute-start(f32[5,8,16,128]{3,0,2,1:T(8,128)S(1)} %fusion.435), channel_id=1, source_target_pairs={{0,8},{8,16},{16,24},{24,32},{32,40},{40,48},{48,56},{56,64},{64,7... | collective-permute-start | bytes 983048 | tf_op jit(solution)/shard_map/while/body/eval_jaxpr/ppermute | solution.py:31
  438.5 17.0 %collective-permute-start = (f32[5,8,16,128]{3,0,2,1:T(8,128)S(1)}, f32[5,8,16,128]{3,0,2,1:T(8,128)S(1)}, u32[]{:S(2)}, u32[]{:S(2)}) collective-permute-start(f32[5,8,16,128]{3,0,2,1:T(8,128)S(1)} %fusion.435), channel_id=1, source_target_pairs={{0,8},{8,16},{16,24},{24,32},{32,40},{40,48},{48,56},{56,64},{64,7... | collective-permute-start | bytes 983048 | tf_op jit(solution)/shard_map/while/body/eval_jaxpr/ppermute | solution.py:31
  456.3 15.5 %collective-permute-start = (f32[5,8,16,128]{3,0,2,1:T(8,128)S(1)}, f32[5,8,16,128]{3,0,2,1:T(8,128)S(1)}, u32[]{:S(2)}, u32[]{:S(2)}) collective-permute-start(f32[5,8,16,128]{3,0,2,1:T(8,128)S(1)} %fusion.435), channel_id=1, source_target_pairs={{0,8},{8,16},{16,24},{24,32},{32,40},{40,48},{48,56},{56,64},{64,7... | collective-permute-start | bytes 983048 | tf_op jit(solution)/shard_map/while/body/eval_jaxpr/ppermute | solution.py:31
  472.6 14.8 %collective-permute-start = (f32[5,8,16,128]{3,0,2,1:T(8,128)S(1)}, f32[5,8,16,128]{3,0,2,1:T(8,128)S(1)}, u32[]{:S(2)}, u32[]{:S(2)}) collective-permute-start(f32[5,8,16,128]{3,0,2,1:T(8,128)S(1)} %fusion.435), channel_id=1, source_target_pairs={{0,8},{8,16},{16,24},{24,32},{32,40},{40,48},{48,56},{56,64},{64,7... | collective-permute-start | bytes 983048 | tf_op jit(solution)/shard_map/while/body/eval_jaxpr/ppermute | solution.py:31
  488.2 17.0 %collective-permute-start = (f32[5,8,16,128]{3,0,2,1:T(8,128)S(1)}, f32[5,8,16,128]{3,0,2,1:T(8,128)S(1)}, u32[]{:S(2)}, u32[]{:S(2)}) collective-permute-start(f32[5,8,16,128]{3,0,2,1:T(8,128)S(1)} %fusion.435), channel_id=1, source_target_pairs={{0,8},{8,16},{16,24},{24,32},{32,40},{40,48},{48,56},{56,64},{64,7... | collective-permute-start | bytes 983048 | tf_op jit(solution)/shard_map/while/body/eval_jaxpr/ppermute | solution.py:31
  506.1 15.5 %collective-permute-start = (f32[5,8,16,128]{3,0,2,1:T(8,128)S(1)}, f32[5,8,16,128]{3,0,2,1:T(8,128)S(1)}, u32[]{:S(2)}, u32[]{:S(2)}) collective-permute-start(f32[5,8,16,128]{3,0,2,1:T(8,128)S(1)} %fusion.435), channel_id=1, source_target_pairs={{0,8},{8,16},{16,24},{24,32},{32,40},{40,48},{48,56},{56,64},{64,7... | collective-permute-start | bytes 983048 | tf_op jit(solution)/shard_map/while/body/eval_jaxpr/ppermute | solution.py:31
  522.4 14.8 %collective-permute-start = (f32[5,8,16,128]{3,0,2,1:T(8,128)S(1)}, f32[5,8,16,128]{3,0,2,1:T(8,128)S(1)}, u32[]{:S(2)}, u32[]{:S(2)}) collective-permute-start(f32[5,8,16,128]{3,0,2,1:T(8,128)S(1)} %fusion.435), channel_id=1, source_target_pairs={{0,8},{8,16},{16,24},{24,32},{32,40},{40,48},{48,56},{56,64},{64,7... | collective-permute-start | bytes 983048 | tf_op jit(solution)/shard_map/while/body/eval_jaxpr/ppermute | solution.py:31
  538.0 17.0 %collective-permute-start = (f32[5,8,16,128]{3,0,2,1:T(8,128)S(1)}, f32[5,8,16,128]{3,0,2,1:T(8,128)S(1)}, u32[]{:S(2)}, u32[]{:S(2)}) collective-permute-start(f32[5,8,16,128]{3,0,2,1:T(8,128)S(1)} %fusion.435), channel_id=1, source_target_pairs={{0,8},{8,16},{16,24},{24,32},{32,40},{40,48},{48,56},{56,64},{64,7... | collective-permute-start | bytes 983048 | tf_op jit(solution)/shard_map/while/body/eval_jaxpr/ppermute | solution.py:31
  555.8 15.5 %collective-permute-start = (f32[5,8,16,128]{3,0,2,1:T(8,128)S(1)}, f32[5,8,16,128]{3,0,2,1:T(8,128)S(1)}, u32[]{:S(2)}, u32[]{:S(2)}) collective-permute-start(f32[5,8,16,128]{3,0,2,1:T(8,128)S(1)} %fusion.435), channel_id=1, source_target_pairs={{0,8},{8,16},{16,24},{24,32},{32,40},{40,48},{48,56},{56,64},{64,7... | collective-permute-start | bytes 983048 | tf_op jit(solution)/shard_map/while/body/eval_jaxpr/ppermute | solution.py:31
  572.1 14.8 %collective-permute-start = (f32[5,8,16,128]{3,0,2,1:T(8,128)S(1)}, f32[5,8,16,128]{3,0,2,1:T(8,128)S(1)}, u32[]{:S(2)}, u32[]{:S(2)}) collective-permute-start(f32[5,8,16,128]{3,0,2,1:T(8,128)S(1)} %fusion.435), channel_id=1, source_target_pairs={{0,8},{8,16},{16,24},{24,32},{32,40},{40,48},{48,56},{56,64},{64,7... | collective-permute-start | bytes 983048 | tf_op jit(solution)/shard_map/while/body/eval_jaxpr/ppermute | solution.py:31
  587.7 17.0 %collective-permute-start = (f32[5,8,16,128]{3,0,2,1:T(8,128)S(1)}, f32[5,8,16,128]{3,0,2,1:T(8,128)S(1)}, u32[]{:S(2)}, u32[]{:S(2)}) collective-permute-start(f32[5,8,16,128]{3,0,2,1:T(8,128)S(1)} %fusion.435), channel_id=1, source_target_pairs={{0,8},{8,16},{16,24},{24,32},{32,40},{40,48},{48,56},{56,64},{64,7... | collective-permute-start | bytes 983048 | tf_op jit(solution)/shard_map/while/body/eval_jaxpr/ppermute | solution.py:31
  605.5 15.5 %collective-permute-start = (f32[5,8,16,128]{3,0,2,1:T(8,128)S(1)}, f32[5,8,16,128]{3,0,2,1:T(8,128)S(1)}, u32[]{:S(2)}, u32[]{:S(2)}) collective-permute-start(f32[5,8,16,128]{3,0,2,1:T(8,128)S(1)} %fusion.435), channel_id=1, source_target_pairs={{0,8},{8,16},{16,24},{24,32},{32,40},{40,48},{48,56},{56,64},{64,7... | collective-permute-start | bytes 983048 | tf_op jit(solution)/shard_map/while/body/eval_jaxpr/ppermute | solution.py:31
  621.9 14.8 %collective-permute-start = (f32[5,8,16,128]{3,0,2,1:T(8,128)S(1)}, f32[5,8,16,128]{3,0,2,1:T(8,128)S(1)}, u32[]{:S(2)}, u32[]{:S(2)}) collective-permute-start(f32[5,8,16,128]{3,0,2,1:T(8,128)S(1)} %fusion.435), channel_id=1, source_target_pairs={{0,8},{8,16},{16,24},{24,32},{32,40},{40,48},{48,56},{56,64},{64,7... | collective-permute-start | bytes 983048 | tf_op jit(solution)/shard_map/while/body/eval_jaxpr/ppermute | solution.py:31
  637.5 17.0 %collective-permute-start = (f32[5,8,16,128]{3,0,2,1:T(8,128)S(1)}, f32[5,8,16,128]{3,0,2,1:T(8,128)S(1)}, u32[]{:S(2)}, u32[]{:S(2)}) collective-permute-start(f32[5,8,16,128]{3,0,2,1:T(8,128)S(1)} %fusion.435), channel_id=1, source_target_pairs={{0,8},{8,16},{16,24},{24,32},{32,40},{40,48},{48,56},{56,64},{64,7... | collective-permute-start | bytes 983048 | tf_op jit(solution)/shard_map/while/body/eval_jaxpr/ppermute | solution.py:31
  655.3 15.5 %collective-permute-start = (f32[5,8,16,128]{3,0,2,1:T(8,128)S(1)}, f32[5,8,16,128]{3,0,2,1:T(8,128)S(1)}, u32[]{:S(2)}, u32[]{:S(2)}) collective-permute-start(f32[5,8,16,128]{3,0,2,1:T(8,128)S(1)} %fusion.435), channel_id=1, source_target_pairs={{0,8},{8,16},{16,24},{24,32},{32,40},{40,48},{48,56},{56,64},{64,7... | collective-permute-start | bytes 983048 | tf_op jit(solution)/shard_map/while/body/eval_jaxpr/ppermute | solution.py:31
  671.6 14.8 %collective-permute-start = (f32[5,8,16,128]{3,0,2,1:T(8,128)S(1)}, f32[5,8,16,128]{3,0,2,1:T(8,128)S(1)}, u32[]{:S(2)}, u32[]{:S(2)}) collective-permute-start(f32[5,8,16,128]{3,0,2,1:T(8,128)S(1)} %fusion.435), channel_id=1, source_target_pairs={{0,8},{8,16},{16,24},{24,32},{32,40},{40,48},{48,56},{56,64},{64,7... | collective-permute-start | bytes 983048 | tf_op jit(solution)/shard_map/while/body/eval_jaxpr/ppermute | solution.py:31
  687.2 17.0 %collective-permute-start = (f32[5,8,16,128]{3,0,2,1:T(8,128)S(1)}, f32[5,8,16,128]{3,0,2,1:T(8,128)S(1)}, u32[]{:S(2)}, u32[]{:S(2)}) collective-permute-start(f32[5,8,16,128]{3,0,2,1:T(8,128)S(1)} %fusion.435), channel_id=1, source_target_pairs={{0,8},{8,16},{16,24},{24,32},{32,40},{40,48},{48,56},{56,64},{64,7... | collective-permute-start | bytes 983048 | tf_op jit(solution)/shard_map/while/body/eval_jaxpr/ppermute | solution.py:31
  (63 other events, 1132.4 us)
where the time goes:
time: 794 us; the launch traced here: 782 us
  waiting for transfers between devices  555 us (70%)
  starting transfers between devices  126 us (16%)
  matrix products  74.3 us (9%)
  local copies, waits for them, and re-layouts  15.5 us (2%)
  other arithmetic  8.07 us (1%)
    ppermute x33, waiting for transfers between devices, from_behind(): return lax.ppermute(array, axis, pairs)  455 us
    dot_general x55, matrix products, apply_mix(): jnp.einsum('ij,...jxyz->...ixyz', mixing, field, precision=lax.Precision....  74.3 us
    ppermute x33, starting transfers between devices, from_behind(): return lax.ppermute(array, axis, pairs)  63.4 us
    ppermute x23, waiting for transfers between devices, padded_2(): lax.ppermute(lax.slice_in_dim(block, block.shape[dim] - width, None, axis...  55 us
    ppermute x23, waiting for transfers between devices, padded_2(): lax.ppermute(lax.slice_in_dim(block, 0, width, axis=dim), axis, backward)  45 us
    ppermute x23, starting transfers between devices, padded_2(): lax.ppermute(lax.slice_in_dim(block, block.shape[dim] - width, None, axis...  39.1 us
    ppermute x23, starting transfers between devices, padded_2(): lax.ppermute(lax.slice_in_dim(block, 0, width, axis=dim), axis, backward)  23.6 us
  transfers between devices with their start and end apart: 79, of which 77 were waited for; matrix products, arithmetic and copies ran while one was open for 2% of the time, Pallas kernels for 0%

commit v1 on v0

v1 whole, which is shorter than its diff:
```python
import functools

import jax
import jax.numpy as jnp
from jax import lax
from jax.experimental import pallas as pl
from jax.experimental.pallas import tpu as pltpu
from jax.sharding import PartitionSpec as P

STEPS = 8
FIELDS = 5
WIDE = 8
DIFFUSION = 0.1
RATE = 0.25
COARSE_STEP = 0.75
KEEP = 1.0 - 6.0 * DIFFUSION - RATE
REACH = [min(m, STEPS - 1 - m) for m in range(STEPS)]
REACH_AT = [sum(REACH[:m]) for m in range(STEPS)]
PACKED = sum(REACH)
HALO = max(min(m + 1, STEPS - 1 - m) for m in range(STEPS))


def mixed(mix, fields):
    out = []
    for i in range(FIELDS):
        total = mix[i][0] * fields[0]
        for j in range(1, FIELDS):
            total = total + mix[i][j] * fields[j]
        out.append(total)
    return out


def scalars(mix_ref):
    return [[mix_ref[i, j] for j in range(FIELDS)] for i in range(FIELDS)]


def stepped(mix, field, beside, slope, source):
    row = lax.broadcasted_iota(jnp.int32, (16, 128), 0)
    first, last = row == 0, row == 15
    out = []
    for f, turned in enumerate(mixed(mix, field)):
        v = field[f]
        around = pltpu.roll(v, 1, 1) + pltpu.roll(v, 127, 1)
        around = around + jnp.where(first, 0.0, pltpu.roll(v, 1, 0))
        around = around + jnp.where(last, 0.0, pltpu.roll(v, 15, 0))
        if beside is not None:
            around = around + beside[f]
        new = KEEP * v + DIFFUSION * around + slope[f] * turned
        out.append(new if source is None else new + source[f])
    return out


def prepare_kernel(mix_ref, primal_ref, slope_ref, up_ref, down_ref):
    mix = scalars(mix_ref)

    def plane(n, carry):
        t, x = n // WIDE, n % WIDE
        for f, value in enumerate(mixed(mix, [primal_ref[t, f, x] for f in range(FIELDS)])):
            tilted = jnp.tanh(value)
            slope_ref[t, f, x] = RATE - RATE * (tilted * tilted)
        return carry

    lax.fori_loop(0, STEPS * WIDE, plane, 0)
    for f in range(FIELDS):
        for m in range(STEPS):
            n, a = REACH[m], REACH_AT[m]
            if n > 0:
                up_ref[f, a : a + n] = slope_ref[m, f, WIDE - n :]
                down_ref[f, a : a + n] = slope_ref[m, f, :n]


def alone_kernel(count, mix_ref, start_ref, slope_ref, source_ref, up_ref, down_ref, one, two):
    mix = scalars(mix_ref)
    for f in range(FIELDS):
        down_ref[f, 0] = start_ref[f, 0]
        up_ref[f, 0] = start_ref[f, WIDE - 1]
    buffers = (one, two)
    for m in range(count - 1):
        here = start_ref if m == 0 else buffers[m % 2]
        there = buffers[(m + 1) % 2]
        for x in range(WIDE):
            if not (x >= m + 1 or x <= WIDE - 2 - m):
                continue
            field = [here[f, x] for f in range(FIELDS)]
            if x == 0:
                beside = [here[f, 1] for f in range(FIELDS)]
            elif x == WIDE - 1:
                beside = [here[f, WIDE - 2] for f in range(FIELDS)]
            else:
                beside = [here[f, x - 1] + here[f, x + 1] for f in range(FIELDS)]
            new = stepped(
                mix,
                field,
                beside,
                [slope_ref[m, f, x] for f in range(FIELDS)],
                [source_ref[m + 1, f, x] for f in range(FIELDS)],
            )
            for f in range(FIELDS):
                there[f, x] = new[f]
                if x == 0:
                    down_ref[f, m + 1] = new[f]
                if x == WIDE - 1:
                    up_ref[f, m + 1] = new[f]


def march_kernel(count, keep_all, mix_ref, start_ref, low_ref, high_ref, slope_ref, source_ref, packed_low, packed_high, out_ref, one, two, added_one, added_two):
    mix = scalars(mix_ref)
    fields = range(FIELDS)
    if keep_all:
        for f in fields:
            out_ref[0, f] = start_ref[f]
    buffers, extras = (one, two), (added_one, added_two)
    sides = (
        (0, low_ref, packed_low, lambda n, p: n - p),
        (WIDE - 1, high_ref, packed_high, lambda n, p: p - 1),
    )
    for m in range(count):
        here = start_ref if m == 0 else buffers[m % 2]
        there, here_added, there_added = buffers[(m + 1) % 2], extras[m % 2], extras[(m + 1) % 2]
        last = m + 1 == count

        def own(x, beside):
            field = [here[f, x] for f in fields]
            slope = [slope_ref[m, f, x] for f in fields]
            source = [source_ref[m + 1, f, x] for f in fields] if m + 1 < STEPS else None
            new = stepped(mix, field, beside, slope, source)
            for f in fields:
                if not last:
                    there[f, x] = new[f]
                if keep_all:
                    out_ref[m + 1, f, x] = new[f]
                elif last:
                    out_ref[f, x] = new[f]

        for side, (edge, alone, packed, place) in enumerate(sides):
            inner = edge + 1 if edge == 0 else edge - 1
            beyond = [alone[f, m] for f in fields]
            if m > 0:
                beyond = [beyond[f] + here_added[side, f, 0] for f in fields]
            own(edge, [here[f, inner] + beyond[f] for f in fields])
            for p in range(1, min(m + 1, count - 1 - m) + 1):
                nearer = [here[f, edge] if p == 1 else here_added[side, f, p - 2] for f in fields]
                if p == m + 1:
                    for f in fields:
                        there_added[side, f, p - 1] = DIFFUSION * nearer[f]
                    continue
                beside = nearer
                if p + 1 <= m:
                    beside = [nearer[f] + here_added[side, f, p] for f in fields]
                at = REACH_AT[m] + place(REACH[m], p)
                new = stepped(
                    mix,
                    [here_added[side, f, p - 1] for f in fields],
                    beside,
                    [packed[f, at] for f in fields],
                    None,
                )
                for f in fields:
                    there_added[side, f, p - 1] = new[f]

        def inside(i, carry):
            for k in range(3):
                x = 1 + 3 * i + k
                own(x, [here[f, x - 1] + here[f, x + 1] for f in fields])
            return carry

        lax.fori_loop(0, 2, inside, 0)


def scan_kernel(mix_ref, slope_ref, resid_ref, error_ref):
    blocks = resid_ref.shape[0]
    mix = scalars(mix_ref)
    error = [resid_ref[0, f] for f in range(FIELDS)]
    for f in range(FIELDS):
        error_ref[0, f] = error[f]

    def turn(i, error):
        new = []
        for f, turned in enumerate(mixed(mix, error)):
            scaled = (COARSE_STEP / RATE) * slope_ref[i, f]
            new.append((1.0 - COARSE_STEP) * error[f] + scaled * turned + resid_ref[i + 1, f])
            error_ref[i + 1, f] = new[f]
        return tuple(new)

    lax.fori_loop(0, blocks - 1, turn, tuple(error))


VMEM = functools.partial(pl.BlockSpec, memory_space=pltpu.VMEM)
SMEM = functools.partial(pl.BlockSpec, memory_space=pltpu.SMEM)


def call(kernel, out, operands, planes, scratch=(), name=None):
    read = sum(4 * operand.size for operand in operands)
    written = sum(4 * leaf.size for leaf in jax.tree.leaves(out))
    return pl.pallas_call(
        kernel,
        out_shape=out,
        in_specs=[SMEM()] + [VMEM()] * (len(operands) - 1),
        out_specs=jax.tree.map(lambda _: VMEM(), out),
        scratch_shapes=list(scratch),
        compiler_params=pltpu.CompilerParams(vmem_limit_bytes=20 << 20),
        cost_estimate=pl.CostEstimate(
            flops=planes * FIELDS * 2048 * 25, bytes_accessed=read + written, transcendentals=0
        ),
        name=name,
    )(*operands)


def struct(*shape):
    return jax.ShapeDtypeStruct(shape, jnp.float32)


def from_behind(array):
    count = lax.axis_size("tm")
    return lax.ppermute(array, "tm", [(i, i + 1) for i in range(count - 1)])


def exchange(up, down):
    count = lax.axis_size("space")
    forward = [(i, (i + 1) % count) for i in range(count)]
    backward = [(b, a) for a, b in forward]
    return lax.ppermute(up, "space", forward), lax.ppermute(down, "space", backward)


def chunked(slab, parts):
    return slab.reshape(FIELDS, parts, -1, 128).transpose(1, 0, 2, 3)


def per_device(primal, source, guess, mixing):
    parts = lax.axis_size("tm")
    leading = lax.axis_index("tm") == 0
    cells = primal.shape[2:]
    slab = (FIELDS,) + cells
    plane = cells[1:]
    packed = struct(FIELDS, PACKED, *plane)
    slope, up, down = call(
        prepare_kernel,
        (struct(*primal.shape), packed, packed),
        (mixing, primal),
        STEPS * WIDE,
        name="prepare",
    )
    packed_low, packed_high = exchange(up, down)
    slope_share = lax.all_to_all(chunked(slope[0], parts), "tm", 0, 0)

    def march(start, count, keep_all, name):
        ends = struct(FIELDS, count, *plane)
        room = pltpu.VMEM(slab, jnp.float32)
        up, down = call(
            functools.partial(alone_kernel, count),
            (ends, ends),
            (mixing, start, slope, source),
            44,
            scratch=[room, room],
            name="alone_" + name,
        )
        low, high = exchange(up, down)
        extra = pltpu.VMEM((2, FIELDS, HALO) + plane, jnp.float32)
        return call(
            functools.partial(march_kernel, count, keep_all),
            struct(STEPS, *slab) if keep_all else struct(*slab),
            (mixing, start, low, high, slope, source, packed_low, packed_high),
            88,
            scratch=[room, room, extra, extra],
            name="march_" + name,
        )

    start = guess[0]
    ended = march(start, STEPS, False, "guess")
    relaxed = jnp.where(leading, start, from_behind(ended) + source[0])
    ended_again = march(relaxed, STEPS, False, "relaxed")
    residual = jnp.where(leading, source[0], from_behind(ended_again) + source[0] - relaxed)
    resid_share = lax.all_to_all(chunked(residual, parts), "tm", 0, 0)
    error_share = call(
        scan_kernel, struct(*resid_share.shape), (mixing, slope_share, resid_share), 16, name="scan"
    )
    error = lax.all_to_all(error_share, "tm", 0, 0)
    error = error.transpose(1, 0, 2, 3).reshape(slab)
    corrected = relaxed + error
    fine_states = march(corrected, STEPS - 1, True, "corrected")
    return fine_states, residual[None]


def solution(mesh):
    split = P("tm", None, "space", None, None)
    return jax.shard_map(
        per_device,
        mesh=mesh,
        in_specs=(split, split, split, P()),
        out_specs=(split, split),
        check_vma=False,
    )
```

time: 794 us -> 177 us (0.22); the launches traced: 782 us -> 174 us
  waiting for transfers between devices: 555 us -> 59.4 us
  starting transfers between devices: 126 us -> 34.2 us
  matrix products: 74.3 us -> 0 us
  blocking collectives: 0 us -> 41 us
  Pallas kernels: 0 us -> 26.7 us
    ppermute x79 -> x10, waiting for transfers between devices: 555 us -> 59.4 us  [the longest x4 29.9 us: exchange(): lax.ppermute(up, 'space', forward)]
    ppermute x79 -> x10, starting transfers between devices: 126 us -> 22.4 us  [the longest x4 11.9 us: exchange(): lax.ppermute(down, 'space', backward)]
    dot_general x55 -> x0, matrix products: 74.3 us -> none  [apply_mix(): jnp.einsum('ij,...jxyz->...ixyz', mixing, field, precision=lax.Precision....]
    all_to_all x0 -> x2, blocking collectives: none -> 41 us  [the longest x1 22.6 us: per_device(): resid_share = lax.all_to_all(chunked(residual, parts), 'tm', 0, 0)]
    pallas_call x0 -> x8, Pallas kernels: none -> 26.7 us  [call(): pl.pallas_call(kernel, out_shape=out, in_specs=[SMEM()] + [VMEM()] * (len...]
    all_to_all x0 -> x1, starting transfers between devices: none -> 11.8 us  [per_device(): slope_share = lax.all_to_all(chunked(slope[0], parts), 'tm', 0, 0)]
    slice x70 -> x1, local copies, waits for them, and re-layouts: 9.84 us -> 0.02 us  [per_device(): slope_share = lax.all_to_all(chunked(slope[0], parts), 'tm', 0, 0)]
  transfers between devices with their start and end apart: 79 -> 11, of which waited for: 77 -> 6; matrix products, arithmetic and copies ran while one was open for 2% -> 1% of each run, Pallas kernels for 0% -> 4%
where the time goes in v1:
time: 177 us; the launch traced here: 174 us
  waiting for transfers between devices  59.4 us (34%)
  blocking collectives  41 us (23%)
  starting transfers between devices  34.2 us (19%)
  Pallas kernels  26.7 us (15%)
  local copies, waits for them, and re-layouts  10.4 us (6%)
    ppermute x4, waiting for transfers between devices, exchange(): lax.ppermute(up, 'space', forward)  29.9 us
    pallas_call x8, Pallas kernels, call(): pl.pallas_call(kernel, out_shape=out, in_specs=[SMEM()] + [VMEM()] * (len...  26.7 us
    all_to_all x1, blocking collectives, per_device(): resid_share = lax.all_to_all(chunked(residual, parts), 'tm', 0, 0)  22.6 us
    ppermute x2, waiting for transfers between devices, from_behind(): return lax.ppermute(array, 'tm', [(i, i + 1) for i in range(count - 1)])  22.6 us
    all_to_all x1, blocking collectives, per_device(): error = lax.all_to_all(error_share, 'tm', 0, 0)  18.4 us
    ppermute x4, starting transfers between devices, exchange(): lax.ppermute(down, 'space', backward)  11.9 us
    all_to_all x1, starting transfers between devices, per_device(): slope_share = lax.all_to_all(chunked(slope[0], parts), 'tm', 0, 0)  11.8 us
    unnamed x28, local copies, waits for them, and re-layouts  8.79 us
  transfers between devices with their start and end apart: 11, of which 6 were waited for; matrix products, arithmetic and copies ran while one was open for 1% of the time, Pallas kernels for 4%

profile of v1, /device:TPU:6, one launch (start us, length us, event | category | flops | bytes accessed | tf_op | source)
XLA Modules:
  0.0 173.9 jit_solution(16069516521191070389)
XLA Ops:
  0.6 1.9 %copy-done.10 = f32[8,5,8,16,128]{4,3,2,1,0:T(8,128)S(1)} copy-done((f32[8,5,8,16,128]{4,3,2,1,0:T(8,128)S(1)}, f32[8,5,8,16,128]{4,3,2,1,0:T(8,128)}, u32[]{:S(2)}) %copy-start.10) | copy-done | bytes 2621464
  3.2 2.9 %prepare.1 = (f32[8,5,8,16,128]{4,3,2,1,0:T(8,128)S(1)}, f32[5,12,16,128]{3,2,1,0:T(8,128)S(1)}, f32[5,12,16,128]{3,2,1,0:T(8,128)S(1)}) custom-call(f32[5,5]{1,0:T(8,128)S(1)} %copy-done.11, f32[8,5,8,16,128]{4,3,2,1,0:T(8,128)S(1)} %copy-done.10), custom_call_target="tpu_custom_call" | custom-call | flops 16384000 | bytes 6226020 | tf_op jit(solution)/shard_map/prepare/pallas_call | solution.py:195
  6.2 2.0 %collective-permute-start.2 = (f32[5,12,16,128]{3,2,1,0:T(8,128)S(1)}, f32[5,12,16,128]{3,2,1,0:T(8,128)S(1)}, u32[]{:S(2)}, u32[]{:S(2)}) collective-permute-start(f32[5,12,16,128]{3,2,1,0:T(8,128)S(1)} %get-tuple-element.14), channel_id=1, source_target_pairs={{0,1},{1,2},{2,3},{3,4},{4,5},{5,6},{6,7},{7,0},{8,9},{9,10},{10,1... | collective-permute-start | bytes 1474568 | tf_op jit(solution)/shard_map/ppermute | solution.py:222
  8.2 2.5 %collective-permute-start.3 = (f32[5,12,16,128]{3,2,1,0:T(8,128)S(1)}, f32[5,12,16,128]{3,2,1,0:T(8,128)S(1)}, u32[]{:S(2)}, u32[]{:S(2)}) collective-permute-start(f32[5,12,16,128]{3,2,1,0:T(8,128)S(1)} %get-tuple-element.15), channel_id=1, source_target_pairs={{1,0},{2,1},{3,2},{4,3},{5,4},{6,5},{7,6},{0,7},{9,8},{10,9},{11,1... | collective-permute-start | bytes 1474568 | tf_op jit(solution)/shard_map/ppermute | solution.py:222
  10.7 1.0 copy-done.8
  11.7 2.2 %alone_guess.1 = (f32[5,8,16,128]{3,2,1,0:T(8,128)S(1)}, f32[5,8,16,128]{3,2,1,0:T(8,128)S(1)}) custom-call(f32[5,5]{1,0:T(8,128)S(1)} %copy-done.11, f32[5,8,16,128]{3,2,1,0:T(8,128)S(1)} %bitcast.25, f32[8,5,8,16,128]{4,3,2,1,0:T(8,128)S(1)} %get-tuple-element.11.slope_ref, f32[8,5,8,16,128]{4,3,2,1,0:T(8,128)S(1)} %copy-done), custom_call_target="tpu_custom_call" | custom-call | flops 11264000 | bytes 6226020 | tf_op jit(solution)/shard_map/alone_guess/pallas_call | solution.py:195
  13.9 4.1 %collective-permute-start.1 = (f32[5,8,16,128]{3,2,1,0:T(8,128)S(1)}, f32[5,8,16,128]{3,2,1,0:T(8,128)S(1)}, u32[]{:S(2)}, u32[]{:S(2)}) collective-permute-start(f32[5,8,16,128]{3,2,1,0:T(8,128)S(1)} %get-tuple-element.13), channel_id=1, source_target_pairs={{1,0},{2,1},{3,2},{4,3},{5,4},{6,5},{7,6},{0,7},{9,8},{10,9},{11,1... | collective-permute-start | bytes 983048 | tf_op jit(solution)/shard_map/ppermute | solution.py:222
  18.1 22.2 %collective-permute-done.low_ref = f32[5,8,16,128]{3,2,1,0:T(8,128)S(1)} collective-permute-done((f32[5,8,16,128]{3,2,1,0:T(8,128)S(1)}, f32[5,8,16,128]{3,2,1,0:T(8,128)S(1)}, u32[]{:S(2)}, u32[]{:S(2)}) %collective-permute-start) | collective-permute-done | bytes 327712 | tf_op jit(solution)/shard_map/ppermute | solution.py:222
  40.2 4.6 %collective-permute-done.1.high_ref = f32[5,8,16,128]{3,2,1,0:T(8,128)S(1)} collective-permute-done((f32[5,8,16,128]{3,2,1,0:T(8,128)S(1)}, f32[5,8,16,128]{3,2,1,0:T(8,128)S(1)}, u32[]{:S(2)}, u32[]{:S(2)}) %collective-permute-start.1) | collective-permute-done | bytes 327712 | tf_op jit(solution)/shard_map/ppermute | solution.py:222
  44.8 4.7 %march_guess.1 = f32[5,8,16,128]{3,2,1,0:T(8,128)S(1)} custom-call(f32[5,5]{1,0:T(8,128)S(1)} %copy-done.11, f32[5,8,16,128]{3,2,1,0:T(8,128)S(1)} %bitcast.26, f32[5,8,16,128]{3,2,1,0:T(8,128)S(1)} %collective-permute-done.low_ref, f32[5,8,16,128]{3,2,1,0:T(8,128)S(1)} %collective-permute-done.1.high_ref, ...), custom_call_target="tpu_custom_call" | custom-call | flops 22528000 | bytes 7536740 | tf_op jit(solution)/shard_map/march_guess/pallas_call | solution.py:195
  49.5 1.9 %collective-permute-start.4 = (f32[5,8,16,128]{3,2,1,0:T(8,128)S(1)}, f32[5,8,16,128]{3,2,1,0:T(8,128)}, u32[]{:S(2)}, u32[]{:S(2)}) collective-permute-start(f32[5,8,16,128]{3,2,1,0:T(8,128)S(1)} %march_guess.1), channel_id=1, source_target_pairs={{0,8},{8,16},{16,24},{24,32},{32,40},{40,48},{48,56},{56,64},{64,7... | collective-permute-start | bytes 983048 | tf_op jit(solution)/shard_map/ppermute | solution.py:215
  51.4 10.6 %collective-permute-done.4 = f32[5,8,16,128]{3,2,1,0:T(8,128)} collective-permute-done((f32[5,8,16,128]{3,2,1,0:T(8,128)S(1)}, f32[5,8,16,128]{3,2,1,0:T(8,128)}, u32[]{:S(2)}, u32[]{:S(2)}) %collective-permute-start.4) | collective-permute-done | bytes 327712 | tf_op jit(solution)/shard_map/ppermute | solution.py:215
  62.0 1.1 fusion.start_ref
  63.2 1.7 copy-done.2
  64.9 2.9 %alone_relaxed.1 = (f32[5,8,16,128]{3,2,1,0:T(8,128)}, f32[5,8,16,128]{3,2,1,0:T(8,128)}) custom-call(f32[5,5]{1,0:T(8,128)S(1)} %copy-done.12, f32[5,8,16,128]{3,2,1,0:T(8,128)S(1)} %fusion.start_ref, f32[8,5,8,16,128]{4,3,2,1,0:T(8,128)S(1)} %copy-done.2, f32[8,5,8,16,128]{4,3,2,1,0:T(8,128)S(1)} %copy-done), custom_call_target="tpu_custom_call" | custom-call | flops 11264000 | bytes 6226020 | tf_op jit(solution)/shard_map/alone_relaxed/pallas_call | solution.py:195
  67.8 4.4 %collective-permute-start.5 = (f32[5,8,16,128]{3,2,1,0:T(8,128)}, f32[5,8,16,128]{3,2,1,0:T(8,128)}, u32[]{:S(2)}, u32[]{:S(2)}) collective-permute-start(f32[5,8,16,128]{3,2,1,0:T(8,128)} %get-tuple-element.16), channel_id=1, source_target_pairs={{0,1},{1,2},{2,3},{3,4},{4,5},{5,6},{6,7},{7,0},{8,9},{9,10},{10,1... | collective-permute-start | bytes 983048 | tf_op jit(solution)/shard_map/ppermute | solution.py:222
  72.2 1.1 collective-permute-start.6
  73.4 0.8 copy.14
  74.2 11.8 %all-to-all-start = ((f32[32,5,4,128]{3,2,1,0:T(4,128)}), f32[32,5,4,128]{3,2,1,0:T(4,128)}, u32[]{:S(2)}, u32[]{:S(2)}) async-start(f32[32,5,4,128]{3,2,1,0:T(4,128)} %bitcast.27), calls=%async_computation | async-start | bytes 655360 | tf_op jit(solution)/shard_map/all_to_all | solution.py:244
  86.1 1.7 copy-done.3
  87.8 1.0 copy-done.6
  88.8 5.1 %march_relaxed.1 = f32[5,8,16,128]{3,2,1,0:T(8,128)S(1)} custom-call(f32[5,5]{1,0:T(8,128)S(1)} %copy-done.12, f32[5,8,16,128]{3,2,1,0:T(8,128)S(1)} %fusion.start_ref, f32[5,8,16,128]{3,2,1,0:T(8,128)} %collective-permute-done.5.low_ref, f32[5,8,16,128]{3,2,1,0:T(8,128)} %collective-permute-done.6.high_ref, f32[8,5,8,16,128]{4,3,2,1,0:T(8,128)S(1)} %copy-done.3, ...), custom_call_target="tpu_custom_call" | custom-call | flops 22528000 | bytes 7536740 | tf_op jit(solution)/shard_map/march_relaxed/pallas_call | solution.py:195
  93.9 2.0 %collective-permute-start.7 = (f32[5,8,16,128]{3,2,1,0:T(8,128)S(1)}, f32[5,8,16,128]{3,2,1,0:T(8,128)S(1)}, u32[]{:S(2)}, u32[]{:S(2)}) collective-permute-start(f32[5,8,16,128]{3,2,1,0:T(8,128)S(1)} %march_relaxed.1), channel_id=1, source_target_pairs={{0,8},{8,16},{16,24},{24,32},{32,40},{40,48},{48,56},{56,64},{64,7... | collective-permute-start | bytes 983048 | tf_op jit(solution)/shard_map/ppermute | solution.py:215
  96.0 12.0 %collective-permute-done.7 = f32[5,8,16,128]{3,2,1,0:T(8,128)S(1)} collective-permute-done((f32[5,8,16,128]{3,2,1,0:T(8,128)S(1)}, f32[5,8,16,128]{3,2,1,0:T(8,128)S(1)}, u32[]{:S(2)}, u32[]{:S(2)}) %collective-permute-start.7) | collective-permute-done | bytes 327712 | tf_op jit(solution)/shard_map/ppermute | solution.py:215
  109.5 22.6 %all_to_all.15.resid_ref = f32[32,5,4,128]{3,2,1,0:T(4,128)S(1)} all-to-all(f32[32,5,4,128]{3,2,1,0:T(4,128)} %bitcast.28), channel_id=1, replica_groups=mesh['tm'=32,'space'=8] {'tm'}, dimensions={0} | all-to-all | bytes 655360 | tf_op jit(solution)/shard_map/all_to_all | solution.py:273
  132.1 1.5 scan.1
  133.6 18.4 %all_to_all.16 = f32[32,5,4,128]{3,2,1,0:T(4,128)S(1)} all-to-all(f32[32,5,4,128]{3,2,1,0:T(4,128)S(1)} %scan.1), channel_id=1, replica_groups=mesh['tm'=32,'space'=8] {'tm'}, dimensions={0} | all-to-all | bytes 655360 | tf_op jit(solution)/shard_map/all_to_all | solution.py:277
  152.2 1.9 %alone_corrected.1 = (f32[5,7,16,128]{3,2,1,0:T(8,128)S(1)}, f32[5,7,16,128]{3,2,1,0:T(8,128)S(1)}) custom-call(f32[5,5]{1,0:T(8,128)S(1)} %copy-done.12, f32[5,8,16,128]{3,2,1,0:T(8,128)S(1)} %bitcast_add_fusion.start_ref, f32[8,5,8,16,128]{4,3,2,1,0:T(8,128)S(1)} %copy-done.4, f32[8,5,8,16,128]{4,3,2,1,0:T(8,128)S(1)} %copy-done), custom_call_target="tpu_custom_call" | custom-call | flops 11264000 | bytes 6144100 | tf_op jit(solution)/shard_map/alone_corrected/pallas_call | solution.py:195
  154.1 4.1 %collective-permute-start.9 = (f32[5,7,16,128]{3,2,1,0:T(8,128)S(1)}, f32[5,7,16,128]{3,2,1,0:T(8,128)S(1)}, u32[]{:S(2)}, u32[]{:S(2)}) collective-permute-start(f32[5,7,16,128]{3,2,1,0:T(8,128)S(1)} %get-tuple-element.19), channel_id=1, source_target_pairs={{1,0},{2,1},{3,2},{4,3},{5,4},{6,5},{7,6},{0,7},{9,8},{10,9},{11,1... | collective-permute-start | bytes 860168 | tf_op jit(solution)/shard_map/ppermute | solution.py:222
  158.2 7.7 %collective-permute-done.8.low_ref = f32[5,7,16,128]{3,2,1,0:T(8,128)S(1)} collective-permute-done((f32[5,7,16,128]{3,2,1,0:T(8,128)S(1)}, f32[5,7,16,128]{3,2,1,0:T(8,128)S(1)}, u32[]{:S(2)}, u32[]{:S(2)}) %collective-permute-start.8) | collective-permute-done | bytes 286752 | tf_op jit(solution)/shard_map/ppermute | solution.py:222
  165.9 2.4 %collective-permute-done.9.high_ref = f32[5,7,16,128]{3,2,1,0:T(8,128)S(1)} collective-permute-done((f32[5,7,16,128]{3,2,1,0:T(8,128)S(1)}, f32[5,7,16,128]{3,2,1,0:T(8,128)S(1)}, u32[]{:S(2)}, u32[]{:S(2)}) %collective-permute-start.9) | collective-permute-done | bytes 286752 | tf_op jit(solution)/shard_map/ppermute | solution.py:222
  168.4 5.6 %march_corrected.1 = f32[8,5,8,16,128]{4,3,2,1,0:T(8,128)} custom-call(f32[5,5]{1,0:T(8,128)S(1)} %copy-done.12, f32[5,8,16,128]{3,2,1,0:T(8,128)S(1)} %bitcast_add_fusion.start_ref, f32[5,7,16,128]{3,2,1,0:T(8,128)S(1)} %collective-permute-done.8.low_ref, f32[5,7,16,128]{3,2,1,0:T(8,128)S(1)} %collective-permute-done.9.high_ref, ...), custom_call_target="tpu_custom_call" | custom-call | flops 22528000 | bytes 9748580 | tf_op jit(solution)/shard_map/march_corrected/pallas_call | solution.py:195
  (35 shorter events, 2.6 us)
Async XLA Ops:
  0.6 10.1 %copy-start = (f32[8,5,8,16,128]{4,3,2,1,0:T(8,128)S(1)}, f32[8,5,8,16,128]{4,3,2,1,0:T(8,128)}, u32[]{:S(2)}) copy-start(f32[8,5,8,16,128]{4,3,2,1,0:T(8,128)} %source_ref.11) | copy-start | bytes 7864324
  0.6 1.9 %copy-start.10 = (f32[8,5,8,16,128]{4,3,2,1,0:T(8,128)S(1)}, f32[8,5,8,16,128]{4,3,2,1,0:T(8,128)}, u32[]{:S(2)}) copy-start(f32[8,5,8,16,128]{4,3,2,1,0:T(8,128)} %primal_ref.1) | copy-start | bytes 7864324
  2.5 0.7 copy-start.11
  6.2 38.7 %copy-start.1 = (f32[8,5,8,16,128]{4,3,2,1,0:T(8,128)}, f32[8,5,8,16,128]{4,3,2,1,0:T(8,128)S(1)}, u32[]{:S(2)}) copy-start(f32[8,5,8,16,128]{4,3,2,1,0:T(8,128)S(1)} %get-tuple-element.11.slope_ref) | copy-start | bytes 7864324
  6.2 38.6 %collective-permute-start.2 = (f32[5,12,16,128]{3,2,1,0:T(8,128)S(1)}, f32[5,12,16,128]{3,2,1,0:T(8,128)S(1)}, u32[]{:S(2)}, u32[]{:S(2)}) collective-permute-start(f32[5,12,16,128]{3,2,1,0:T(8,128)S(1)} %get-tuple-element.14), channel_id=1, source_target_pairs={{0,1},{1,2},{2,3},{3,4},{4,5},{5,6},{6,7},{7,0},{8,9},{9,10},{10,1... | collective-permute-start | bytes 1474568 | tf_op jit(solution)/shard_map/ppermute | solution.py:222
  8.2 36.6 %collective-permute-start.3 = (f32[5,12,16,128]{3,2,1,0:T(8,128)S(1)}, f32[5,12,16,128]{3,2,1,0:T(8,128)S(1)}, u32[]{:S(2)}, u32[]{:S(2)}) collective-permute-start(f32[5,12,16,128]{3,2,1,0:T(8,128)S(1)} %get-tuple-element.15), channel_id=1, source_target_pairs={{1,0},{2,1},{3,2},{4,3},{5,4},{6,5},{7,6},{0,7},{9,8},{10,9},{11,1... | collective-permute-start | bytes 1474568 | tf_op jit(solution)/shard_map/ppermute | solution.py:222
  10.7 1.0 copy-start.8
  11.7 33.1 %copy-start.9 = (f32[1,5,8,16,128]{4,3,2,1,0:T(8,128)S(1)}, f32[1,5,8,16,128]{4,3,2,1,0:T(8,128)}, u32[]{:S(2)}) copy-start(f32[1,5,8,16,128]{4,3,2,1,0:T(8,128)} %param.6) | copy-start | bytes 983044
  13.8 26.4 %collective-permute-start = (f32[5,8,16,128]{3,2,1,0:T(8,128)S(1)}, f32[5,8,16,128]{3,2,1,0:T(8,128)S(1)}, u32[]{:S(2)}, u32[]{:S(2)}) collective-permute-start(f32[5,8,16,128]{3,2,1,0:T(8,128)S(1)} %get-tuple-element.12), channel_id=1, source_target_pairs={{0,1},{1,2},{2,3},{3,4},{4,5},{5,6},{6,7},{7,0},{8,9},{9,10},{10,1... | collective-permute-start | bytes 983048 | tf_op jit(solution)/shard_map/ppermute | solution.py:222
  13.9 49.2 %copy-start.12 = (f32[5,5]{1,0:T(8,128)S(1)}, f32[5,5]{1,0:T(8,128)}, u32[]{:S(2)}) copy-start(f32[5,5]{1,0:T(8,128)} %mix_ref.15) | copy-start | bytes 304
  13.9 30.9 %collective-permute-start.1 = (f32[5,8,16,128]{3,2,1,0:T(8,128)S(1)}, f32[5,8,16,128]{3,2,1,0:T(8,128)S(1)}, u32[]{:S(2)}, u32[]{:S(2)}) collective-permute-start(f32[5,8,16,128]{3,2,1,0:T(8,128)S(1)} %get-tuple-element.13), channel_id=1, source_target_pairs={{1,0},{2,1},{3,2},{4,3},{5,4},{6,5},{7,6},{0,7},{9,8},{10,9},{11,1... | collective-permute-start | bytes 983048 | tf_op jit(solution)/shard_map/ppermute | solution.py:222
  44.8 4.7 %copy-start.5 = (f32[5,12,16,128]{3,2,1,0:T(8,128)}, f32[5,12,16,128]{3,2,1,0:T(8,128)S(1)}, u32[]{:S(2)}) copy-start(f32[5,12,16,128]{3,2,1,0:T(8,128)S(1)} %collective-permute-done.3.packed_high) | copy-start | bytes 1474564
  49.5 12.5 %collective-permute-start.4 = (f32[5,8,16,128]{3,2,1,0:T(8,128)S(1)}, f32[5,8,16,128]{3,2,1,0:T(8,128)}, u32[]{:S(2)}, u32[]{:S(2)}) collective-permute-start(f32[5,8,16,128]{3,2,1,0:T(8,128)S(1)} %march_guess.1), channel_id=1, source_target_pairs={{0,8},{8,16},{16,24},{24,32},{32,40},{40,48},{48,56},{56,64},{64,7... | collective-permute-start | bytes 983048 | tf_op jit(solution)/shard_map/ppermute | solution.py:215
  63.1 1.7 %copy-start.2 = (f32[8,5,8,16,128]{4,3,2,1,0:T(8,128)S(1)}, f32[8,5,8,16,128]{4,3,2,1,0:T(8,128)}, u32[]{:S(2)}) copy-start(f32[8,5,8,16,128]{4,3,2,1,0:T(8,128)} %copy-done.1) | copy-start | bytes 7864324
  67.8 18.2 %collective-permute-start.5 = (f32[5,8,16,128]{3,2,1,0:T(8,128)}, f32[5,8,16,128]{3,2,1,0:T(8,128)}, u32[]{:S(2)}, u32[]{:S(2)}) collective-permute-start(f32[5,8,16,128]{3,2,1,0:T(8,128)} %get-tuple-element.16), channel_id=1, source_target_pairs={{0,1},{1,2},{2,3},{3,4},{4,5},{5,6},{6,7},{7,0},{8,9},{9,10},{10,1... | collective-permute-start | bytes 983048 | tf_op jit(solution)/shard_map/ppermute | solution.py:222
  72.2 13.8 %collective-permute-start.6 = (f32[5,8,16,128]{3,2,1,0:T(8,128)}, f32[5,8,16,128]{3,2,1,0:T(8,128)}, u32[]{:S(2)}, u32[]{:S(2)}) collective-permute-start(f32[5,8,16,128]{3,2,1,0:T(8,128)} %get-tuple-element.17), channel_id=1, source_target_pairs={{1,0},{2,1},{3,2},{4,3},{5,4},{6,5},{7,6},{0,7},{9,8},{10,9},{11,1... | collective-permute-start | bytes 983048 | tf_op jit(solution)/shard_map/ppermute | solution.py:222
  74.2 35.3 %all-to-all-start = ((f32[32,5,4,128]{3,2,1,0:T(4,128)}), f32[32,5,4,128]{3,2,1,0:T(4,128)}, u32[]{:S(2)}, u32[]{:S(2)}) async-start(f32[32,5,4,128]{3,2,1,0:T(4,128)} %bitcast.27), calls=%async_computation | async-start | bytes 655360 | tf_op jit(solution)/shard_map/all_to_all | solution.py:244
  86.0 1.7 %copy-start.3 = (f32[8,5,8,16,128]{4,3,2,1,0:T(8,128)S(1)}, f32[8,5,8,16,128]{4,3,2,1,0:T(8,128)}, u32[]{:S(2)}) copy-start(f32[8,5,8,16,128]{4,3,2,1,0:T(8,128)} %copy-done.1) | copy-start | bytes 7864324
  87.8 1.0 copy-start.6
  93.9 14.0 %collective-permute-start.7 = (f32[5,8,16,128]{3,2,1,0:T(8,128)S(1)}, f32[5,8,16,128]{3,2,1,0:T(8,128)S(1)}, u32[]{:S(2)}, u32[]{:S(2)}) collective-permute-start(f32[5,8,16,128]{3,2,1,0:T(8,128)S(1)} %march_relaxed.1), channel_id=1, source_target_pairs={{0,8},{8,16},{16,24},{24,32},{32,40},{40,48},{48,56},{56,64},{64,7... | collective-permute-start | bytes 983048 | tf_op jit(solution)/shard_map/ppermute | solution.py:215
  108.0 0.7 copy-start.13
  109.5 42.6 %copy-start.4 = (f32[8,5,8,16,128]{4,3,2,1,0:T(8,128)S(1)}, f32[8,5,8,16,128]{4,3,2,1,0:T(8,128)}, u32[]{:S(2)}) copy-start(f32[8,5,8,16,128]{4,3,2,1,0:T(8,128)} %copy-done.1) | copy-start | bytes 7864324
  152.2 16.2 %copy-start.7 = (f32[5,12,16,128]{3,2,1,0:T(8,128)S(1)}, f32[5,12,16,128]{3,2,1,0:T(8,128)}, u32[]{:S(2)}) copy-start(f32[5,12,16,128]{3,2,1,0:T(8,128)} %copy-done.5) | copy-start | bytes 1474564
  154.0 11.9 %collective-permute-start.8 = (f32[5,7,16,128]{3,2,1,0:T(8,128)S(1)}, f32[5,7,16,128]{3,2,1,0:T(8,128)S(1)}, u32[]{:S(2)}, u32[]{:S(2)}) collective-permute-start(f32[5,7,16,128]{3,2,1,0:T(8,128)S(1)} %get-tuple-element.18), channel_id=1, source_target_pairs={{0,1},{1,2},{2,3},{3,4},{4,5},{5,6},{6,7},{7,0},{8,9},{9,10},{10,1... | collective-permute-start | bytes 860168 | tf_op jit(solution)/shard_map/ppermute | solution.py:222
  154.1 14.2 %collective-permute-start.9 = (f32[5,7,16,128]{3,2,1,0:T(8,128)S(1)}, f32[5,7,16,128]{3,2,1,0:T(8,128)S(1)}, u32[]{:S(2)}, u32[]{:S(2)}) collective-permute-start(f32[5,7,16,128]{3,2,1,0:T(8,128)S(1)} %get-tuple-element.19), channel_id=1, source_target_pairs={{1,0},{2,1},{3,2},{4,3},{5,4},{6,5},{7,6},{0,7},{9,8},{10,9},{11,1... | collective-permute-start | bytes 860168 | tf_op jit(solution)/shard_map/ppermute | solution.py:222

commit v2 on v1

v2 whole, which is shorter than its diff:
```python
import functools

import jax
import jax.numpy as jnp
from jax import lax
from jax.experimental import pallas as pl
from jax.experimental.pallas import tpu as pltpu
from jax.sharding import PartitionSpec as P


STEPS = 8
FIELDS = 5
WIDE = 8
DIFFUSION = 0.1
RATE = 0.25
COARSE_STEP = 0.75
KEEP = 1.0 - 6.0 * DIFFUSION - RATE
REACH = [min(m, STEPS - 1 - m) for m in range(STEPS)]
REACH_AT = [sum(REACH[:m]) for m in range(STEPS)]
PACKED = sum(REACH)
HALF = STEPS // 2
HALO = max(min(m + 1, STEPS - 1 - m) for m in range(STEPS))


def mixed(mix, fields):
    out = []
    for i in range(FIELDS):
        total = mix[i][0] * fields[0]
        for j in range(1, FIELDS):
            total = total + mix[i][j] * fields[j]
        out.append(total)
    return out


def scalars(mix_ref):
    return [[mix_ref[i, j] for j in range(FIELDS)] for i in range(FIELDS)]


def wall_neighbours(v):
    row = lax.broadcasted_iota(jnp.int32, (8, 128), 0)
    first, last = row == 0, row == 7
    a, b = v[:8], v[8:]
    a_next, b_next = pltpu.roll(a, 1, 0), pltpu.roll(b, 1, 0)
    a_prev, b_prev = pltpu.roll(a, 7, 0), pltpu.roll(b, 7, 0)
    upper = jnp.where(first, 0.0, a_next) + jnp.where(last, b_prev, a_prev)
    lower = jnp.where(first, a_next, b_next) + jnp.where(last, 0.0, b_prev)
    return jnp.concatenate([upper, lower], axis=0)


def stepped(mix, field, beside, slope, source):
    out = []
    for f, turned in enumerate(mixed(mix, field)):
        v = field[f]
        around = pltpu.roll(v, 1, 1) + pltpu.roll(v, 127, 1) + wall_neighbours(v)
        around = around + beside[f]
        new = KEEP * v + DIFFUSION * around + slope[f] * turned
        out.append(new if source is None else new + source[f])
    return out


class Streamed:
    def __init__(self, hbm, room, sems, wanted):
        self.copies = {t: pltpu.make_async_copy(hbm.at[t], room.at[t], sems.at[t]) for t in wanted}
        for copy in self.copies.values():
            copy.start()

    def ready(self, t):
        if t in self.copies:
            self.copies.pop(t).wait()


def slopes(mix, state):
    out = []
    for value in mixed(mix, state):
        tilted = jnp.tanh(value)
        out.append(RATE - RATE * (tilted * tilted))
    return out


def border_kernel(mix_ref, primal_hbm, up_ref, down_ref, up_state, down_state, sems):
    mix = scalars(mix_ref)
    copies = []
    for m in range(STEPS):
        n, a = REACH[m], REACH_AT[m]
        if n > 0:
            ends = (pl.ds(WIDE - n, n), up_state), (pl.ds(0, n), down_state)
            for planes, state in ends:
                copies.append(
                    pltpu.make_async_copy(
                        primal_hbm.at[m, :, planes], state.at[:, a : a + n], sems.at[len(copies)]
                    )
                )
    for copy in copies:
        copy.start()
    for copy in copies:
        copy.wait()
    for state, out_ref in ((up_state, up_ref), (down_state, down_ref)):

        def plane(n, carry):
            for k in range(2):
                x = 2 * n + k
                for f, value in enumerate(slopes(mix, [state[f, x] for f in range(FIELDS)])):
                    out_ref[f, x] = value
            return carry

        lax.fori_loop(0, PACKED // 2, plane, 0)


def shares(part):
    return [(part * x + q, x, 4 * q) for x in range(WIDE) for q in range(part)]


def alone_step(mix, m, here, there, slope_ref, source_ref, ends):
    for x in range(WIDE):
        if not (x >= m + 1 or x <= WIDE - 2 - m):
            continue
        field = [here[f, x] for f in range(FIELDS)]
        if x == 0:
            beside = [here[f, 1] for f in range(FIELDS)]
        elif x == WIDE - 1:
            beside = [here[f, WIDE - 2] for f in range(FIELDS)]
        else:
            beside = [here[f, x - 1] + here[f, x + 1] for f in range(FIELDS)]
        slope = [slope_ref[m, f, x] for f in range(FIELDS)]
        source = None
        if source_ref is not None:
            source = [source_ref[m + 1, f, x] for f in range(FIELDS)]
        new = stepped(mix, field, beside, slope, source)
        for f in range(FIELDS):
            there[f, x] = new[f]
            if x == 0 or x == WIDE - 1:
                ends[(m + 1) // HALF][int(x == 0)][f, (m + 1) % HALF] = new[f]


def guess_kernel(mix_ref, primal_hbm, source_hbm, guess_ref, slope_ref, share_ref, up_one, down_one, up_two, down_two, primal, source_ref, one, two, sems):
    mix = scalars(mix_ref)
    primal_in = Streamed(primal_hbm, primal, sems.at[0], range(STEPS))
    source_in = Streamed(source_hbm, source_ref, sems.at[1], range(1, STEPS))
    start_ref = guess_ref.at[0]
    ends = [(up_one, down_one), (up_two, down_two)]
    for f in range(FIELDS):
        down_one[f, 0] = start_ref[f, 0]
        up_one[f, 0] = start_ref[f, WIDE - 1]
    buffers = (one, two)
    for t in range(STEPS):
        primal_in.ready(t)

        def plane(n, carry):
            for k in range(2):
                x = 2 * n + k
                state = [primal[t, f, x] for f in range(FIELDS)]
                for f, value in enumerate(slopes(mix, state)):
                    slope_ref[t, f, x] = value
            return carry

        lax.fori_loop(0, WIDE // 2, plane, 0)
        if t == 0:
            for share, x, row in shares(4):
                for f in range(FIELDS):
                    share_ref[share, f] = slope_ref[0, f, x, row : row + 4]
        source_in.ready(t + 1)
        if t + 1 < STEPS:
            here = start_ref if t == 0 else buffers[t % 2]
            alone_step(mix, t, here, buffers[(t + 1) % 2], slope_ref, source_ref, ends)


def relaxed_kernel(mix_ref, leads_ref, source_hbm, ended_ref, guess_ref, slope_ref, relaxed_hbm, change_ref, middle_ref, up_ref, down_ref, source_ref, relaxed_ref, one, two, sems):
    source_in = Streamed(source_hbm, source_ref, sems, [0])
    mix = scalars(mix_ref)
    leads = leads_ref[0] == 1
    source_in.ready(0)
    for f in range(FIELDS):
        for x in range(WIDE):
            before = guess_ref[0, f, x]
            after = jnp.where(leads, before, ended_ref[f, x] + source_ref[0, f, x])
            relaxed_ref[f, x] = after
            change_ref[f, x] = after - before
        down_ref[f, 0] = change_ref[f, 0]
        up_ref[f, 0] = change_ref[f, WIDE - 1]
    relaxed_out = pltpu.make_async_copy(relaxed_ref, relaxed_hbm, sems.at[1])
    relaxed_out.start()
    buffers = (one, two)
    for m in range(HALF - 1):
        here = change_ref if m == 0 else buffers[m % 2]
        there = middle_ref if m == HALF - 2 else buffers[(m + 1) % 2]
        alone_step(mix, m, here, there, slope_ref, None, [(up_ref, down_ref)])
    relaxed_out.wait()


def rest_kernel(count, forced, mix_ref, source_hbm, middle_ref, slope_ref, up_ref, down_ref, one, two, source_ref, sems):
    source_in = Streamed(source_hbm, source_ref, sems, range(HALF, count) if forced else [])
    mix = scalars(mix_ref)
    buffers = (one, two)
    for m in range(HALF - 1, count - 1):
        source_in.ready(m + 1)
        here = middle_ref if m == HALF - 1 else buffers[m % 2]
        source = source_ref if forced else None
        alone_step(mix, m, here, buffers[(m + 1) % 2], slope_ref, source, [None, (up_ref, down_ref)])


def corrected_kernel(mix_ref, leads_ref, relaxed_hbm, source_hbm, share_ref, slope_ref, corrected_ref, middle_ref, up_ref, down_ref, relaxed_ref, source_ref, one, two, sems):
    relaxed_in = pltpu.make_async_copy(relaxed_hbm, relaxed_ref, sems.at[STEPS])
    relaxed_in.start()
    source_in = Streamed(source_hbm, source_ref, sems, range(HALF))
    mix = scalars(mix_ref)
    leads = leads_ref[0] == 1
    relaxed_in.wait()
    source_in.ready(0)
    for share, x, row in shares(4):
        for f in range(FIELDS):
            rows = slice(row, row + 4)
            error = jnp.where(leads, source_ref[0, f, x, rows], share_ref[share, f])
            corrected_ref[f, x, rows] = relaxed_ref[f, x, rows] + error
    for f in range(FIELDS):
        down_ref[f, 0] = corrected_ref[f, 0]
        up_ref[f, 0] = corrected_ref[f, WIDE - 1]
    buffers = (one, two)
    for m in range(HALF - 1):
        source_in.ready(m + 1)
        here = corrected_ref if m == 0 else buffers[m % 2]
        there = middle_ref if m == HALF - 2 else buffers[(m + 1) % 2]
        alone_step(mix, m, here, there, slope_ref, source_ref, [(up_ref, down_ref)])


def march_steps(count, steps, forced, done, step_opens, step_ends, mix, start_ref, start_added, low_ref, high_ref, slope_ref, source_ref, packed_low, packed_high, one, two, added_one, added_two, middle=None):
    fields = range(FIELDS)
    buffers, extras = (one, two), (added_one, added_two)
    sides = (
        (0, low_ref, packed_low, lambda n, p: n - p),
        (WIDE - 1, high_ref, packed_high, lambda n, p: p - 1),
    )
    for m in steps:
        here = start_ref if m == steps[0] else buffers[m % 2]
        step_opens(m)
        here_added = start_added if m == steps[0] else extras[m % 2]
        there, there_added = buffers[(m + 1) % 2], extras[(m + 1) % 2]
        if middle is not None and m == steps[-1]:
            there, there_added = middle
        last = m + 1 == count

        def own(x, beside):
            field = [here[f, x] for f in fields]
            slope = [slope_ref[m, f, x] for f in fields]
            source = [source_ref[m + 1, f, x] for f in fields] if forced and m + 1 < STEPS else None
            new = stepped(mix, field, beside, slope, source)
            for f in fields:
                if not last:
                    there[f, x] = new[f]
                done(m + 1, f, x, new[f])

        for side, (edge, alone, packed, place) in enumerate(sides):
            inner = edge + 1 if edge == 0 else edge - 1
            beyond = [alone[m // HALF][f, m % HALF] for f in fields]
            if m > 0:
                beyond = [beyond[f] + here_added[side, f, 0] for f in fields]
            own(edge, [here[f, inner] + beyond[f] for f in fields])
            for p in range(1, min(m + 1, count - 1 - m) + 1):
                nearer = [here[f, edge] if p == 1 else here_added[side, f, p - 2] for f in fields]
                if p == m + 1:
                    for f in fields:
                        there_added[side, f, p - 1] = DIFFUSION * nearer[f]
                    continue
                beside = nearer
                if p + 1 <= m:
                    beside = [nearer[f] + here_added[side, f, p] for f in fields]
                at = REACH_AT[m] + place(REACH[m], p)
                new = stepped(
                    mix,
                    [here_added[side, f, p - 1] for f in fields],
                    beside,
                    [packed[f, at] for f in fields],
                    None,
                )
                for f in fields:
                    there_added[side, f, p - 1] = new[f]

        def inside(i, carry):
            for k in range(3):
                x = 1 + 3 * i + k
                own(x, [here[f, x - 1] + here[f, x + 1] for f in fields])
            return carry

        lax.fori_loop(0, 2, inside, 0)
        step_ends(m)


def nothing(m):
    pass


def march_first_kernel(count, forced, mix_ref, source_hbm, start_ref, low_ref, high_ref, slope_ref, packed_low, packed_high, middle_ref, middle_added, *rest):
    later_ref, (one, two, added_one, added_two, source_ref, sems) = rest[0], rest[-6:]
    source_in = Streamed(source_hbm, source_ref, sems, range(1, HALF + 1) if forced else [])
    later = pltpu.make_async_copy(source_hbm.at[HALF + 1 :], later_ref, sems.at[HALF + 1]) if forced else None
    if forced:
        later.start()
    march_steps(
        count, range(HALF), forced, lambda *_: None, lambda m: source_in.ready(m + 1), nothing, scalars(mix_ref),
        start_ref, None, (low_ref, None), (high_ref, None), slope_ref, source_ref, packed_low, packed_high,
        one, two, added_one, added_two, (middle_ref, middle_added),
    )
    if forced:
        later.wait()


class Later:
    def __init__(self, ref):
        self.ref = ref

    def __getitem__(self, index):
        return self.ref[(index[0] - HALF - 1,) + index[1:]]


def end_kernel(mix_ref, later_ref, middle_ref, middle_added, low_ref, high_ref, slope_ref, packed_low, packed_high, out_ref, one, two, added_one, added_two):
    def done(step, f, x, value):
        if step == STEPS:
            out_ref[f, x] = value

    march_steps(
        STEPS, range(HALF, STEPS), True, done, nothing, nothing, scalars(mix_ref),
        middle_ref, middle_added, (None, low_ref), (None, high_ref), slope_ref, Later(later_ref), packed_low, packed_high,
        one, two, added_one, added_two,
    )


def change_kernel(mix_ref, leads_ref, source_hbm, middle_ref, middle_added, low_ref, high_ref, slope_ref, packed_low, packed_high, out_hbm, share_ref, one, two, added_one, added_two, source_ref, out_ref, sems):
    source_in = Streamed(source_hbm, source_ref, sems, [0])
    mix = scalars(mix_ref)

    def done(step, f, x, value):
        if step == STEPS:
            out_ref[f, x] = value

    march_steps(
        STEPS, range(HALF, STEPS), False, done, nothing, nothing, mix,
        middle_ref, middle_added, (None, low_ref), (None, high_ref), slope_ref, None, packed_low, packed_high,
        one, two, added_one, added_two,
    )
    out = pltpu.make_async_copy(out_ref, out_hbm, sems.at[1])
    out.start()
    source_in.ready(0)
    leads = leads_ref[0] == 1
    for x in range(WIDE):
        error = [source_ref[0, f, x] for f in range(FIELDS)]
        slope = [slope_ref[0, f, x] for f in range(FIELDS)]
        moved = coarse_turn(mix, error, slope)
        for f in range(FIELDS):
            value = out_ref[f, x]
            value = jnp.where(leads, moved[f] + value, value)
            for q in range(4):
                share_ref[4 * x + q, f] = value[4 * q : 4 * q + 4]
    out.wait()


def states_first_kernel(mix_ref, source_hbm, start_ref, low_ref, high_ref, slope_ref, packed_low, packed_high, out_hbm, middle_ref, middle_added, later_ref, one, two, added_one, added_two, source_ref, out_ref, sems, out_sems):
    source_in = Streamed(source_hbm, source_ref, sems, range(1, HALF + 1))
    later = pltpu.make_async_copy(source_hbm.at[HALF + 1 :], later_ref, sems.at[HALF + 1])
    later.start()
    outs = [
        pltpu.make_async_copy(start_ref if t == 0 else out_ref.at[t], out_hbm.at[t], out_sems.at[t])
        for t in range(HALF + 1)
    ]
    outs[0].start()

    def done(step, f, x, value):
        out_ref[step, f, x] = value

    march_steps(
        STEPS - 1, range(HALF), True, done, lambda m: source_in.ready(m + 1), lambda m: outs[m + 1].start(),
        scalars(mix_ref),
        start_ref, None, (low_ref, None), (high_ref, None), slope_ref, source_ref, packed_low, packed_high,
        one, two, added_one, added_two, (middle_ref, middle_added),
    )
    later.wait()
    for out in outs:
        out.wait()


def states_rest_kernel(mix_ref, earlier_hbm, later_ref, middle_ref, middle_added, low_ref, high_ref, slope_ref, packed_low, packed_high, out_hbm, one, two, added_one, added_two, out_ref, out_sems):
    outs = {
        t: pltpu.make_async_copy(out_ref.at[t], out_hbm.at[t], out_sems.at[t])
        for t in range(HALF + 1, STEPS)
    }

    def done(step, f, x, value):
        out_ref[step, f, x] = value

    march_steps(
        STEPS - 1, range(HALF, STEPS - 1), True, done, nothing, lambda m: outs[m + 1].start(), scalars(mix_ref),
        middle_ref, middle_added, (None, low_ref), (None, high_ref), slope_ref, Later(later_ref),
        packed_low, packed_high, one, two, added_one, added_two,
    )
    for out in outs.values():
        out.wait()


def coarse_turn(mix, error, slope):
    out = []
    for f, turned in enumerate(mixed(mix, error)):
        out.append((1.0 - COARSE_STEP) * error[f] + (COARSE_STEP / RATE) * slope[f] * turned)
    return out


def scan_kernel(mix_ref, slope_ref, resid_ref, error_ref):
    mix = scalars(mix_ref)
    blocks = resid_ref.shape[0]
    error = tuple(resid_ref[0, f] for f in range(FIELDS))
    for f in range(FIELDS):
        error_ref[0, f] = error[f]
        error_ref[1, f] = error[f]

    def turn(i, error):
        moved = coarse_turn(mix, error, [slope_ref[i, f] for f in range(FIELDS)])
        new = tuple(moved[f] + resid_ref[i, f] for f in range(FIELDS))
        for f in range(FIELDS):
            error_ref[i + 1, f] = new[f]
        return new

    lax.fori_loop(1, blocks - 1, turn, error)


VMEM = pl.BlockSpec(memory_space=pltpu.VMEM)
SMEM = pl.BlockSpec(memory_space=pltpu.SMEM)
HBM = pl.BlockSpec(memory_space=pltpu.HBM)


def call(kernel, out, operands, places, planes, scratch=(), first_out=None, alias=None):
    read = sum(4 * operand.size for operand in operands)
    written = sum(4 * leaf.size for leaf in jax.tree.leaves(out))
    if first_out is not None:
        out = (pltpu.HBM(out[0].shape, out[0].dtype),) + tuple(out[1:])
    return pl.pallas_call(
        kernel,
        input_output_aliases=alias or {},
        out_shape=out,
        in_specs=places + [VMEM] * (len(operands) - len(places)),
        out_specs=[first_out or VMEM] + [VMEM] * (len(out) - 1),
        scratch_shapes=list(scratch),
        compiler_params=pltpu.CompilerParams(vmem_limit_bytes=20 << 20),
        cost_estimate=pl.CostEstimate(
            flops=planes * FIELDS * 2048 * 25, bytes_accessed=read + written, transcendentals=0
        ),
    )(*operands)


def in_hbm(array):
    return pltpu.with_memory_space_constraint(array, pltpu.HBM)


def struct(*shape):
    return jax.ShapeDtypeStruct(shape, jnp.float32)


def from_behind(array):
    count = lax.axis_size("tm")
    return lax.ppermute(array, "tm", [(i, i + 1) for i in range(count - 1)])


def exchange(up, down):
    count = lax.axis_size("space")
    forward = [(i, (i + 1) % count) for i in range(count)]
    backward = [(b, a) for a, b in forward]
    return lax.ppermute(up, "space", forward), lax.ppermute(down, "space", backward)


def per_device(primal, source, guess, mixing):
    parts = lax.axis_size("tm")
    leading = lax.axis_index("tm") == 0
    leads = leading.astype(jnp.int32)[None]
    plane = primal.shape[3:]
    slab = struct(*primal.shape[1:])
    whole = struct(*primal.shape)
    share = struct(parts, FIELDS, 4, plane[1])
    room = pltpu.VMEM(slab.shape, jnp.float32)
    extra = pltpu.VMEM((2, FIELDS, HALO) + plane, jnp.float32)
    march_room = [room, room, extra, extra]
    packed = struct(FIELDS, PACKED, *plane)

    packed_room = pltpu.VMEM(packed.shape, jnp.float32)
    up, down = call(
        border_kernel,
        (packed, packed),
        (mixing, in_hbm(primal)),
        [SMEM, HBM],
        2 * PACKED,
        scratch=[packed_room, packed_room, pltpu.SemaphoreType.DMA((2 * STEPS,))],
    )
    packed_low, packed_high = exchange(up, down)
    first_source = source[0]
    primal, source = in_hbm(primal), in_hbm(source)
    stream = [pltpu.VMEM(whole.shape, jnp.float32), pltpu.SemaphoreType.DMA((STEPS,))]
    half, rest = struct(FIELDS, HALF, *plane), struct(FIELDS, HALF - 1, *plane)
    added = struct(2, FIELDS, HALO, *plane)

    def march_first(start, low, high, forced):
        later = (struct(STEPS - HALF - 1, *slab.shape),) if forced else ()
        return call(
            functools.partial(march_first_kernel, STEPS, forced),
            (slab, added) + later,
            (mixing, source, start, low, high, slope, packed_low, packed_high),
            [SMEM, HBM],
            42,
            scratch=march_room + stream,
        )

    slope, slope_share, up, down, up_rest, down_rest = call(
        guess_kernel,
        (whole, share, half, half, half, half),
        (mixing, primal, source, guess),
        [SMEM, HBM, HBM],
        100,
        scratch=[stream[0], stream[0], room, room, pltpu.SemaphoreType.DMA((2, STEPS))],
    )
    low, high = exchange(up, down)
    low_rest, high_rest = exchange(up_rest, down_rest)
    middle, middle_added, later = march_first(guess[0], low, high, True)
    (ended,) = call(
        end_kernel,
        (slab,),
        (mixing, later, middle, middle_added, low_rest, high_rest, slope, packed_low, packed_high),
        [SMEM],
        46,
        scratch=march_room,
    )
    ended = from_behind(ended)
    slope_shares = lax.all_to_all(slope_share, "tm", 0, 0)
    relaxed, change, middle, up, down = call(
        relaxed_kernel,
        (slab, slab, slab, half, half),
        (mixing, leads, source, ended, guess, slope),
        [SMEM, SMEM, HBM],
        30,
        scratch=[pltpu.VMEM((1,) + slab.shape, jnp.float32), room, room, room, stream[1]],
        first_out=HBM,
    )
    low, high = exchange(up, down)
    up_rest, down_rest = call(
        functools.partial(rest_kernel, STEPS, False),
        (half, half),
        (mixing, source, middle, slope),
        [SMEM, HBM],
        20,
        scratch=[room, room] + stream,
    )
    low_rest, high_rest = exchange(up_rest, down_rest)
    middle, middle_added = march_first(change, low, high, False)
    change, change_share = call(
        change_kernel,
        (slab, share),
        (mixing, leads, source, middle, middle_added, low_rest, high_rest, slope, packed_low, packed_high),
        [SMEM, SMEM, HBM],
        50,
        scratch=march_room + [pltpu.VMEM((1,) + slab.shape, jnp.float32), room, stream[1]],
        first_out=HBM,
    )
    change_shares = lax.all_to_all(change_share, "tm", 0, 0)
    residual = jnp.where(leading, first_source, from_behind(change))
    (error_shares,) = call(scan_kernel, (share,), (mixing, slope_shares, change_shares), [SMEM], 16)
    error_share = lax.all_to_all(error_shares, "tm", 0, 0)
    corrected, middle, up, down = call(
        corrected_kernel,
        (slab, slab, half, half),
        (mixing, leads, relaxed, source, error_share, slope),
        [SMEM, SMEM, HBM, HBM],
        30,
        scratch=[room, stream[0], room, room, pltpu.SemaphoreType.DMA((STEPS + 1,))],
    )
    low, high = exchange(up, down)
    up_rest, down_rest = call(
        functools.partial(rest_kernel, STEPS - 1, True),
        (rest, rest),
        (mixing, source, middle, slope),
        [SMEM, HBM],
        16,
        scratch=[room, room] + stream,
    )
    low_rest, high_rest = exchange(up_rest, down_rest)
    states_room = march_room + [stream[0], stream[0], stream[1], stream[1]]
    later = struct(STEPS - HALF - 1, *slab.shape)
    earlier, middle, middle_added, later = call(
        states_first_kernel,
        (whole, slab, added, later),
        (mixing, source, corrected, low, high, slope, packed_low, packed_high),
        [SMEM, HBM],
        42,
        scratch=states_room,
        first_out=HBM,
    )
    (fine_states,) = call(
        states_rest_kernel,
        (whole,),
        (mixing, earlier, later, middle, middle_added, low_rest, high_rest, slope, packed_low, packed_high),
        [SMEM, HBM],
        34,
        scratch=march_room + [stream[0], stream[1]],
        first_out=HBM,
        alias={1: 0},
    )
    return fine_states, residual[None]


def solution(mesh):
    split = P("tm", None, "space", None, None)
    return jax.shard_map(
        per_device,
        mesh=mesh,
        in_specs=(split, split, split, P()),
        out_specs=(split, split),
        check_vma=False,
    )
```

time: 177 us -> 162 us (0.915)
  the two profiles are of different devices: /device:TPU:6 before, /device:TPU:1 now
where the time goes in v2:
time: 162 us; the launch traced here: 161 us
  starting transfers between devices  53.2 us (33%)
  Pallas kernels  44.2 us (27%)
  waiting for transfers between devices  32 us (20%)
  blocking collectives  25.2 us (16%)
  local copies, waits for them, and re-layouts  3.95 us (2%)
  other arithmetic  1.84 us (1%)
    pallas_call x13, Pallas kernels, call(): pl.pallas_call(kernel, input_output_aliases=alias or {}, out_shape=out, i...  44.2 us
    all_to_all x1, blocking collectives, per_device(): change_shares = lax.all_to_all(change_share, 'tm', 0, 0)  25.2 us
    ppermute x7, starting transfers between devices, exchange(): lax.ppermute(down, 'space', backward)  24.1 us
    all_to_all x1, starting transfers between devices, per_device(): slope_shares = lax.all_to_all(slope_share, 'tm', 0, 0)  13.2 us
    ppermute x7, waiting for transfers between devices, exchange(): lax.ppermute(up, 'space', forward)  12.7 us
    ppermute x2, waiting for transfers between devices, from_behind(): return lax.ppermute(array, 'tm', [(i, i + 1) for i in range(count - 1)])  9.84 us
    all_to_all x1, waiting for transfers between devices, per_device(): error_share = lax.all_to_all(error_shares, 'tm', 0, 0)  9.42 us
    ppermute x2, starting transfers between devices, from_behind(): return lax.ppermute(array, 'tm', [(i, i + 1) for i in range(count - 1)])  8.87 us
  transfers between devices with their start and end apart: 18, of which 3 were waited for; matrix products, arithmetic and copies ran while one was open for 1% of the time, Pallas kernels for 22%

profile of v2, /device:TPU:1, one launch (start us, length us, event | category | flops | bytes accessed | tf_op | source)
XLA Modules:
  0.0 161.4 jit_solution(264265563065220758)
XLA Ops:
  1.3 3.5 %shard_map.60 = (f32[5,12,16,128]{3,2,1,0:T(8,128)}, f32[5,12,16,128]{3,2,1,0:T(8,128)}) custom-call(f32[5,5]{1,0:T(8,128)S(1)} %copy-done.1, f32[8,5,8,16,128]{4,3,2,1,0:T(8,128)} %primal_hbm.3), custom_call_target="tpu_custom_call" | custom-call | flops 6144000 | bytes 3604580 | tf_op jit(solution)/shard_map/pallas_call | solution.py:432
  4.8 2.5 %collective-permute-start.2 = (f32[5,12,16,128]{3,2,1,0:T(8,128)}, f32[5,12,16,128]{3,2,1,0:T(8,128)S(1)}, u32[]{:S(2)}, u32[]{:S(2)}) collective-permute-start(f32[5,12,16,128]{3,2,1,0:T(8,128)} %get-tuple-element.37), channel_id=1, source_target_pairs={{0,1},{1,2},{2,3},{3,4},{4,5},{5,6},{6,7},{7,0},{8,9},{9,10},{10,1... | collective-permute-start | bytes 1474568 | tf_op jit(solution)/shard_map/ppermute | solution.py:463
  7.4 2.5 %collective-permute-start.3 = (f32[5,12,16,128]{3,2,1,0:T(8,128)}, f32[5,12,16,128]{3,2,1,0:T(8,128)}, u32[]{:S(2)}, u32[]{:S(2)}) collective-permute-start(f32[5,12,16,128]{3,2,1,0:T(8,128)} %get-tuple-element.38), channel_id=1, source_target_pairs={{1,0},{2,1},{3,2},{4,3},{5,4},{6,5},{7,6},{0,7},{9,8},{10,9},{11,1... | collective-permute-start | bytes 1474568 | tf_op jit(solution)/shard_map/ppermute | solution.py:463
  9.9 6.3 %shard_map.59 = (f32[8,5,8,16,128]{4,3,2,1,0:T(8,128)S(1)}, f32[32,5,4,128]{3,2,1,0:T(4,128)S(1)}, f32[5,4,16,128]{3,2,1,0:T(8,128)S(1)}, f32[5,4,16,128]{3,2,1,...) custom-call(f32[5,5]{1,0:T(8,128)S(1)} %copy-done.1, f32[8,5,8,16,128]{4,3,2,1,0:T(8,128)} %primal_hbm.3, ...), custom_call_target="tpu_custom_call" | custom-call | flops 25600000 | bytes 9175140 | tf_op jit(solution)/shard_map/pallas_call | solution.py:432
  16.9 3.6 %collective-permute-start.1 = (f32[5,4,16,128]{3,2,1,0:T(8,128)}, f32[5,4,16,128]{3,2,1,0:T(8,128)}, u32[]{:S(2)}, u32[]{:S(2)}) collective-permute-start(f32[5,4,16,128]{3,2,1,0:T(8,128)} %get-tuple-element.35), channel_id=1, source_target_pairs={{1,0},{2,1},{3,2},{4,3},{5,4},{6,5},{7,6},{0,7},{9,8},{10,9},{11,1... | collective-permute-start | bytes 491528 | tf_op jit(solution)/shard_map/ppermute | solution.py:463
  20.5 12.7 %collective-permute-done.low_ref = f32[5,4,16,128]{3,2,1,0:T(8,128)S(1)} collective-permute-done((f32[5,4,16,128]{3,2,1,0:T(8,128)S(1)}, f32[5,4,16,128]{3,2,1,0:T(8,128)S(1)}, u32[]{:S(2)}, u32[]{:S(2)}) %collective-permute-start) | collective-permute-done | bytes 163872 | tf_op jit(solution)/shard_map/ppermute | solution.py:463
  33.9 2.9 %collective-permute-start.5 = (f32[5,4,16,128]{3,2,1,0:T(8,128)}, f32[5,4,16,128]{3,2,1,0:T(8,128)}, u32[]{:S(2)}, u32[]{:S(2)}) collective-permute-start(f32[5,4,16,128]{3,2,1,0:T(8,128)} %get-tuple-element.43), channel_id=1, source_target_pairs={{1,0},{2,1},{3,2},{4,3},{5,4},{6,5},{7,6},{0,7},{9,8},{10,9},{11,1... | collective-permute-start | bytes 491528 | tf_op jit(solution)/shard_map/ppermute | solution.py:463
  36.8 13.2 %all-to-all-start = ((f32[32,5,4,128]{3,2,1,0:T(4,128)}), f32[32,5,4,128]{3,2,1,0:T(4,128)}, u32[]{:S(2)}, u32[]{:S(2)}) async-start(f32[32,5,4,128]{3,2,1,0:T(4,128)} %copy-done.3), calls=%async_computation | async-start | bytes 655360 | tf_op jit(solution)/shard_map/all_to_all | solution.py:526
  50.1 0.9 copy-done.6
  51.0 4.1 %shard_map.61 = (f32[5,8,16,128]{3,2,1,0:T(8,128)S(1)}, f32[2,5,4,16,128]{4,3,2,1,0:T(8,128)S(1)}, f32[3,5,8,16,128]{4,3,2,1,0:T(8,128)S(1)}) custom-call(f32[5,5]{1,0:T(8,128)S(1)} %copy-done.2, f32[8,5,8,16,128]{4,3,2,1,0:T(8,128)} %source_hbm.17, f32[5,8,16,128]{3,2,1,0:T(8,128)S(1)} %bitcast.8, f32[5,4,16,128]{3,2,1,0:T(8,128)S(1)} %copy-done.6, ...), custom_call_target="tpu_custom_call" | custom-call | flops 10752000 | bytes 8519780 | tf_op jit(solution)/shard_map/pallas_call | solution.py:432
  55.1 3.9 %shard_map.62 = f32[5,8,16,128]{3,2,1,0:T(8,128)} custom-call(f32[5,5]{1,0:T(8,128)S(1)} %copy-done.2, f32[3,5,8,16,128]{4,3,2,1,0:T(8,128)S(1)} %get-tuple-element.39.later_ref, f32[5,8,16,128]{3,2,1,0:T(8,128)S(1)} %get-tuple-element.40.middle_ref, f32[2,5,4,16,128]{4,3,2,1,0:T(8,128)S(1)} %get-tuple-element.41.middle_added, ...), custom_call_target="tpu_custom_call" | custom-call | flops 11776000 | bytes 5898340 | tf_op jit(solution)/shard_map/pallas_call | solution.py:432
  59.0 4.4 %collective-permute-start.6 = (f32[5,8,16,128]{3,2,1,0:T(8,128)}, f32[5,8,16,128]{3,2,1,0:T(8,128)}, u32[]{:S(2)}, u32[]{:S(2)}) collective-permute-start(f32[5,8,16,128]{3,2,1,0:T(8,128)} %shard_map.62), channel_id=1, source_target_pairs={{0,8},{8,16},{16,24},{24,32},{32,40},{40,48},{48,56},{56,64},{64,7... | collective-permute-start | bytes 983048 | tf_op jit(solution)/shard_map/ppermute | solution.py:456
  63.5 9.8 %collective-permute-done.6.ended_ref = f32[5,8,16,128]{3,2,1,0:T(8,128)} collective-permute-done((f32[5,8,16,128]{3,2,1,0:T(8,128)}, f32[5,8,16,128]{3,2,1,0:T(8,128)}, u32[]{:S(2)}, u32[]{:S(2)}) %collective-permute-start.6) | collective-permute-done | bytes 327712 | tf_op jit(solution)/shard_map/ppermute | solution.py:456
  73.3 3.0 %shard_map.63 = (f32[5,8,16,128]{3,2,1,0:T(8,128)}, f32[5,8,16,128]{3,2,1,0:T(8,128)S(1)}, f32[5,8,16,128]{3,2,1,0:T(8,128)S(1)}, f32[5,4,16,128]{3,2,1,0:T(8,128)S(1)}, f32[5,4,16,128]{3,2,1,0:T(8,128)S(1)}) custom-call(f32[5,5]{1,0:T(8,128)S(1)} %copy-done.2, s32[1]{0:T(128)} %bitcast.leads_ref, f32[8,5,8,16,128]{4,3,2,1,0:T(8,128)} %source_hbm.17, ...), custom_call_target="tpu_custom_call" | custom-call | flops 7680000 | bytes 7209064 | tf_op jit(solution)/shard_map/pallas_call | solution.py:432
  76.4 3.6 %collective-permute-start.8 = (f32[5,4,16,128]{3,2,1,0:T(8,128)S(1)}, f32[5,4,16,128]{3,2,1,0:T(8,128)S(1)}, u32[]{:S(2)}, u32[]{:S(2)}) collective-permute-start(f32[5,4,16,128]{3,2,1,0:T(8,128)S(1)} %get-tuple-element.48), channel_id=1, source_target_pairs={{1,0},{2,1},{3,2},{4,3},{5,4},{6,5},{7,6},{0,7},{9,8},{10,9},{11,1... | collective-permute-start | bytes 491528 | tf_op jit(solution)/shard_map/ppermute | solution.py:463
  79.9 1.3 shard_map.65
  81.3 3.6 %collective-permute-start.10 = (f32[5,4,16,128]{3,2,1,0:T(8,128)S(1)}, f32[5,4,16,128]{3,2,1,0:T(8,128)S(1)}, u32[]{:S(2)}, u32[]{:S(2)}) collective-permute-start(f32[5,4,16,128]{3,2,1,0:T(8,128)S(1)} %get-tuple-element.53), channel_id=1, source_target_pairs={{1,0},{2,1},{3,2},{4,3},{5,4},{6,5},{7,6},{0,7},{9,8},{10,9},{11,1... | collective-permute-start | bytes 491528 | tf_op jit(solution)/shard_map/ppermute | solution.py:463
  84.9 3.0 %shard_map.64 = (f32[5,8,16,128]{3,2,1,0:T(8,128)S(1)}, f32[2,5,4,16,128]{4,3,2,1,0:T(8,128)S(1)}) custom-call(f32[5,5]{1,0:T(8,128)S(1)} %copy-done.2, f32[8,5,8,16,128]{4,3,2,1,0:T(8,128)} %source_hbm.17, f32[5,8,16,128]{3,2,1,0:T(8,128)S(1)} %get-tuple-element.46.start_ref, f32[5,4,16,128]{3,2,1,0:T(8,128)S(1)} %collective-permute-done.7.low_ref, ...), custom_call_target="tpu_custom_call" | custom-call | flops 10752000 | bytes 7536740 | tf_op jit(solution)/shard_map/pallas_call | solution.py:432
  88.0 3.8 %shard_map.66 = (f32[5,8,16,128]{3,2,1,0:T(8,128)}, f32[32,5,4,128]{3,2,1,0:T(4,128)S(1)}) custom-call(f32[5,5]{1,0:T(8,128)S(1)} %copy-done.2, s32[1]{0:T(128)} %bitcast.leads_ref, f32[8,5,8,16,128]{4,3,2,1,0:T(8,128)} %source_hbm.17, f32[5,8,16,128]{3,2,1,0:T(8,128)S(1)} %get-tuple-element.49.middle_ref, ...), custom_call_target="tpu_custom_call" | custom-call | flops 12800000 | bytes 7864424 | tf_op jit(solution)/shard_map/pallas_call | solution.py:432
  91.7 25.2 %all_to_all.15.resid_ref = f32[32,5,4,128]{3,2,1,0:T(4,128)S(1)} all-to-all(f32[32,5,4,128]{3,2,1,0:T(4,128)S(1)} %get-tuple-element.54), channel_id=1, replica_groups=mesh['tm'=32,'space'=8] {'tm'}, dimensions={0} | all-to-all | bytes 655360 | tf_op jit(solution)/shard_map/all_to_all | solution.py:556
  117.0 2.2 %shard_map.67 = f32[32,5,4,128]{3,2,1,0:T(4,128)} custom-call(f32[5,5]{1,0:T(8,128)S(1)} %copy-done.2, f32[32,5,4,128]{3,2,1,0:T(4,128)} %all-to-all-done.slope_ref, f32[32,5,4,128]{3,2,1,0:T(4,128)S(1)} %all_to_all.15.resid_ref), custom_call_target="tpu_custom_call" | custom-call | flops 4096000 | bytes 983140 | tf_op jit(solution)/shard_map/pallas_call | solution.py:432
  119.2 4.2 %all-to-all-start.2 = ((f32[32,5,4,128]{3,2,1,0:T(4,128)}), f32[32,5,4,128]{3,2,1,0:T(4,128)S(1)}, u32[]{:S(2)}, u32[]{:S(2)}) async-start(f32[32,5,4,128]{3,2,1,0:T(4,128)} %shard_map.67), calls=%async_computation.2 | async-start | bytes 655360 | tf_op jit(solution)/shard_map/all_to_all | solution.py:559
  123.4 4.4 %collective-permute-start.15 = (f32[5,8,16,128]{3,2,1,0:T(8,128)}, f32[5,8,16,128]{3,2,1,0:T(8,128)}, u32[]{:S(2)}, u32[]{:S(2)}) collective-permute-start(f32[5,8,16,128]{3,2,1,0:T(8,128)} %get-tuple-element.65), channel_id=1, source_target_pairs={{0,8},{8,16},{16,24},{24,32},{32,40},{40,48},{48,56},{56,64},{64,7... | collective-permute-start | bytes 983048 | tf_op jit(solution)/shard_map/ppermute | solution.py:456
  127.8 9.4 %all-to-all-done.2.share_ref = f32[32,5,4,128]{3,2,1,0:T(4,128)S(1)} async-done(((f32[32,5,4,128]{3,2,1,0:T(4,128)}), f32[32,5,4,128]{3,2,1,0:T(4,128)S(1)}, u32[]{:S(2)}, u32[]{:S(2)}) %all-to-all-start.2) | async-done | bytes 327712 | tf_op jit(solution)/shard_map/all_to_all | solution.py:559
  137.3 1.0 copy-done.4
  138.2 2.7 %shard_map.68 = (f32[5,8,16,128]{3,2,1,0:T(8,128)S(1)}, f32[5,8,16,128]{3,2,1,0:T(8,128)S(1)}, f32[5,4,16,128]{3,2,1,0:T(8,128)S(1)}, f32[5,4,16,128]{3,2,1,0:T(8,128)S(1)}) custom-call(f32[5,5]{1,0:T(8,128)S(1)} %copy-done.2, s32[1]{0:T(128)} %bitcast.leads_ref, f32[5,8,16,128]{3,2,1,0:T(8,128)S(1)} %copy-done.4, f32[8,5,8,16,128]{4,3,2,1,0:T(8,128)} %source_hbm.17, ...), custom_call_target="tpu_custom_call" | custom-call | flops 7680000 | bytes 6881384 | tf_op jit(solution)/shard_map/pallas_call | solution.py:432
  141.1 4.3 %collective-permute-start.12 = (f32[5,4,16,128]{3,2,1,0:T(8,128)S(1)}, f32[5,4,16,128]{3,2,1,0:T(8,128)S(1)}, u32[]{:S(2)}, u32[]{:S(2)}) collective-permute-start(f32[5,4,16,128]{3,2,1,0:T(8,128)S(1)} %get-tuple-element.57), channel_id=1, source_target_pairs={{1,0},{2,1},{3,2},{4,3},{5,4},{6,5},{7,6},{0,7},{9,8},{10,9},{11,1... | collective-permute-start | bytes 491528 | tf_op jit(solution)/shard_map/ppermute | solution.py:463
  145.4 2.1 %shard_map.70 = (f32[5,3,16,128]{3,2,1,0:T(8,128)S(1)}, f32[5,3,16,128]{3,2,1,0:T(8,128)S(1)}) custom-call(f32[5,5]{1,0:T(8,128)S(1)} %copy-done.2, f32[8,5,8,16,128]{4,3,2,1,0:T(8,128)} %source_hbm.17, f32[5,8,16,128]{3,2,1,0:T(8,128)S(1)} %get-tuple-element.62.middle_ref, f32[8,5,8,16,128]{4,3,2,1,0:T(8,128)S(1)} %get-tuple-element.36.slope_ref), custom_call_target="tpu_custom_call" | custom-call | flops 4096000 | bytes 5816420 | tf_op jit(solution)/shard_map/pallas_call | solution.py:432
  147.6 3.6 %collective-permute-start.14 = (f32[5,3,16,128]{3,2,1,0:T(8,128)S(1)}, f32[5,3,16,128]{3,2,1,0:T(8,128)S(1)}, u32[]{:S(2)}, u32[]{:S(2)}) collective-permute-start(f32[5,3,16,128]{3,2,1,0:T(8,128)S(1)} %get-tuple-element.64), channel_id=1, source_target_pairs={{1,0},{2,1},{3,2},{4,3},{5,4},{6,5},{7,6},{0,7},{9,8},{10,9},{11,1... | collective-permute-start | bytes 368648 | tf_op jit(solution)/shard_map/ppermute | solution.py:463
  151.2 1.8 %fusion = f32[1,5,8,16,128]{4,3,2,1,0:T(8,128)} fusion(f32[5,8,16,128]{3,2,1,0:T(8,128)} %collective-permute-done.15, f32[8,5,8,16,128]{4,3,2,1,0:T(8,128)} %source_hbm.17, pred[]{:T(512)S(6)} %eq.3), kind=kLoop, calls=%fused_computation.1 | loop fusion | flops 81920 | bytes 983041 | tf_op jit(solution)/shard_map/broadcast_in_dim | solution.py:599
  153.0 4.9 %shard_map.69 = (f32[8,5,8,16,128]{4,3,2,1,0:T(8,128)}, f32[5,8,16,128]{3,2,1,0:T(8,128)S(1)}, f32[2,5,4,16,128]{4,3,2,1,0:T(8,128)S(1)}, f32[3,5,8,16,128]{4,3,2,1,0:T(8,128)S(1)}) custom-call(f32[5,5]{1,0:T(8,128)S(1)} %copy-done.2, f32[8,5,8,16,128]{4,3,2,1,0:T(8,128)} %source_hbm.17, f32[5,8,16,128]{3,2,1,0:T(8,128)S(1)} %get-tuple-element.55.start_ref, ...), custom_call_target="tpu_custom_call" | custom-call | flops 10752000 | bytes 11141220 | tf_op jit(solution)/shard_map/pallas_call | solution.py:432
  158.0 3.2 %shard_map.71 = f32[8,5,8,16,128]{4,3,2,1,0:T(8,128)} custom-call(f32[5,5]{1,0:T(8,128)S(1)} %copy-done.2, f32[8,5,8,16,128]{4,3,2,1,0:T(8,128)} %get-tuple-element.58.earlier_hbm, f32[3,5,8,16,128]{4,3,2,1,0:T(8,128)S(1)} %get-tuple-element.59.later_ref, f32[5,8,16,128]{3,2,1,0:T(8,128)S(1)} %get-tuple-element.60.middle_ref, ...), custom_call_target="tpu_custom_call", output_to_operand_aliasing={{}: (1, {})} | custom-call | flops 8704000 | bytes 10731620 | tf_op jit(solution)/shard_map/pallas_call | solution.py:432
  (33 shorter events, 2.5 us)
Async XLA Ops:
  0.6 0.7 copy-start.1
  1.3 8.6 %copy-start = (f32[1,5,8,16,128]{4,3,2,1,0:T(8,128)S(1)}, f32[1,5,8,16,128]{4,3,2,1,0:T(8,128)}, u32[]{:S(2)}) copy-start(f32[1,5,8,16,128]{4,3,2,1,0:T(8,128)} %guess_ref.3) | copy-start | bytes 983044
  4.8 45.2 %collective-permute-start.2 = (f32[5,12,16,128]{3,2,1,0:T(8,128)}, f32[5,12,16,128]{3,2,1,0:T(8,128)S(1)}, u32[]{:S(2)}, u32[]{:S(2)}) collective-permute-start(f32[5,12,16,128]{3,2,1,0:T(8,128)} %get-tuple-element.37), channel_id=1, source_target_pairs={{0,1},{1,2},{2,3},{3,4},{4,5},{5,6},{6,7},{7,0},{8,9},{9,10},{10,1... | collective-permute-start | bytes 1474568 | tf_op jit(solution)/shard_map/ppermute | solution.py:463
  7.4 42.7 %copy-start.2 = (f32[5,5]{1,0:T(8,128)S(1)}, f32[5,5]{1,0:T(8,128)}, u32[]{:S(2)}) copy-start(f32[5,5]{1,0:T(8,128)} %mix_ref.25) | copy-start | bytes 304
  7.4 42.7 %collective-permute-start.3 = (f32[5,12,16,128]{3,2,1,0:T(8,128)}, f32[5,12,16,128]{3,2,1,0:T(8,128)}, u32[]{:S(2)}, u32[]{:S(2)}) collective-permute-start(f32[5,12,16,128]{3,2,1,0:T(8,128)} %get-tuple-element.38), channel_id=1, source_target_pairs={{1,0},{2,1},{3,2},{4,3},{5,4},{6,5},{7,6},{0,7},{9,8},{10,9},{11,1... | collective-permute-start | bytes 1474568 | tf_op jit(solution)/shard_map/ppermute | solution.py:463
  16.2 0.7 copy-start.3
  16.9 16.3 %collective-permute-start = (f32[5,4,16,128]{3,2,1,0:T(8,128)S(1)}, f32[5,4,16,128]{3,2,1,0:T(8,128)S(1)}, u32[]{:S(2)}, u32[]{:S(2)}) collective-permute-start(f32[5,4,16,128]{3,2,1,0:T(8,128)S(1)} %get-tuple-element.34), channel_id=1, source_target_pairs={{0,1},{1,2},{2,3},{3,4},{4,5},{5,6},{6,7},{7,0},{8,9},{9,10},{10,1... | collective-permute-start | bytes 491528 | tf_op jit(solution)/shard_map/ppermute | solution.py:463
  16.9 33.1 %collective-permute-start.1 = (f32[5,4,16,128]{3,2,1,0:T(8,128)}, f32[5,4,16,128]{3,2,1,0:T(8,128)}, u32[]{:S(2)}, u32[]{:S(2)}) collective-permute-start(f32[5,4,16,128]{3,2,1,0:T(8,128)} %get-tuple-element.35), channel_id=1, source_target_pairs={{1,0},{2,1},{3,2},{4,3},{5,4},{6,5},{7,6},{0,7},{9,8},{10,9},{11,1... | collective-permute-start | bytes 491528 | tf_op jit(solution)/shard_map/ppermute | solution.py:463
  20.5 34.6 %collective-permute-start.4 = (f32[5,4,16,128]{3,2,1,0:T(8,128)}, f32[5,4,16,128]{3,2,1,0:T(8,128)}, u32[]{:S(2)}, u32[]{:S(2)}) collective-permute-start(f32[5,4,16,128]{3,2,1,0:T(8,128)} %get-tuple-element.42), channel_id=1, source_target_pairs={{0,1},{1,2},{2,3},{3,4},{4,5},{5,6},{6,7},{7,0},{8,9},{9,10},{10,1... | collective-permute-start | bytes 491528 | tf_op jit(solution)/shard_map/ppermute | solution.py:463
  33.2 0.7 copy-start.5
  33.9 21.2 %collective-permute-start.5 = (f32[5,4,16,128]{3,2,1,0:T(8,128)}, f32[5,4,16,128]{3,2,1,0:T(8,128)}, u32[]{:S(2)}, u32[]{:S(2)}) collective-permute-start(f32[5,4,16,128]{3,2,1,0:T(8,128)} %get-tuple-element.43), channel_id=1, source_target_pairs={{1,0},{2,1},{3,2},{4,3},{5,4},{6,5},{7,6},{0,7},{9,8},{10,9},{11,1... | collective-permute-start | bytes 491528 | tf_op jit(solution)/shard_map/ppermute | solution.py:463
  36.8 54.9 %all-to-all-start = ((f32[32,5,4,128]{3,2,1,0:T(4,128)}), f32[32,5,4,128]{3,2,1,0:T(4,128)}, u32[]{:S(2)}, u32[]{:S(2)}) async-start(f32[32,5,4,128]{3,2,1,0:T(4,128)} %copy-done.3), calls=%async_computation | async-start | bytes 655360 | tf_op jit(solution)/shard_map/all_to_all | solution.py:526
  50.1 0.9 copy-start.6
  59.0 14.3 %collective-permute-start.6 = (f32[5,8,16,128]{3,2,1,0:T(8,128)}, f32[5,8,16,128]{3,2,1,0:T(8,128)}, u32[]{:S(2)}, u32[]{:S(2)}) collective-permute-start(f32[5,8,16,128]{3,2,1,0:T(8,128)} %shard_map.62), channel_id=1, source_target_pairs={{0,8},{8,16},{16,24},{24,32},{32,40},{40,48},{48,56},{56,64},{64,7... | collective-permute-start | bytes 983048 | tf_op jit(solution)/shard_map/ppermute | solution.py:456
  76.3 8.6 %collective-permute-start.7 = (f32[5,4,16,128]{3,2,1,0:T(8,128)S(1)}, f32[5,4,16,128]{3,2,1,0:T(8,128)S(1)}, u32[]{:S(2)}, u32[]{:S(2)}) collective-permute-start(f32[5,4,16,128]{3,2,1,0:T(8,128)S(1)} %get-tuple-element.47), channel_id=1, source_target_pairs={{0,1},{1,2},{2,3},{3,4},{4,5},{5,6},{6,7},{7,0},{8,9},{9,10},{10,1... | collective-permute-start | bytes 491528 | tf_op jit(solution)/shard_map/ppermute | solution.py:463
  76.4 8.6 %collective-permute-start.8 = (f32[5,4,16,128]{3,2,1,0:T(8,128)S(1)}, f32[5,4,16,128]{3,2,1,0:T(8,128)S(1)}, u32[]{:S(2)}, u32[]{:S(2)}) collective-permute-start(f32[5,4,16,128]{3,2,1,0:T(8,128)S(1)} %get-tuple-element.48), channel_id=1, source_target_pairs={{1,0},{2,1},{3,2},{4,3},{5,4},{6,5},{7,6},{0,7},{9,8},{10,9},{11,1... | collective-permute-start | bytes 491528 | tf_op jit(solution)/shard_map/ppermute | solution.py:463
  81.3 6.7 %collective-permute-start.9 = (f32[5,4,16,128]{3,2,1,0:T(8,128)S(1)}, f32[5,4,16,128]{3,2,1,0:T(8,128)S(1)}, u32[]{:S(2)}, u32[]{:S(2)}) collective-permute-start(f32[5,4,16,128]{3,2,1,0:T(8,128)S(1)} %get-tuple-element.52), channel_id=1, source_target_pairs={{0,1},{1,2},{2,3},{3,4},{4,5},{5,6},{6,7},{7,0},{8,9},{9,10},{10,1... | collective-permute-start | bytes 491528 | tf_op jit(solution)/shard_map/ppermute | solution.py:463
  81.3 6.6 %collective-permute-start.10 = (f32[5,4,16,128]{3,2,1,0:T(8,128)S(1)}, f32[5,4,16,128]{3,2,1,0:T(8,128)S(1)}, u32[]{:S(2)}, u32[]{:S(2)}) collective-permute-start(f32[5,4,16,128]{3,2,1,0:T(8,128)S(1)} %get-tuple-element.53), channel_id=1, source_target_pairs={{1,0},{2,1},{3,2},{4,3},{5,4},{6,5},{7,6},{0,7},{9,8},{10,9},{11,1... | collective-permute-start | bytes 491528 | tf_op jit(solution)/shard_map/ppermute | solution.py:463
  119.2 18.1 %all-to-all-start.2 = ((f32[32,5,4,128]{3,2,1,0:T(4,128)}), f32[32,5,4,128]{3,2,1,0:T(4,128)S(1)}, u32[]{:S(2)}, u32[]{:S(2)}) async-start(f32[32,5,4,128]{3,2,1,0:T(4,128)} %shard_map.67), calls=%async_computation.2 | async-start | bytes 655360 | tf_op jit(solution)/shard_map/all_to_all | solution.py:559
  123.4 27.8 %collective-permute-start.15 = (f32[5,8,16,128]{3,2,1,0:T(8,128)}, f32[5,8,16,128]{3,2,1,0:T(8,128)}, u32[]{:S(2)}, u32[]{:S(2)}) collective-permute-start(f32[5,8,16,128]{3,2,1,0:T(8,128)} %get-tuple-element.65), channel_id=1, source_target_pairs={{0,8},{8,16},{16,24},{24,32},{32,40},{40,48},{48,56},{56,64},{64,7... | collective-permute-start | bytes 983048 | tf_op jit(solution)/shard_map/ppermute | solution.py:456
  137.3 1.0 copy-start.4
  141.0 12.1 %collective-permute-start.11 = (f32[5,4,16,128]{3,2,1,0:T(8,128)S(1)}, f32[5,4,16,128]{3,2,1,0:T(8,128)S(1)}, u32[]{:S(2)}, u32[]{:S(2)}) collective-permute-start(f32[5,4,16,128]{3,2,1,0:T(8,128)S(1)} %get-tuple-element.56), channel_id=1, source_target_pairs={{0,1},{1,2},{2,3},{3,4},{4,5},{5,6},{6,7},{7,0},{8,9},{9,10},{10,1... | collective-permute-start | bytes 491528 | tf_op jit(solution)/shard_map/ppermute | solution.py:463
  141.1 12.0 %collective-permute-start.12 = (f32[5,4,16,128]{3,2,1,0:T(8,128)S(1)}, f32[5,4,16,128]{3,2,1,0:T(8,128)S(1)}, u32[]{:S(2)}, u32[]{:S(2)}) collective-permute-start(f32[5,4,16,128]{3,2,1,0:T(8,128)S(1)} %get-tuple-element.57), channel_id=1, source_target_pairs={{1,0},{2,1},{3,2},{4,3},{5,4},{6,5},{7,6},{0,7},{9,8},{10,9},{11,1... | collective-permute-start | bytes 491528 | tf_op jit(solution)/shard_map/ppermute | solution.py:463
  147.5 10.5 %collective-permute-start.13 = (f32[5,3,16,128]{3,2,1,0:T(8,128)S(1)}, f32[5,3,16,128]{3,2,1,0:T(8,128)S(1)}, u32[]{:S(2)}, u32[]{:S(2)}) collective-permute-start(f32[5,3,16,128]{3,2,1,0:T(8,128)S(1)} %get-tuple-element.63), channel_id=1, source_target_pairs={{0,1},{1,2},{2,3},{3,4},{4,5},{5,6},{6,7},{7,0},{8,9},{9,10},{10,1... | collective-permute-start | bytes 368648 | tf_op jit(solution)/shard_map/ppermute | solution.py:463
  147.6 10.4 %collective-permute-start.14 = (f32[5,3,16,128]{3,2,1,0:T(8,128)S(1)}, f32[5,3,16,128]{3,2,1,0:T(8,128)S(1)}, u32[]{:S(2)}, u32[]{:S(2)}) collective-permute-start(f32[5,3,16,128]{3,2,1,0:T(8,128)S(1)} %get-tuple-element.64), channel_id=1, source_target_pairs={{1,0},{2,1},{3,2},{4,3},{5,4},{6,5},{7,6},{0,7},{9,8},{10,9},{11,1... | collective-permute-start | bytes 368648 | tf_op jit(solution)/shard_map/ppermute | solution.py:463

commit v3 on v2

--- a/solution.py
+++ b/solution.py
@@ -132,7 +132,7 @@
                 ends[(m + 1) // HALF][int(x == 0)][f, (m + 1) % HALF] = new[f]
 
 
-def guess_kernel(mix_ref, primal_hbm, source_hbm, guess_ref, slope_ref, share_ref, up_one, down_one, up_two, down_two, primal, source_ref, one, two, sems):
+def guess_kernel(mix_ref, primal_hbm, source_hbm, guess_ref, share_hbm, slope_ref, up_one, down_one, up_two, down_two, primal, source_ref, one, two, share_ref, sems):
     mix = scalars(mix_ref)
     primal_in = Streamed(primal_hbm, primal, sems.at[0], range(STEPS))
     source_in = Streamed(source_hbm, source_ref, sems.at[1], range(1, STEPS))
@@ -158,10 +158,13 @@
             for share, x, row in shares(4):
                 for f in range(FIELDS):
                     share_ref[share, f] = slope_ref[0, f, x, row : row + 4]
+            share_out = pltpu.make_async_copy(share_ref, share_hbm, sems.at[1, 0])
+            share_out.start()
         source_in.ready(t + 1)
         if t + 1 < STEPS:
             here = start_ref if t == 0 else buffers[t % 2]
             alone_step(mix, t, here, buffers[(t + 1) % 2], slope_ref, source_ref, ends)
+    share_out.wait()
 
 
 def relaxed_kernel(mix_ref, leads_ref, source_hbm, ended_ref, guess_ref, slope_ref, relaxed_hbm, change_ref, middle_ref, up_ref, down_ref, source_ref, relaxed_ref, one, two, sems):
@@ -187,7 +190,11 @@
     relaxed_out.wait()
 
 
-def rest_kernel(count, forced, mix_ref, source_hbm, middle_ref, slope_ref, up_ref, down_ref, one, two, source_ref, sems):
+def rest_kernel(count, forced, mix_ref, source_hbm, middle_ref, slope_ref, up_ref, down_ref, *rest):
+    next_ref, (one, two, source_ref, sems) = rest[0], rest[-4:]
+    if forced:
+        fetch = pltpu.make_async_copy(source_hbm.at[1], next_ref, sems.at[0])
+        fetch.start()
     source_in = Streamed(source_hbm, source_ref, sems, range(HALF, count) if forced else [])
     mix = scalars(mix_ref)
     buffers = (one, two)
@@ -196,6 +203,8 @@
         here = middle_ref if m == HALF - 1 else buffers[m % 2]
         source = source_ref if forced else None
         alone_step(mix, m, here, buffers[(m + 1) % 2], slope_ref, source, [None, (up_ref, down_ref)])
+    if forced:
+        fetch.wait()
 
 
 def corrected_kernel(mix_ref, leads_ref, relaxed_hbm, source_hbm, share_ref, slope_ref, corrected_ref, middle_ref, up_ref, down_ref, relaxed_ref, source_ref, one, two, sems):
@@ -303,12 +312,16 @@
         later.wait()
 
 
-class Later:
-    def __init__(self, ref):
-        self.ref = ref
+class Parts:
+    def __init__(self, parts):
+        self.parts = parts
 
     def __getitem__(self, index):
-        return self.ref[(index[0] - HALF - 1,) + index[1:]]
+        return self.parts[index[0]][index[1:]]
+
+
+def later_parts(ref):
+    return {t: ref.at[t - HALF - 1] for t in range(HALF + 1, STEPS)}
 
 
 def end_kernel(mix_ref, later_ref, middle_ref, middle_added, low_ref, high_ref, slope_ref, packed_low, packed_high, out_ref, one, two, added_one, added_two):
@@ -318,7 +331,7 @@
 
     march_steps(
         STEPS, range(HALF, STEPS), True, done, nothing, nothing, scalars(mix_ref),
-        middle_ref, middle_added, (None, low_ref), (None, high_ref), slope_ref, Later(later_ref), packed_low, packed_high,
+        middle_ref, middle_added, (None, low_ref), (None, high_ref), slope_ref, Parts(later_parts(later_ref)), packed_low, packed_high,
         one, two, added_one, added_two,
     )
 
@@ -338,37 +351,43 @@
     )
     out = pltpu.make_async_copy(out_ref, out_hbm, sems.at[1])
     out.start()
+    for share, x, row in shares(4):
+        for f in range(FIELDS):
+            share_ref[share, f] = out_ref[f, x, row : row + 4]
     source_in.ready(0)
-    leads = leads_ref[0] == 1
-    for x in range(WIDE):
-        error = [source_ref[0, f, x] for f in range(FIELDS)]
-        slope = [slope_ref[0, f, x] for f in range(FIELDS)]
-        moved = coarse_turn(mix, error, slope)
-        for f in range(FIELDS):
-            value = out_ref[f, x]
-            value = jnp.where(leads, moved[f] + value, value)
-            for q in range(4):
-                share_ref[4 * x + q, f] = value[4 * q : 4 * q + 4]
+
+    @pl.when(leads_ref[0] == 1)
+    def _():
+        for x in range(WIDE):
+            error = [source_ref[0, f, x] for f in range(FIELDS)]
+            slope = [slope_ref[0, f, x] for f in range(FIELDS)]
+            for f, moved in enumerate(coarse_turn(mix, error, slope)):
+                value = moved + out_ref[f, x]
+                for q in range(4):
+                    share_ref[4 * x + q, f] = value[4 * q : 4 * q + 4]
+
     out.wait()
 
 
-def states_first_kernel(mix_ref, source_hbm, start_ref, low_ref, high_ref, slope_ref, packed_low, packed_high, out_hbm, middle_ref, middle_added, later_ref, one, two, added_one, added_two, source_ref, out_ref, sems, out_sems):
-    source_in = Streamed(source_hbm, source_ref, sems, range(1, HALF + 1))
+def states_first_kernel(mix_ref, source_hbm, next_ref, start_ref, low_ref, high_ref, slope_ref, packed_low, packed_high, out_hbm, middle_ref, middle_added, later_ref, one, two, added_one, added_two, source_ref, out_ref, sems, out_sems):
+    source_in = Streamed(source_hbm, source_ref, sems, range(2, HALF + 1))
+    parts = {1: next_ref} | {t: source_ref.at[t] for t in range(2, HALF + 1)}
     later = pltpu.make_async_copy(source_hbm.at[HALF + 1 :], later_ref, sems.at[HALF + 1])
     later.start()
     outs = [
         pltpu.make_async_copy(start_ref if t == 0 else out_ref.at[t], out_hbm.at[t], out_sems.at[t])
-        for t in range(HALF + 1)
+        for t in range(HALF)
     ]
     outs[0].start()
 
     def done(step, f, x, value):
-        out_ref[step, f, x] = value
+        if step < HALF:
+            out_ref[step, f, x] = value
 
     march_steps(
-        STEPS - 1, range(HALF), True, done, lambda m: source_in.ready(m + 1), lambda m: outs[m + 1].start(),
+        STEPS - 1, range(HALF), True, done, lambda m: source_in.ready(m + 1), lambda m: outs[m + 1].start() if m + 1 < HALF else None,
         scalars(mix_ref),
-        start_ref, None, (low_ref, None), (high_ref, None), slope_ref, source_ref, packed_low, packed_high,
+        start_ref, None, (low_ref, None), (high_ref, None), slope_ref, Parts(parts), packed_low, packed_high,
         one, two, added_one, added_two, (middle_ref, middle_added),
     )
     later.wait()
@@ -378,16 +397,17 @@
 
 def states_rest_kernel(mix_ref, earlier_hbm, later_ref, middle_ref, middle_added, low_ref, high_ref, slope_ref, packed_low, packed_high, out_hbm, one, two, added_one, added_two, out_ref, out_sems):
     outs = {
-        t: pltpu.make_async_copy(out_ref.at[t], out_hbm.at[t], out_sems.at[t])
-        for t in range(HALF + 1, STEPS)
+        t: pltpu.make_async_copy(middle_ref if t == HALF else out_ref.at[t], out_hbm.at[t], out_sems.at[t])
+        for t in range(HALF, STEPS)
     }
+    outs[HALF].start()
 
     def done(step, f, x, value):
         out_ref[step, f, x] = value
 
     march_steps(
         STEPS - 1, range(HALF, STEPS - 1), True, done, nothing, lambda m: outs[m + 1].start(), scalars(mix_ref),
-        middle_ref, middle_added, (None, low_ref), (None, high_ref), slope_ref, Later(later_ref),
+        middle_ref, middle_added, (None, low_ref), (None, high_ref), slope_ref, Parts(later_parts(later_ref)),
         packed_low, packed_high, one, two, added_one, added_two,
     )
     for out in outs.values():
@@ -416,7 +436,7 @@
             error_ref[i + 1, f] = new[f]
         return new
 
-    lax.fori_loop(1, blocks - 1, turn, error)
+    lax.fori_loop(1, blocks - 1, turn, error, unroll=3 if (blocks - 2) % 3 == 0 else 1)
 
 
 VMEM = pl.BlockSpec(memory_space=pltpu.VMEM)
@@ -480,7 +500,7 @@
     up, down = call(
         border_kernel,
         (packed, packed),
-        (mixing, in_hbm(primal)),
+        (in_hbm(mixing), in_hbm(primal)),
         [SMEM, HBM],
         2 * PACKED,
         scratch=[packed_room, packed_room, pltpu.SemaphoreType.DMA((2 * STEPS,))],
@@ -503,13 +523,14 @@
             scratch=march_room + stream,
         )
 
-    slope, slope_share, up, down, up_rest, down_rest = call(
+    slope_share, slope, up, down, up_rest, down_rest = call(
         guess_kernel,
-        (whole, share, half, half, half, half),
+        (share, whole, half, half, half, half),
         (mixing, primal, source, guess),
         [SMEM, HBM, HBM],
         100,
-        scratch=[stream[0], stream[0], room, room, pltpu.SemaphoreType.DMA((2, STEPS))],
+        scratch=[stream[0], stream[0], room, room, pltpu.VMEM(share.shape, jnp.float32), pltpu.SemaphoreType.DMA((2, STEPS))],
+        first_out=HBM,
     )
     low, high = exchange(up, down)
     low_rest, high_rest = exchange(up_rest, down_rest)
@@ -560,15 +581,15 @@
     corrected, middle, up, down = call(
         corrected_kernel,
         (slab, slab, half, half),
-        (mixing, leads, relaxed, source, error_share, slope),
+        (mixing, leads, in_hbm(relaxed), source, error_share, slope),
         [SMEM, SMEM, HBM, HBM],
         30,
         scratch=[room, stream[0], room, room, pltpu.SemaphoreType.DMA((STEPS + 1,))],
     )
     low, high = exchange(up, down)
-    up_rest, down_rest = call(
+    up_rest, down_rest, upcoming = call(
         functools.partial(rest_kernel, STEPS - 1, True),
-        (rest, rest),
+        (rest, rest, slab),
         (mixing, source, middle, slope),
         [SMEM, HBM],
         16,
@@ -580,7 +601,7 @@
     earlier, middle, middle_added, later = call(
         states_first_kernel,
         (whole, slab, added, later),
-        (mixing, source, corrected, low, high, slope, packed_low, packed_high),
+        (mixing, source, upcoming, corrected, low, high, slope, packed_low, packed_high),
         [SMEM, HBM],
         42,
         scratch=states_room,

time: 162 us -> 161 us (level)
  local copies, waits for them, and re-layouts: 3.95 us -> 2.3 us
    unnamed x14 -> x10, local copies, waits for them, and re-layouts: 3.95 us -> 2.3 us
where the time goes in v3:
time: 161 us; the launch traced here: 160 us
  starting transfers between devices  53.2 us (33%)
  Pallas kernels  43.5 us (27%)
  waiting for transfers between devices  32.6 us (20%)
  blocking collectives  25.4 us (16%)
  local copies, waits for them, and re-layouts  2.3 us (1%)
  other arithmetic  1.84 us (1%)
    pallas_call x13, Pallas kernels, call(): pl.pallas_call(kernel, input_output_aliases=alias or {}, out_shape=out, i...  43.5 us
    all_to_all x1, blocking collectives, per_device(): change_shares = lax.all_to_all(change_share, 'tm', 0, 0)  25.4 us
    ppermute x7, starting transfers between devices, exchange(): lax.ppermute(down, 'space', backward)  24 us
    ppermute x7, waiting for transfers between devices, exchange(): lax.ppermute(up, 'space', forward)  13.3 us
    all_to_all x1, starting transfers between devices, per_device(): slope_shares = lax.all_to_all(slope_share, 'tm', 0, 0)  13.2 us
    ppermute x2, waiting for transfers between devices, from_behind(): return lax.ppermute(array, 'tm', [(i, i + 1) for i in range(count - 1)])  9.84 us
    all_to_all x1, waiting for transfers between devices, per_device(): error_share = lax.all_to_all(error_shares, 'tm', 0, 0)  9.42 us
    ppermute x2, starting transfers between devices, from_behind(): return lax.ppermute(array, 'tm', [(i, i + 1) for i in range(count - 1)])  8.87 us
  transfers between devices with their start and end apart: 18, of which 3 were waited for; matrix products, arithmetic and copies ran while one was open for 1% of the time, Pallas kernels for 22%

profile of v3, /device:TPU:1, one launch (start us, length us, event | category | flops | bytes accessed | tf_op | source)
XLA Modules:
  0.0 160.0 jit_solution(3499538640289253496)
XLA Ops:
  0.6 3.8 %shard_map.60 = (f32[5,12,16,128]{3,2,1,0:T(8,128)}, f32[5,12,16,128]{3,2,1,0:T(8,128)}) custom-call(f32[5,5]{1,0:T(8,128)} %mix_ref.25, f32[8,5,8,16,128]{4,3,2,1,0:T(8,128)} %primal_hbm.3), custom_call_target="tpu_custom_call" | custom-call | flops 6144000 | bytes 3604580 | tf_op jit(solution)/shard_map/pallas_call | solution.py:452
  4.4 2.5 %collective-permute-start.2 = (f32[5,12,16,128]{3,2,1,0:T(8,128)}, f32[5,12,16,128]{3,2,1,0:T(8,128)S(1)}, u32[]{:S(2)}, u32[]{:S(2)}) collective-permute-start(f32[5,12,16,128]{3,2,1,0:T(8,128)} %get-tuple-element.38), channel_id=1, source_target_pairs={{0,1},{1,2},{2,3},{3,4},{4,5},{5,6},{6,7},{7,0},{8,9},{9,10},{10,1... | collective-permute-start | bytes 1474568 | tf_op jit(solution)/shard_map/ppermute | solution.py:483
  6.9 2.5 %collective-permute-start.3 = (f32[5,12,16,128]{3,2,1,0:T(8,128)}, f32[5,12,16,128]{3,2,1,0:T(8,128)}, u32[]{:S(2)}, u32[]{:S(2)}) collective-permute-start(f32[5,12,16,128]{3,2,1,0:T(8,128)} %get-tuple-element.39), channel_id=1, source_target_pairs={{1,0},{2,1},{3,2},{4,3},{5,4},{6,5},{7,6},{0,7},{9,8},{10,9},{11,1... | collective-permute-start | bytes 1474568 | tf_op jit(solution)/shard_map/ppermute | solution.py:483
  9.5 6.3 %shard_map.59 = (f32[32,5,4,128]{3,2,1,0:T(4,128)}, f32[8,5,8,16,128]{4,3,2,1,0:T(8,128)S(1)}, f32[5,4,16,128]{3,2,1,0:T(8,128)S(1)}, f32[5,4,16,128]{3,2,1,0:T(...) custom-call(f32[5,5]{1,0:T(8,128)S(1)} %copy-done.1, f32[8,5,8,16,128]{4,3,2,1,0:T(8,128)} %primal_hbm.3, ...), custom_call_target="tpu_custom_call" | custom-call | flops 25600000 | bytes 9175140 | tf_op jit(solution)/shard_map/pallas_call | solution.py:452
  15.9 3.6 %collective-permute-start.1 = (f32[5,4,16,128]{3,2,1,0:T(8,128)}, f32[5,4,16,128]{3,2,1,0:T(8,128)}, u32[]{:S(2)}, u32[]{:S(2)}) collective-permute-start(f32[5,4,16,128]{3,2,1,0:T(8,128)} %get-tuple-element.36), channel_id=1, source_target_pairs={{1,0},{2,1},{3,2},{4,3},{5,4},{6,5},{7,6},{0,7},{9,8},{10,9},{11,1... | collective-permute-start | bytes 491528 | tf_op jit(solution)/shard_map/ppermute | solution.py:483
  19.5 13.3 %collective-permute-done.low_ref = f32[5,4,16,128]{3,2,1,0:T(8,128)S(1)} collective-permute-done((f32[5,4,16,128]{3,2,1,0:T(8,128)S(1)}, f32[5,4,16,128]{3,2,1,0:T(8,128)S(1)}, u32[]{:S(2)}, u32[]{:S(2)}) %collective-permute-start) | collective-permute-done | bytes 163872 | tf_op jit(solution)/shard_map/ppermute | solution.py:483
  33.5 2.9 %collective-permute-start.5 = (f32[5,4,16,128]{3,2,1,0:T(8,128)}, f32[5,4,16,128]{3,2,1,0:T(8,128)}, u32[]{:S(2)}, u32[]{:S(2)}) collective-permute-start(f32[5,4,16,128]{3,2,1,0:T(8,128)} %get-tuple-element.44), channel_id=1, source_target_pairs={{1,0},{2,1},{3,2},{4,3},{5,4},{6,5},{7,6},{0,7},{9,8},{10,9},{11,1... | collective-permute-start | bytes 491528 | tf_op jit(solution)/shard_map/ppermute | solution.py:483
  36.4 13.2 %all-to-all-start = ((f32[32,5,4,128]{3,2,1,0:T(4,128)}), f32[32,5,4,128]{3,2,1,0:T(4,128)}, u32[]{:S(2)}, u32[]{:S(2)}) async-start(f32[32,5,4,128]{3,2,1,0:T(4,128)} %get-tuple-element.46), calls=%async_computation | async-start | bytes 655360 | tf_op jit(solution)/shard_map/all_to_all | solution.py:547
  49.6 0.9 copy-done.4
  50.5 4.1 %shard_map.61 = (f32[5,8,16,128]{3,2,1,0:T(8,128)S(1)}, f32[2,5,4,16,128]{4,3,2,1,0:T(8,128)S(1)}, f32[3,5,8,16,128]{4,3,2,1,0:T(8,128)S(1)}) custom-call(f32[5,5]{1,0:T(8,128)S(1)} %copy-done.1, f32[8,5,8,16,128]{4,3,2,1,0:T(8,128)} %source_hbm.17, f32[5,8,16,128]{3,2,1,0:T(8,128)S(1)} %bitcast.8, f32[5,4,16,128]{3,2,1,0:T(8,128)S(1)} %copy-done.4, ...), custom_call_target="tpu_custom_call" | custom-call | flops 10752000 | bytes 8519780 | tf_op jit(solution)/shard_map/pallas_call | solution.py:452
  54.7 3.9 %shard_map.62 = f32[5,8,16,128]{3,2,1,0:T(8,128)} custom-call(f32[5,5]{1,0:T(8,128)S(1)} %copy-done.1, f32[3,5,8,16,128]{4,3,2,1,0:T(8,128)S(1)} %get-tuple-element.40.later_ref, f32[5,8,16,128]{3,2,1,0:T(8,128)S(1)} %get-tuple-element.41.middle_ref, f32[2,5,4,16,128]{4,3,2,1,0:T(8,128)S(1)} %get-tuple-element.42.middle_added, ...), custom_call_target="tpu_custom_call" | custom-call | flops 11776000 | bytes 5898340 | tf_op jit(solution)/shard_map/pallas_call | solution.py:452
  58.6 4.4 %collective-permute-start.6 = (f32[5,8,16,128]{3,2,1,0:T(8,128)}, f32[5,8,16,128]{3,2,1,0:T(8,128)}, u32[]{:S(2)}, u32[]{:S(2)}) collective-permute-start(f32[5,8,16,128]{3,2,1,0:T(8,128)} %shard_map.62), channel_id=1, source_target_pairs={{0,8},{8,16},{16,24},{24,32},{32,40},{40,48},{48,56},{56,64},{64,7... | collective-permute-start | bytes 983048 | tf_op jit(solution)/shard_map/ppermute | solution.py:476
  63.0 9.8 %collective-permute-done.6.ended_ref = f32[5,8,16,128]{3,2,1,0:T(8,128)} collective-permute-done((f32[5,8,16,128]{3,2,1,0:T(8,128)}, f32[5,8,16,128]{3,2,1,0:T(8,128)}, u32[]{:S(2)}, u32[]{:S(2)}) %collective-permute-start.6) | collective-permute-done | bytes 327712 | tf_op jit(solution)/shard_map/ppermute | solution.py:476
  72.9 3.0 %shard_map.63 = (f32[5,8,16,128]{3,2,1,0:T(8,128)}, f32[5,8,16,128]{3,2,1,0:T(8,128)S(1)}, f32[5,8,16,128]{3,2,1,0:T(8,128)S(1)}, f32[5,4,16,128]{3,2,1,0:T(8,128)S(1)}, f32[5,4,16,128]{3,2,1,0:T(8,128)S(1)}) custom-call(f32[5,5]{1,0:T(8,128)S(1)} %copy-done.1, s32[1]{0:T(128)} %bitcast.leads_ref, f32[8,5,8,16,128]{4,3,2,1,0:T(8,128)} %source_hbm.17, ...), custom_call_target="tpu_custom_call" | custom-call | flops 7680000 | bytes 7209064 | tf_op jit(solution)/shard_map/pallas_call | solution.py:452
  75.9 3.6 %collective-permute-start.8 = (f32[5,4,16,128]{3,2,1,0:T(8,128)S(1)}, f32[5,4,16,128]{3,2,1,0:T(8,128)S(1)}, u32[]{:S(2)}, u32[]{:S(2)}) collective-permute-start(f32[5,4,16,128]{3,2,1,0:T(8,128)S(1)} %get-tuple-element.49), channel_id=1, source_target_pairs={{1,0},{2,1},{3,2},{4,3},{5,4},{6,5},{7,6},{0,7},{9,8},{10,9},{11,1... | collective-permute-start | bytes 491528 | tf_op jit(solution)/shard_map/ppermute | solution.py:483
  79.5 1.3 shard_map.65
  80.9 3.6 %collective-permute-start.10 = (f32[5,4,16,128]{3,2,1,0:T(8,128)S(1)}, f32[5,4,16,128]{3,2,1,0:T(8,128)S(1)}, u32[]{:S(2)}, u32[]{:S(2)}) collective-permute-start(f32[5,4,16,128]{3,2,1,0:T(8,128)S(1)} %get-tuple-element.54), channel_id=1, source_target_pairs={{1,0},{2,1},{3,2},{4,3},{5,4},{6,5},{7,6},{0,7},{9,8},{10,9},{11,1... | collective-permute-start | bytes 491528 | tf_op jit(solution)/shard_map/ppermute | solution.py:483
  84.5 3.0 %shard_map.64 = (f32[5,8,16,128]{3,2,1,0:T(8,128)S(1)}, f32[2,5,4,16,128]{4,3,2,1,0:T(8,128)S(1)}) custom-call(f32[5,5]{1,0:T(8,128)S(1)} %copy-done.1, f32[8,5,8,16,128]{4,3,2,1,0:T(8,128)} %source_hbm.17, f32[5,8,16,128]{3,2,1,0:T(8,128)S(1)} %get-tuple-element.47.start_ref, f32[5,4,16,128]{3,2,1,0:T(8,128)S(1)} %collective-permute-done.7.low_ref, ...), custom_call_target="tpu_custom_call" | custom-call | flops 10752000 | bytes 7536740 | tf_op jit(solution)/shard_map/pallas_call | solution.py:452
  87.6 3.8 %shard_map.66 = (f32[5,8,16,128]{3,2,1,0:T(8,128)}, f32[32,5,4,128]{3,2,1,0:T(4,128)S(1)}) custom-call(f32[5,5]{1,0:T(8,128)S(1)} %copy-done.1, s32[1]{0:T(128)} %bitcast.leads_ref, f32[8,5,8,16,128]{4,3,2,1,0:T(8,128)} %source_hbm.17, f32[5,8,16,128]{3,2,1,0:T(8,128)S(1)} %get-tuple-element.50.middle_ref, ...), custom_call_target="tpu_custom_call" | custom-call | flops 12800000 | bytes 7864424 | tf_op jit(solution)/shard_map/pallas_call | solution.py:452
  91.4 0.7 copy-done.2
  92.1 25.4 %all_to_all.15.resid_ref = f32[32,5,4,128]{3,2,1,0:T(4,128)S(1)} all-to-all(f32[32,5,4,128]{3,2,1,0:T(4,128)} %copy-done.2), channel_id=1, replica_groups=mesh['tm'=32,'space'=8] {'tm'}, dimensions={0} | all-to-all | bytes 655360 | tf_op jit(solution)/shard_map/all_to_all | solution.py:577
  117.5 2.1 %shard_map.67 = f32[32,5,4,128]{3,2,1,0:T(4,128)} custom-call(f32[5,5]{1,0:T(8,128)S(1)} %copy-done.1, f32[32,5,4,128]{3,2,1,0:T(4,128)} %all-to-all-done.slope_ref, f32[32,5,4,128]{3,2,1,0:T(4,128)S(1)} %all_to_all.15.resid_ref), custom_call_target="tpu_custom_call" | custom-call | flops 4096000 | bytes 983140 | tf_op jit(solution)/shard_map/pallas_call | solution.py:452
  119.6 4.2 %all-to-all-start.2 = ((f32[32,5,4,128]{3,2,1,0:T(4,128)}), f32[32,5,4,128]{3,2,1,0:T(4,128)S(1)}, u32[]{:S(2)}, u32[]{:S(2)}) async-start(f32[32,5,4,128]{3,2,1,0:T(4,128)} %shard_map.67), calls=%async_computation.2 | async-start | bytes 655360 | tf_op jit(solution)/shard_map/all_to_all | solution.py:580
  123.7 4.4 %collective-permute-start.15 = (f32[5,8,16,128]{3,2,1,0:T(8,128)}, f32[5,8,16,128]{3,2,1,0:T(8,128)}, u32[]{:S(2)}, u32[]{:S(2)}) collective-permute-start(f32[5,8,16,128]{3,2,1,0:T(8,128)} %get-tuple-element.67), channel_id=1, source_target_pairs={{0,8},{8,16},{16,24},{24,32},{32,40},{40,48},{48,56},{56,64},{64,7... | collective-permute-start | bytes 983048 | tf_op jit(solution)/shard_map/ppermute | solution.py:476
  128.2 9.4 %all-to-all-done.2.share_ref = f32[32,5,4,128]{3,2,1,0:T(4,128)S(1)} async-done(((f32[32,5,4,128]{3,2,1,0:T(4,128)}), f32[32,5,4,128]{3,2,1,0:T(4,128)S(1)}, u32[]{:S(2)}, u32[]{:S(2)}) %all-to-all-start.2) | async-done | bytes 327712 | tf_op jit(solution)/shard_map/all_to_all | solution.py:580
  137.6 2.7 %shard_map.68 = (f32[5,8,16,128]{3,2,1,0:T(8,128)S(1)}, f32[5,8,16,128]{3,2,1,0:T(8,128)S(1)}, f32[5,4,16,128]{3,2,1,0:T(8,128)S(1)}, f32[5,4,16,128]{3,2,1,0:T(8,128)S(1)}) custom-call(f32[5,5]{1,0:T(8,128)S(1)} %copy-done.1, s32[1]{0:T(128)} %bitcast.leads_ref, f32[5,8,16,128]{3,2,1,0:T(8,128)} %get-tuple-element.45.relaxed_hbm, ...), custom_call_target="tpu_custom_call" | custom-call | flops 7680000 | bytes 6881384 | tf_op jit(solution)/shard_map/pallas_call | solution.py:452
  140.4 4.3 %collective-permute-start.12 = (f32[5,4,16,128]{3,2,1,0:T(8,128)S(1)}, f32[5,4,16,128]{3,2,1,0:T(8,128)S(1)}, u32[]{:S(2)}, u32[]{:S(2)}) collective-permute-start(f32[5,4,16,128]{3,2,1,0:T(8,128)S(1)} %get-tuple-element.60), channel_id=1, source_target_pairs={{1,0},{2,1},{3,2},{4,3},{5,4},{6,5},{7,6},{0,7},{9,8},{10,9},{11,1... | collective-permute-start | bytes 491528 | tf_op jit(solution)/shard_map/ppermute | solution.py:483
  144.8 2.2 %shard_map.69 = (f32[5,3,16,128]{3,2,1,0:T(8,128)S(1)}, f32[5,3,16,128]{3,2,1,0:T(8,128)S(1)}, f32[5,8,16,128]{3,2,1,0:T(8,128)S(1)}) custom-call(f32[5,5]{1,0:T(8,128)S(1)} %copy-done.1, f32[8,5,8,16,128]{4,3,2,1,0:T(8,128)} %source_hbm.17, f32[5,8,16,128]{3,2,1,0:T(8,128)S(1)} %get-tuple-element.56.middle_ref, ...), custom_call_target="tpu_custom_call" | custom-call | flops 4096000 | bytes 6144100 | tf_op jit(solution)/shard_map/pallas_call | solution.py:452
  147.1 3.6 %collective-permute-start.14 = (f32[5,3,16,128]{3,2,1,0:T(8,128)S(1)}, f32[5,3,16,128]{3,2,1,0:T(8,128)S(1)}, u32[]{:S(2)}, u32[]{:S(2)}) collective-permute-start(f32[5,3,16,128]{3,2,1,0:T(8,128)S(1)} %get-tuple-element.66), channel_id=1, source_target_pairs={{1,0},{2,1},{3,2},{4,3},{5,4},{6,5},{7,6},{0,7},{9,8},{10,9},{11,1... | collective-permute-start | bytes 368648 | tf_op jit(solution)/shard_map/ppermute | solution.py:483
  150.7 1.8 %fusion = f32[1,5,8,16,128]{4,3,2,1,0:T(8,128)} fusion(f32[5,8,16,128]{3,2,1,0:T(8,128)} %collective-permute-done.15, f32[8,5,8,16,128]{4,3,2,1,0:T(8,128)} %source_hbm.17, pred[]{:T(512)S(6)} %eq.3), kind=kLoop, calls=%fused_computation.1 | loop fusion | flops 81920 | bytes 983041 | tf_op jit(solution)/shard_map/broadcast_in_dim | solution.py:620
  152.5 4.0 %shard_map.70 = (f32[8,5,8,16,128]{4,3,2,1,0:T(8,128)}, f32[5,8,16,128]{3,2,1,0:T(8,128)S(1)}, f32[2,5,4,16,128]{4,3,2,1,0:T(8,128)S(1)}, f32[3,5,8,16,128]{4,3,2,1,0:T(8,128)S(1)}) custom-call(f32[5,5]{1,0:T(8,128)S(1)} %copy-done.1, f32[8,5,8,16,128]{4,3,2,1,0:T(8,128)} %source_hbm.17, f32[5,8,16,128]{3,2,1,0:T(8,128)S(1)} %get-tuple-element.57.next_ref, ...), custom_call_target="tpu_custom_call" | custom-call | flops 10752000 | bytes 11468900 | tf_op jit(solution)/shard_map/pallas_call | solution.py:452
  156.6 3.2 %shard_map.71 = f32[8,5,8,16,128]{4,3,2,1,0:T(8,128)} custom-call(f32[5,5]{1,0:T(8,128)S(1)} %copy-done.1, f32[8,5,8,16,128]{4,3,2,1,0:T(8,128)} %get-tuple-element.61.earlier_hbm, f32[3,5,8,16,128]{4,3,2,1,0:T(8,128)S(1)} %get-tuple-element.62.later_ref, f32[5,8,16,128]{3,2,1,0:T(8,128)S(1)} %get-tuple-element.63.middle_ref, ...), custom_call_target="tpu_custom_call", output_to_operand_aliasing={{}: (1, {})} | custom-call | flops 8704000 | bytes 10731620 | tf_op jit(solution)/shard_map/pallas_call | solution.py:452
  (29 shorter events, 1.1 us)
Async XLA Ops:
  0.6 8.9 %copy-start.1 = (f32[5,5]{1,0:T(8,128)S(1)}, f32[5,5]{1,0:T(8,128)}, u32[]{:S(2)}) copy-start(f32[5,5]{1,0:T(8,128)} %mix_ref.25) | copy-start | bytes 304
  0.6 8.8 %copy-start = (f32[1,5,8,16,128]{4,3,2,1,0:T(8,128)S(1)}, f32[1,5,8,16,128]{4,3,2,1,0:T(8,128)}, u32[]{:S(2)}) copy-start(f32[1,5,8,16,128]{4,3,2,1,0:T(8,128)} %guess_ref.3) | copy-start | bytes 983044
  4.4 45.2 %collective-permute-start.2 = (f32[5,12,16,128]{3,2,1,0:T(8,128)}, f32[5,12,16,128]{3,2,1,0:T(8,128)S(1)}, u32[]{:S(2)}, u32[]{:S(2)}) collective-permute-start(f32[5,12,16,128]{3,2,1,0:T(8,128)} %get-tuple-element.38), channel_id=1, source_target_pairs={{0,1},{1,2},{2,3},{3,4},{4,5},{5,6},{6,7},{7,0},{8,9},{9,10},{10,1... | collective-permute-start | bytes 1474568 | tf_op jit(solution)/shard_map/ppermute | solution.py:483
  6.9 42.7 %collective-permute-start.3 = (f32[5,12,16,128]{3,2,1,0:T(8,128)}, f32[5,12,16,128]{3,2,1,0:T(8,128)}, u32[]{:S(2)}, u32[]{:S(2)}) collective-permute-start(f32[5,12,16,128]{3,2,1,0:T(8,128)} %get-tuple-element.39), channel_id=1, source_target_pairs={{1,0},{2,1},{3,2},{4,3},{5,4},{6,5},{7,6},{0,7},{9,8},{10,9},{11,1... | collective-permute-start | bytes 1474568 | tf_op jit(solution)/shard_map/ppermute | solution.py:483
  15.8 17.0 %collective-permute-start = (f32[5,4,16,128]{3,2,1,0:T(8,128)S(1)}, f32[5,4,16,128]{3,2,1,0:T(8,128)S(1)}, u32[]{:S(2)}, u32[]{:S(2)}) collective-permute-start(f32[5,4,16,128]{3,2,1,0:T(8,128)S(1)} %get-tuple-element.35), channel_id=1, source_target_pairs={{0,1},{1,2},{2,3},{3,4},{4,5},{5,6},{6,7},{7,0},{8,9},{9,10},{10,1... | collective-permute-start | bytes 491528 | tf_op jit(solution)/shard_map/ppermute | solution.py:483
  15.9 33.7 %collective-permute-start.1 = (f32[5,4,16,128]{3,2,1,0:T(8,128)}, f32[5,4,16,128]{3,2,1,0:T(8,128)}, u32[]{:S(2)}, u32[]{:S(2)}) collective-permute-start(f32[5,4,16,128]{3,2,1,0:T(8,128)} %get-tuple-element.36), channel_id=1, source_target_pairs={{1,0},{2,1},{3,2},{4,3},{5,4},{6,5},{7,6},{0,7},{9,8},{10,9},{11,1... | collective-permute-start | bytes 491528 | tf_op jit(solution)/shard_map/ppermute | solution.py:483
  19.5 35.2 %collective-permute-start.4 = (f32[5,4,16,128]{3,2,1,0:T(8,128)}, f32[5,4,16,128]{3,2,1,0:T(8,128)}, u32[]{:S(2)}, u32[]{:S(2)}) collective-permute-start(f32[5,4,16,128]{3,2,1,0:T(8,128)} %get-tuple-element.43), channel_id=1, source_target_pairs={{0,1},{1,2},{2,3},{3,4},{4,5},{5,6},{6,7},{7,0},{8,9},{9,10},{10,1... | collective-permute-start | bytes 491528 | tf_op jit(solution)/shard_map/ppermute | solution.py:483
  32.8 0.7 copy-start.3
  33.5 21.2 %collective-permute-start.5 = (f32[5,4,16,128]{3,2,1,0:T(8,128)}, f32[5,4,16,128]{3,2,1,0:T(8,128)}, u32[]{:S(2)}, u32[]{:S(2)}) collective-permute-start(f32[5,4,16,128]{3,2,1,0:T(8,128)} %get-tuple-element.44), channel_id=1, source_target_pairs={{1,0},{2,1},{3,2},{4,3},{5,4},{6,5},{7,6},{0,7},{9,8},{10,9},{11,1... | collective-permute-start | bytes 491528 | tf_op jit(solution)/shard_map/ppermute | solution.py:483
  36.4 55.7 %all-to-all-start = ((f32[32,5,4,128]{3,2,1,0:T(4,128)}), f32[32,5,4,128]{3,2,1,0:T(4,128)}, u32[]{:S(2)}, u32[]{:S(2)}) async-start(f32[32,5,4,128]{3,2,1,0:T(4,128)} %get-tuple-element.46), calls=%async_computation | async-start | bytes 655360 | tf_op jit(solution)/shard_map/all_to_all | solution.py:547
  49.6 0.9 copy-start.4
  58.6 14.3 %collective-permute-start.6 = (f32[5,8,16,128]{3,2,1,0:T(8,128)}, f32[5,8,16,128]{3,2,1,0:T(8,128)}, u32[]{:S(2)}, u32[]{:S(2)}) collective-permute-start(f32[5,8,16,128]{3,2,1,0:T(8,128)} %shard_map.62), channel_id=1, source_target_pairs={{0,8},{8,16},{16,24},{24,32},{32,40},{40,48},{48,56},{56,64},{64,7... | collective-permute-start | bytes 983048 | tf_op jit(solution)/shard_map/ppermute | solution.py:476
  75.9 8.6 %collective-permute-start.7 = (f32[5,4,16,128]{3,2,1,0:T(8,128)S(1)}, f32[5,4,16,128]{3,2,1,0:T(8,128)S(1)}, u32[]{:S(2)}, u32[]{:S(2)}) collective-permute-start(f32[5,4,16,128]{3,2,1,0:T(8,128)S(1)} %get-tuple-element.48), channel_id=1, source_target_pairs={{0,1},{1,2},{2,3},{3,4},{4,5},{5,6},{6,7},{7,0},{8,9},{9,10},{10,1... | collective-permute-start | bytes 491528 | tf_op jit(solution)/shard_map/ppermute | solution.py:483
  75.9 8.6 %collective-permute-start.8 = (f32[5,4,16,128]{3,2,1,0:T(8,128)S(1)}, f32[5,4,16,128]{3,2,1,0:T(8,128)S(1)}, u32[]{:S(2)}, u32[]{:S(2)}) collective-permute-start(f32[5,4,16,128]{3,2,1,0:T(8,128)S(1)} %get-tuple-element.49), channel_id=1, source_target_pairs={{1,0},{2,1},{3,2},{4,3},{5,4},{6,5},{7,6},{0,7},{9,8},{10,9},{11,1... | collective-permute-start | bytes 491528 | tf_op jit(solution)/shard_map/ppermute | solution.py:483
  80.8 6.7 %collective-permute-start.9 = (f32[5,4,16,128]{3,2,1,0:T(8,128)S(1)}, f32[5,4,16,128]{3,2,1,0:T(8,128)S(1)}, u32[]{:S(2)}, u32[]{:S(2)}) collective-permute-start(f32[5,4,16,128]{3,2,1,0:T(8,128)S(1)} %get-tuple-element.53), channel_id=1, source_target_pairs={{0,1},{1,2},{2,3},{3,4},{4,5},{5,6},{6,7},{7,0},{8,9},{9,10},{10,1... | collective-permute-start | bytes 491528 | tf_op jit(solution)/shard_map/ppermute | solution.py:483
  80.9 6.6 %collective-permute-start.10 = (f32[5,4,16,128]{3,2,1,0:T(8,128)S(1)}, f32[5,4,16,128]{3,2,1,0:T(8,128)S(1)}, u32[]{:S(2)}, u32[]{:S(2)}) collective-permute-start(f32[5,4,16,128]{3,2,1,0:T(8,128)S(1)} %get-tuple-element.54), channel_id=1, source_target_pairs={{1,0},{2,1},{3,2},{4,3},{5,4},{6,5},{7,6},{0,7},{9,8},{10,9},{11,1... | collective-permute-start | bytes 491528 | tf_op jit(solution)/shard_map/ppermute | solution.py:483
  91.3 0.7 copy-start.2
  119.6 18.1 %all-to-all-start.2 = ((f32[32,5,4,128]{3,2,1,0:T(4,128)}), f32[32,5,4,128]{3,2,1,0:T(4,128)S(1)}, u32[]{:S(2)}, u32[]{:S(2)}) async-start(f32[32,5,4,128]{3,2,1,0:T(4,128)} %shard_map.67), calls=%async_computation.2 | async-start | bytes 655360 | tf_op jit(solution)/shard_map/all_to_all | solution.py:580
  123.7 26.9 %collective-permute-start.15 = (f32[5,8,16,128]{3,2,1,0:T(8,128)}, f32[5,8,16,128]{3,2,1,0:T(8,128)}, u32[]{:S(2)}, u32[]{:S(2)}) collective-permute-start(f32[5,8,16,128]{3,2,1,0:T(8,128)} %get-tuple-element.67), channel_id=1, source_target_pairs={{0,8},{8,16},{16,24},{24,32},{32,40},{40,48},{48,56},{56,64},{64,7... | collective-permute-start | bytes 983048 | tf_op jit(solution)/shard_map/ppermute | solution.py:476
  140.4 12.2 %collective-permute-start.11 = (f32[5,4,16,128]{3,2,1,0:T(8,128)S(1)}, f32[5,4,16,128]{3,2,1,0:T(8,128)S(1)}, u32[]{:S(2)}, u32[]{:S(2)}) collective-permute-start(f32[5,4,16,128]{3,2,1,0:T(8,128)S(1)} %get-tuple-element.59), channel_id=1, source_target_pairs={{0,1},{1,2},{2,3},{3,4},{4,5},{5,6},{6,7},{7,0},{8,9},{9,10},{10,1... | collective-permute-start | bytes 491528 | tf_op jit(solution)/shard_map/ppermute | solution.py:483
  140.4 12.1 %collective-permute-start.12 = (f32[5,4,16,128]{3,2,1,0:T(8,128)S(1)}, f32[5,4,16,128]{3,2,1,0:T(8,128)S(1)}, u32[]{:S(2)}, u32[]{:S(2)}) collective-permute-start(f32[5,4,16,128]{3,2,1,0:T(8,128)S(1)} %get-tuple-element.60), channel_id=1, source_target_pairs={{1,0},{2,1},{3,2},{4,3},{5,4},{6,5},{7,6},{0,7},{9,8},{10,9},{11,1... | collective-permute-start | bytes 491528 | tf_op jit(solution)/shard_map/ppermute | solution.py:483
  147.0 9.5 %collective-permute-start.13 = (f32[5,3,16,128]{3,2,1,0:T(8,128)S(1)}, f32[5,3,16,128]{3,2,1,0:T(8,128)S(1)}, u32[]{:S(2)}, u32[]{:S(2)}) collective-permute-start(f32[5,3,16,128]{3,2,1,0:T(8,128)S(1)} %get-tuple-element.65), channel_id=1, source_target_pairs={{0,1},{1,2},{2,3},{3,4},{4,5},{5,6},{6,7},{7,0},{8,9},{9,10},{10,1... | collective-permute-start | bytes 368648 | tf_op jit(solution)/shard_map/ppermute | solution.py:483
  147.1 9.4 %collective-permute-start.14 = (f32[5,3,16,128]{3,2,1,0:T(8,128)S(1)}, f32[5,3,16,128]{3,2,1,0:T(8,128)S(1)}, u32[]{:S(2)}, u32[]{:S(2)}) collective-permute-start(f32[5,3,16,128]{3,2,1,0:T(8,128)S(1)} %get-tuple-element.66), channel_id=1, source_target_pairs={{1,0},{2,1},{3,2},{4,3},{5,4},{6,5},{7,6},{0,7},{9,8},{10,9},{11,1... | collective-permute-start | bytes 368648 | tf_op jit(solution)/shard_map/ppermute | solution.py:483

commit v4 on v3

--- a/solution.py
+++ b/solution.py
@@ -18,7 +18,7 @@
 REACH = [min(m, STEPS - 1 - m) for m in range(STEPS)]
 REACH_AT = [sum(REACH[:m]) for m in range(STEPS)]
 PACKED = sum(REACH)
-HALF = STEPS // 2
+HALF = 5
 HALO = max(min(m + 1, STEPS - 1 - m) for m in range(STEPS))
 
 
@@ -509,7 +509,8 @@
     first_source = source[0]
     primal, source = in_hbm(primal), in_hbm(source)
     stream = [pltpu.VMEM(whole.shape, jnp.float32), pltpu.SemaphoreType.DMA((STEPS,))]
-    half, rest = struct(FIELDS, HALF, *plane), struct(FIELDS, HALF - 1, *plane)
+    half, rest = struct(FIELDS, HALF, *plane), struct(FIELDS, STEPS - HALF, *plane)
+    fewer = struct(FIELDS, STEPS - 1 - HALF, *plane)
     added = struct(2, FIELDS, HALO, *plane)
 
     def march_first(start, low, high, forced):
@@ -525,7 +526,7 @@
 
     slope_share, slope, up, down, up_rest, down_rest = call(
         guess_kernel,
-        (share, whole, half, half, half, half),
+        (share, whole, half, half, rest, rest),
         (mixing, primal, source, guess),
         [SMEM, HBM, HBM],
         100,
@@ -557,7 +558,7 @@
     low, high = exchange(up, down)
     up_rest, down_rest = call(
         functools.partial(rest_kernel, STEPS, False),
-        (half, half),
+        (rest, rest),
         (mixing, source, middle, slope),
         [SMEM, HBM],
         20,
@@ -589,7 +590,7 @@
     low, high = exchange(up, down)
     up_rest, down_rest, upcoming = call(
         functools.partial(rest_kernel, STEPS - 1, True),
-        (rest, rest, slab),
+        (fewer, fewer, slab),
         (mixing, source, middle, slope),
         [SMEM, HBM],
         16,

time: 161 us -> 169 us (1.050)
  the two profiles are of different devices: /device:TPU:1 before, /device:TPU:6 now
where the time goes in v4:
time: 169 us; the launch traced here: 167 us
  starting transfers between devices  51.9 us (31%)
  waiting for transfers between devices  45.3 us (27%)
  Pallas kernels  43.6 us (26%)
  blocking collectives  20.6 us (12%)
  local copies, waits for them, and re-layouts  2.33 us (1%)
  other arithmetic  1.84 us (1%)
    pallas_call x13, Pallas kernels, call(): pl.pallas_call(kernel, input_output_aliases=alias or {}, out_shape=out, i...  43.6 us
    ppermute x7, starting transfers between devices, exchange(): lax.ppermute(down, 'space', backward)  28.2 us
    all_to_all x1, blocking collectives, per_device(): change_shares = lax.all_to_all(change_share, 'tm', 0, 0)  20.6 us
    ppermute x7, waiting for transfers between devices, exchange(): lax.ppermute(up, 'space', forward)  20.6 us
    ppermute x2, waiting for transfers between devices, from_behind(): return lax.ppermute(array, 'tm', [(i, i + 1) for i in range(count - 1)])  13 us
    all_to_all x1, starting transfers between devices, per_device(): slope_shares = lax.all_to_all(slope_share, 'tm', 0, 0)  10.8 us
    all_to_all x1, waiting for transfers between devices, per_device(): error_share = lax.all_to_all(error_shares, 'tm', 0, 0)  10.1 us
    all_to_all x1, starting transfers between devices, per_device(): error_share = lax.all_to_all(error_shares, 'tm', 0, 0)  6.29 us
  transfers between devices with their start and end apart: 18, of which 6 were waited for; matrix products, arithmetic and copies ran while one was open for 1% of the time, Pallas kernels for 21%

profile of v4, /device:TPU:6, one launch (start us, length us, event | category | flops | bytes accessed | tf_op | source)
XLA Modules:
  0.0 166.7 jit_solution(4879519560974912801)
XLA Ops:
  0.6 3.8 %shard_map.60 = (f32[5,12,16,128]{3,2,1,0:T(8,128)}, f32[5,12,16,128]{3,2,1,0:T(8,128)}) custom-call(f32[5,5]{1,0:T(8,128)} %mix_ref.25, f32[8,5,8,16,128]{4,3,2,1,0:T(8,128)} %primal_hbm.3), custom_call_target="tpu_custom_call" | custom-call | flops 6144000 | bytes 3604580 | tf_op jit(solution)/shard_map/pallas_call | solution.py:452
  4.4 2.0 %collective-permute-start.2 = (f32[5,12,16,128]{3,2,1,0:T(8,128)}, f32[5,12,16,128]{3,2,1,0:T(8,128)S(1)}, u32[]{:S(2)}, u32[]{:S(2)}) collective-permute-start(f32[5,12,16,128]{3,2,1,0:T(8,128)} %get-tuple-element.38), channel_id=1, source_target_pairs={{0,1},{1,2},{2,3},{3,4},{4,5},{5,6},{6,7},{7,0},{8,9},{9,10},{10,1... | collective-permute-start | bytes 1474568 | tf_op jit(solution)/shard_map/ppermute | solution.py:483
  6.4 2.5 %collective-permute-start.3 = (f32[5,12,16,128]{3,2,1,0:T(8,128)}, f32[5,12,16,128]{3,2,1,0:T(8,128)}, u32[]{:S(2)}, u32[]{:S(2)}) collective-permute-start(f32[5,12,16,128]{3,2,1,0:T(8,128)} %get-tuple-element.39), channel_id=1, source_target_pairs={{1,0},{2,1},{3,2},{4,3},{5,4},{6,5},{7,6},{0,7},{9,8},{10,9},{11,1... | collective-permute-start | bytes 1474568 | tf_op jit(solution)/shard_map/ppermute | solution.py:483
  8.9 6.4 %shard_map.59 = (f32[32,5,4,128]{3,2,1,0:T(4,128)}, f32[8,5,8,16,128]{4,3,2,1,0:T(8,128)S(1)}, f32[5,5,16,128]{3,2,1,0:T(8,128)S(1)}, f32[5,5,16,128]{3,2,1,0:T(...) custom-call(f32[5,5]{1,0:T(8,128)S(1)} %copy-done.1, f32[8,5,8,16,128]{4,3,2,1,0:T(8,128)} %primal_hbm.3, ...), custom_call_target="tpu_custom_call" | custom-call | flops 25600000 | bytes 9175140 | tf_op jit(solution)/shard_map/pallas_call | solution.py:452
  15.4 4.1 %collective-permute-start.1 = (f32[5,5,16,128]{3,2,1,0:T(8,128)}, f32[5,5,16,128]{3,2,1,0:T(8,128)}, u32[]{:S(2)}, u32[]{:S(2)}) collective-permute-start(f32[5,5,16,128]{3,2,1,0:T(8,128)} %get-tuple-element.36), channel_id=1, source_target_pairs={{1,0},{2,1},{3,2},{4,3},{5,4},{6,5},{7,6},{0,7},{9,8},{10,9},{11,1... | collective-permute-start | bytes 614408 | tf_op jit(solution)/shard_map/ppermute | solution.py:483
  19.6 16.5 %collective-permute-done.low_ref = f32[5,5,16,128]{3,2,1,0:T(8,128)S(1)} collective-permute-done((f32[5,5,16,128]{3,2,1,0:T(8,128)S(1)}, f32[5,5,16,128]{3,2,1,0:T(8,128)S(1)}, u32[]{:S(2)}, u32[]{:S(2)}) %collective-permute-start) | collective-permute-done | bytes 204832 | tf_op jit(solution)/shard_map/ppermute | solution.py:483
  36.7 2.0 %collective-permute-start.5 = (f32[5,3,16,128]{3,2,1,0:T(8,128)}, f32[5,3,16,128]{3,2,1,0:T(8,128)}, u32[]{:S(2)}, u32[]{:S(2)}) collective-permute-start(f32[5,3,16,128]{3,2,1,0:T(8,128)} %get-tuple-element.44), channel_id=1, source_target_pairs={{1,0},{2,1},{3,2},{4,3},{5,4},{6,5},{7,6},{0,7},{9,8},{10,9},{11,1... | collective-permute-start | bytes 368648 | tf_op jit(solution)/shard_map/ppermute | solution.py:483
  38.8 10.8 %all-to-all-start = ((f32[32,5,4,128]{3,2,1,0:T(4,128)}), f32[32,5,4,128]{3,2,1,0:T(4,128)}, u32[]{:S(2)}, u32[]{:S(2)}) async-start(f32[32,5,4,128]{3,2,1,0:T(4,128)} %get-tuple-element.46), calls=%async_computation | async-start | bytes 655360 | tf_op jit(solution)/shard_map/all_to_all | solution.py:548
  49.6 0.9 copy-done.4
  50.5 4.8 %shard_map.61 = (f32[5,8,16,128]{3,2,1,0:T(8,128)S(1)}, f32[2,5,4,16,128]{4,3,2,1,0:T(8,128)S(1)}, f32[2,5,8,16,128]{4,3,2,1,0:T(8,128)S(1)}) custom-call(f32[5,5]{1,0:T(8,128)S(1)} %copy-done.1, f32[8,5,8,16,128]{4,3,2,1,0:T(8,128)} %source_hbm.17, f32[5,8,16,128]{3,2,1,0:T(8,128)S(1)} %bitcast.8, f32[5,5,16,128]{3,2,1,0:T(8,128)S(1)} %copy-done.4, ...), custom_call_target="tpu_custom_call" | custom-call | flops 10752000 | bytes 8274020 | tf_op jit(solution)/shard_map/pallas_call | solution.py:452
  55.3 3.3 %shard_map.62 = f32[5,8,16,128]{3,2,1,0:T(8,128)} custom-call(f32[5,5]{1,0:T(8,128)S(1)} %copy-done.1, f32[2,5,8,16,128]{4,3,2,1,0:T(8,128)S(1)} %get-tuple-element.40.later_ref, f32[5,8,16,128]{3,2,1,0:T(8,128)S(1)} %get-tuple-element.41.middle_ref, f32[2,5,4,16,128]{4,3,2,1,0:T(8,128)S(1)} %get-tuple-element.42.middle_added, ...), custom_call_target="tpu_custom_call" | custom-call | flops 11776000 | bytes 5488740 | tf_op jit(solution)/shard_map/pallas_call | solution.py:452
  58.5 2.0 %collective-permute-start.6 = (f32[5,8,16,128]{3,2,1,0:T(8,128)}, f32[5,8,16,128]{3,2,1,0:T(8,128)}, u32[]{:S(2)}, u32[]{:S(2)}) collective-permute-start(f32[5,8,16,128]{3,2,1,0:T(8,128)} %shard_map.62), channel_id=1, source_target_pairs={{0,8},{8,16},{16,24},{24,32},{32,40},{40,48},{48,56},{56,64},{64,7... | collective-permute-start | bytes 983048 | tf_op jit(solution)/shard_map/ppermute | solution.py:476
  60.6 13.0 %collective-permute-done.6.ended_ref = f32[5,8,16,128]{3,2,1,0:T(8,128)} collective-permute-done((f32[5,8,16,128]{3,2,1,0:T(8,128)}, f32[5,8,16,128]{3,2,1,0:T(8,128)}, u32[]{:S(2)}, u32[]{:S(2)}) %collective-permute-start.6) | collective-permute-done | bytes 327712 | tf_op jit(solution)/shard_map/ppermute | solution.py:476
  73.6 3.1 %shard_map.63 = (f32[5,8,16,128]{3,2,1,0:T(8,128)}, f32[5,8,16,128]{3,2,1,0:T(8,128)S(1)}, f32[5,8,16,128]{3,2,1,0:T(8,128)S(1)}, f32[5,5,16,128]{3,2,1,0:T(8,128)S(1)}, f32[5,5,16,128]{3,2,1,0:T(8,128)S(1)}) custom-call(f32[5,5]{1,0:T(8,128)S(1)} %copy-done.1, s32[1]{0:T(128)} %bitcast.leads_ref, f32[8,5,8,16,128]{4,3,2,1,0:T(8,128)} %source_hbm.17, ...), custom_call_target="tpu_custom_call" | custom-call | flops 7680000 | bytes 7290984 | tf_op jit(solution)/shard_map/pallas_call | solution.py:452
  77.0 4.0 %collective-permute-start.8 = (f32[5,5,16,128]{3,2,1,0:T(8,128)S(1)}, f32[5,5,16,128]{3,2,1,0:T(8,128)S(1)}, u32[]{:S(2)}, u32[]{:S(2)}) collective-permute-start(f32[5,5,16,128]{3,2,1,0:T(8,128)S(1)} %get-tuple-element.49), channel_id=1, source_target_pairs={{1,0},{2,1},{3,2},{4,3},{5,4},{6,5},{7,6},{0,7},{9,8},{10,9},{11,1... | collective-permute-start | bytes 614408 | tf_op jit(solution)/shard_map/ppermute | solution.py:483
  81.1 1.1 shard_map.65
  82.3 4.1 %collective-permute-start.10 = (f32[5,3,16,128]{3,2,1,0:T(8,128)S(1)}, f32[5,3,16,128]{3,2,1,0:T(8,128)S(1)}, u32[]{:S(2)}, u32[]{:S(2)}) collective-permute-start(f32[5,3,16,128]{3,2,1,0:T(8,128)S(1)} %get-tuple-element.54), channel_id=1, source_target_pairs={{1,0},{2,1},{3,2},{4,3},{5,4},{6,5},{7,6},{0,7},{9,8},{10,9},{11,1... | collective-permute-start | bytes 368648 | tf_op jit(solution)/shard_map/ppermute | solution.py:483
  87.1 3.6 %shard_map.64 = (f32[5,8,16,128]{3,2,1,0:T(8,128)S(1)}, f32[2,5,4,16,128]{4,3,2,1,0:T(8,128)S(1)}) custom-call(f32[5,5]{1,0:T(8,128)S(1)} %copy-done.1, f32[8,5,8,16,128]{4,3,2,1,0:T(8,128)} %source_hbm.17, f32[5,8,16,128]{3,2,1,0:T(8,128)S(1)} %get-tuple-element.47.start_ref, f32[5,5,16,128]{3,2,1,0:T(8,128)S(1)} %collective-permute-done.7.low_ref, ...), custom_call_target="tpu_custom_call" | custom-call | flops 10752000 | bytes 7618660 | tf_op jit(solution)/shard_map/pallas_call | solution.py:452
  90.7 3.2 %shard_map.66 = (f32[5,8,16,128]{3,2,1,0:T(8,128)}, f32[32,5,4,128]{3,2,1,0:T(4,128)S(1)}) custom-call(f32[5,5]{1,0:T(8,128)S(1)} %copy-done.1, s32[1]{0:T(128)} %bitcast.leads_ref, f32[8,5,8,16,128]{4,3,2,1,0:T(8,128)} %source_hbm.17, f32[5,8,16,128]{3,2,1,0:T(8,128)S(1)} %get-tuple-element.50.middle_ref, ...), custom_call_target="tpu_custom_call" | custom-call | flops 12800000 | bytes 7782504 | tf_op jit(solution)/shard_map/pallas_call | solution.py:452
  94.7 20.6 %all_to_all.15.resid_ref = f32[32,5,4,128]{3,2,1,0:T(4,128)S(1)} all-to-all(f32[32,5,4,128]{3,2,1,0:T(4,128)} %copy-done.2), channel_id=1, replica_groups=mesh['tm'=32,'space'=8] {'tm'}, dimensions={0} | all-to-all | bytes 655360 | tf_op jit(solution)/shard_map/all_to_all | solution.py:578
  115.3 2.1 %shard_map.67 = f32[32,5,4,128]{3,2,1,0:T(4,128)} custom-call(f32[5,5]{1,0:T(8,128)S(1)} %copy-done.1, f32[32,5,4,128]{3,2,1,0:T(4,128)} %all-to-all-done.slope_ref, f32[32,5,4,128]{3,2,1,0:T(4,128)S(1)} %all_to_all.15.resid_ref), custom_call_target="tpu_custom_call" | custom-call | flops 4096000 | bytes 983140 | tf_op jit(solution)/shard_map/pallas_call | solution.py:452
  117.4 6.3 %all-to-all-start.2 = ((f32[32,5,4,128]{3,2,1,0:T(4,128)}), f32[32,5,4,128]{3,2,1,0:T(4,128)S(1)}, u32[]{:S(2)}, u32[]{:S(2)}) async-start(f32[32,5,4,128]{3,2,1,0:T(4,128)} %shard_map.67), calls=%async_computation.2 | async-start | bytes 655360 | tf_op jit(solution)/shard_map/all_to_all | solution.py:581
  123.7 2.0 %collective-permute-start.15 = (f32[5,8,16,128]{3,2,1,0:T(8,128)}, f32[5,8,16,128]{3,2,1,0:T(8,128)}, u32[]{:S(2)}, u32[]{:S(2)}) collective-permute-start(f32[5,8,16,128]{3,2,1,0:T(8,128)} %get-tuple-element.67), channel_id=1, source_target_pairs={{0,8},{8,16},{16,24},{24,32},{32,40},{40,48},{48,56},{56,64},{64,7... | collective-permute-start | bytes 983048 | tf_op jit(solution)/shard_map/ppermute | solution.py:476
  125.7 10.1 %all-to-all-done.2.share_ref = f32[32,5,4,128]{3,2,1,0:T(4,128)S(1)} async-done(((f32[32,5,4,128]{3,2,1,0:T(4,128)}), f32[32,5,4,128]{3,2,1,0:T(4,128)S(1)}, u32[]{:S(2)}, u32[]{:S(2)}) %all-to-all-start.2) | async-done | bytes 327712 | tf_op jit(solution)/shard_map/all_to_all | solution.py:581
  135.8 3.0 %shard_map.68 = (f32[5,8,16,128]{3,2,1,0:T(8,128)S(1)}, f32[5,8,16,128]{3,2,1,0:T(8,128)S(1)}, f32[5,5,16,128]{3,2,1,0:T(8,128)S(1)}, f32[5,5,16,128]{3,2,1,0:T(8,128)S(1)}) custom-call(f32[5,5]{1,0:T(8,128)S(1)} %copy-done.1, s32[1]{0:T(128)} %bitcast.leads_ref, f32[5,8,16,128]{3,2,1,0:T(8,128)} %get-tuple-element.45.relaxed_hbm, ...), custom_call_target="tpu_custom_call" | custom-call | flops 7680000 | bytes 6963304 | tf_op jit(solution)/shard_map/pallas_call | solution.py:452
  138.8 2.0 %shard_map.69 = (f32[5,2,16,128]{3,2,1,0:T(8,128)S(1)}, f32[5,2,16,128]{3,2,1,0:T(8,128)S(1)}, f32[5,8,16,128]{3,2,1,0:T(8,128)S(1)}) custom-call(f32[5,5]{1,0:T(8,128)S(1)} %copy-done.1, f32[8,5,8,16,128]{4,3,2,1,0:T(8,128)} %source_hbm.17, f32[5,8,16,128]{3,2,1,0:T(8,128)S(1)} %get-tuple-element.56.middle_ref, ...), custom_call_target="tpu_custom_call" | custom-call | flops 4096000 | bytes 6062180 | tf_op jit(solution)/shard_map/pallas_call | solution.py:452
  141.0 7.2 %collective-permute-start.14 = (f32[5,2,16,128]{3,2,1,0:T(8,128)S(1)}, f32[5,2,16,128]{3,2,1,0:T(8,128)S(1)}, u32[]{:S(2)}, u32[]{:S(2)}) collective-permute-start(f32[5,2,16,128]{3,2,1,0:T(8,128)S(1)} %get-tuple-element.66), channel_id=1, source_target_pairs={{1,0},{2,1},{3,2},{4,3},{5,4},{6,5},{7,6},{0,7},{9,8},{10,9},{11,1... | collective-permute-start | bytes 245768 | tf_op jit(solution)/shard_map/ppermute | solution.py:483
  148.2 4.1 %collective-permute-start.12 = (f32[5,5,16,128]{3,2,1,0:T(8,128)S(1)}, f32[5,5,16,128]{3,2,1,0:T(8,128)S(1)}, u32[]{:S(2)}, u32[]{:S(2)}) collective-permute-start(f32[5,5,16,128]{3,2,1,0:T(8,128)S(1)} %get-tuple-element.60), channel_id=1, source_target_pairs={{1,0},{2,1},{3,2},{4,3},{5,4},{6,5},{7,6},{0,7},{9,8},{10,9},{11,1... | collective-permute-start | bytes 614408 | tf_op jit(solution)/shard_map/ppermute | solution.py:483
  152.3 1.8 %fusion = f32[1,5,8,16,128]{4,3,2,1,0:T(8,128)} fusion(f32[5,8,16,128]{3,2,1,0:T(8,128)} %collective-permute-done.15, f32[8,5,8,16,128]{4,3,2,1,0:T(8,128)} %source_hbm.17, pred[]{:T(512)S(6)} %eq.3), kind=kLoop, calls=%fused_computation.1 | loop fusion | flops 81920 | bytes 983041 | tf_op jit(solution)/shard_map/broadcast_in_dim | solution.py:621
  154.2 4.1 %collective-permute-done.11.low_ref = f32[5,5,16,128]{3,2,1,0:T(8,128)S(1)} collective-permute-done((f32[5,5,16,128]{3,2,1,0:T(8,128)S(1)}, f32[5,5,16,128]{3,2,1,0:T(8,128)S(1)}, u32[]{:S(2)}, u32[]{:S(2)}) %collective-permute-start.11) | collective-permute-done | bytes 204832 | tf_op jit(solution)/shard_map/ppermute | solution.py:483
  159.2 4.6 %shard_map.70 = (f32[8,5,8,16,128]{4,3,2,1,0:T(8,128)}, f32[5,8,16,128]{3,2,1,0:T(8,128)S(1)}, f32[2,5,4,16,128]{4,3,2,1,0:T(8,128)S(1)}, f32[2,5,8,16,128]{4,3,2,1,0:T(8,128)S(1)}) custom-call(f32[5,5]{1,0:T(8,128)S(1)} %copy-done.1, f32[8,5,8,16,128]{4,3,2,1,0:T(8,128)} %source_hbm.17, f32[5,8,16,128]{3,2,1,0:T(8,128)S(1)} %get-tuple-element.57.next_ref, ...), custom_call_target="tpu_custom_call" | custom-call | flops 10752000 | bytes 11223140 | tf_op jit(solution)/shard_map/pallas_call | solution.py:452
  163.8 2.7 %shard_map.71 = f32[8,5,8,16,128]{4,3,2,1,0:T(8,128)} custom-call(f32[5,5]{1,0:T(8,128)S(1)} %copy-done.1, f32[8,5,8,16,128]{4,3,2,1,0:T(8,128)} %get-tuple-element.61.earlier_hbm, f32[2,5,8,16,128]{4,3,2,1,0:T(8,128)S(1)} %get-tuple-element.62.later_ref, f32[5,8,16,128]{3,2,1,0:T(8,128)S(1)} %get-tuple-element.63.middle_ref, ...), custom_call_target="tpu_custom_call", output_to_operand_aliasing={{}: (1, {})} | custom-call | flops 8704000 | bytes 10322020 | tf_op jit(solution)/shard_map/pallas_call | solution.py:452
  (29 shorter events, 3.7 us)
Async XLA Ops:
  0.6 8.3 %copy-start.1 = (f32[5,5]{1,0:T(8,128)S(1)}, f32[5,5]{1,0:T(8,128)}, u32[]{:S(2)}) copy-start(f32[5,5]{1,0:T(8,128)} %mix_ref.25) | copy-start | bytes 304
  0.6 8.3 %copy-start = (f32[1,5,8,16,128]{4,3,2,1,0:T(8,128)S(1)}, f32[1,5,8,16,128]{4,3,2,1,0:T(8,128)}, u32[]{:S(2)}) copy-start(f32[1,5,8,16,128]{4,3,2,1,0:T(8,128)} %guess_ref.3) | copy-start | bytes 983044
  4.4 45.1 %collective-permute-start.2 = (f32[5,12,16,128]{3,2,1,0:T(8,128)}, f32[5,12,16,128]{3,2,1,0:T(8,128)S(1)}, u32[]{:S(2)}, u32[]{:S(2)}) collective-permute-start(f32[5,12,16,128]{3,2,1,0:T(8,128)} %get-tuple-element.38), channel_id=1, source_target_pairs={{0,1},{1,2},{2,3},{3,4},{4,5},{5,6},{6,7},{7,0},{8,9},{9,10},{10,1... | collective-permute-start | bytes 1474568 | tf_op jit(solution)/shard_map/ppermute | solution.py:483
  6.4 43.1 %collective-permute-start.3 = (f32[5,12,16,128]{3,2,1,0:T(8,128)}, f32[5,12,16,128]{3,2,1,0:T(8,128)}, u32[]{:S(2)}, u32[]{:S(2)}) collective-permute-start(f32[5,12,16,128]{3,2,1,0:T(8,128)} %get-tuple-element.39), channel_id=1, source_target_pairs={{1,0},{2,1},{3,2},{4,3},{5,4},{6,5},{7,6},{0,7},{9,8},{10,9},{11,1... | collective-permute-start | bytes 1474568 | tf_op jit(solution)/shard_map/ppermute | solution.py:483
  15.3 20.7 %collective-permute-start = (f32[5,5,16,128]{3,2,1,0:T(8,128)S(1)}, f32[5,5,16,128]{3,2,1,0:T(8,128)S(1)}, u32[]{:S(2)}, u32[]{:S(2)}) collective-permute-start(f32[5,5,16,128]{3,2,1,0:T(8,128)S(1)} %get-tuple-element.35), channel_id=1, source_target_pairs={{0,1},{1,2},{2,3},{3,4},{4,5},{5,6},{6,7},{7,0},{8,9},{9,10},{10,1... | collective-permute-start | bytes 614408 | tf_op jit(solution)/shard_map/ppermute | solution.py:483
  15.4 34.1 %collective-permute-start.1 = (f32[5,5,16,128]{3,2,1,0:T(8,128)}, f32[5,5,16,128]{3,2,1,0:T(8,128)}, u32[]{:S(2)}, u32[]{:S(2)}) collective-permute-start(f32[5,5,16,128]{3,2,1,0:T(8,128)} %get-tuple-element.36), channel_id=1, source_target_pairs={{1,0},{2,1},{3,2},{4,3},{5,4},{6,5},{7,6},{0,7},{9,8},{10,9},{11,1... | collective-permute-start | bytes 614408 | tf_op jit(solution)/shard_map/ppermute | solution.py:483
  19.5 35.7 %collective-permute-start.4 = (f32[5,3,16,128]{3,2,1,0:T(8,128)}, f32[5,3,16,128]{3,2,1,0:T(8,128)}, u32[]{:S(2)}, u32[]{:S(2)}) collective-permute-start(f32[5,3,16,128]{3,2,1,0:T(8,128)} %get-tuple-element.43), channel_id=1, source_target_pairs={{0,1},{1,2},{2,3},{3,4},{4,5},{5,6},{6,7},{7,0},{8,9},{9,10},{10,1... | collective-permute-start | bytes 368648 | tf_op jit(solution)/shard_map/ppermute | solution.py:483
  36.1 0.7 copy-start.3
  36.7 18.5 %collective-permute-start.5 = (f32[5,3,16,128]{3,2,1,0:T(8,128)}, f32[5,3,16,128]{3,2,1,0:T(8,128)}, u32[]{:S(2)}, u32[]{:S(2)}) collective-permute-start(f32[5,3,16,128]{3,2,1,0:T(8,128)} %get-tuple-element.44), channel_id=1, source_target_pairs={{1,0},{2,1},{3,2},{4,3},{5,4},{6,5},{7,6},{0,7},{9,8},{10,9},{11,1... | collective-permute-start | bytes 368648 | tf_op jit(solution)/shard_map/ppermute | solution.py:483
  38.8 55.9 %all-to-all-start = ((f32[32,5,4,128]{3,2,1,0:T(4,128)}), f32[32,5,4,128]{3,2,1,0:T(4,128)}, u32[]{:S(2)}, u32[]{:S(2)}) async-start(f32[32,5,4,128]{3,2,1,0:T(4,128)} %get-tuple-element.46), calls=%async_computation | async-start | bytes 655360 | tf_op jit(solution)/shard_map/all_to_all | solution.py:548
  49.5 0.9 copy-start.4
  58.5 15.0 %collective-permute-start.6 = (f32[5,8,16,128]{3,2,1,0:T(8,128)}, f32[5,8,16,128]{3,2,1,0:T(8,128)}, u32[]{:S(2)}, u32[]{:S(2)}) collective-permute-start(f32[5,8,16,128]{3,2,1,0:T(8,128)} %shard_map.62), channel_id=1, source_target_pairs={{0,8},{8,16},{16,24},{24,32},{32,40},{40,48},{48,56},{56,64},{64,7... | collective-permute-start | bytes 983048 | tf_op jit(solution)/shard_map/ppermute | solution.py:476
  76.7 9.7 %collective-permute-start.7 = (f32[5,5,16,128]{3,2,1,0:T(8,128)S(1)}, f32[5,5,16,128]{3,2,1,0:T(8,128)S(1)}, u32[]{:S(2)}, u32[]{:S(2)}) collective-permute-start(f32[5,5,16,128]{3,2,1,0:T(8,128)S(1)} %get-tuple-element.48), channel_id=1, source_target_pairs={{0,1},{1,2},{2,3},{3,4},{4,5},{5,6},{6,7},{7,0},{8,9},{9,10},{10,1... | collective-permute-start | bytes 614408 | tf_op jit(solution)/shard_map/ppermute | solution.py:483
  77.0 10.1 %collective-permute-start.8 = (f32[5,5,16,128]{3,2,1,0:T(8,128)S(1)}, f32[5,5,16,128]{3,2,1,0:T(8,128)S(1)}, u32[]{:S(2)}, u32[]{:S(2)}) collective-permute-start(f32[5,5,16,128]{3,2,1,0:T(8,128)S(1)} %get-tuple-element.49), channel_id=1, source_target_pairs={{1,0},{2,1},{3,2},{4,3},{5,4},{6,5},{7,6},{0,7},{9,8},{10,9},{11,1... | collective-permute-start | bytes 614408 | tf_op jit(solution)/shard_map/ppermute | solution.py:483
  82.2 8.6 %collective-permute-start.9 = (f32[5,3,16,128]{3,2,1,0:T(8,128)S(1)}, f32[5,3,16,128]{3,2,1,0:T(8,128)S(1)}, u32[]{:S(2)}, u32[]{:S(2)}) collective-permute-start(f32[5,3,16,128]{3,2,1,0:T(8,128)S(1)} %get-tuple-element.53), channel_id=1, source_target_pairs={{0,1},{1,2},{2,3},{3,4},{4,5},{5,6},{6,7},{7,0},{8,9},{9,10},{10,1... | collective-permute-start | bytes 368648 | tf_op jit(solution)/shard_map/ppermute | solution.py:483
  82.3 8.5 %collective-permute-start.10 = (f32[5,3,16,128]{3,2,1,0:T(8,128)S(1)}, f32[5,3,16,128]{3,2,1,0:T(8,128)S(1)}, u32[]{:S(2)}, u32[]{:S(2)}) collective-permute-start(f32[5,3,16,128]{3,2,1,0:T(8,128)S(1)} %get-tuple-element.54), channel_id=1, source_target_pairs={{1,0},{2,1},{3,2},{4,3},{5,4},{6,5},{7,6},{0,7},{9,8},{10,9},{11,1... | collective-permute-start | bytes 368648 | tf_op jit(solution)/shard_map/ppermute | solution.py:483
  94.0 0.7 copy-start.2
  117.4 18.4 %all-to-all-start.2 = ((f32[32,5,4,128]{3,2,1,0:T(4,128)}), f32[32,5,4,128]{3,2,1,0:T(4,128)S(1)}, u32[]{:S(2)}, u32[]{:S(2)}) async-start(f32[32,5,4,128]{3,2,1,0:T(4,128)} %shard_map.67), calls=%async_computation.2 | async-start | bytes 655360 | tf_op jit(solution)/shard_map/all_to_all | solution.py:581
  123.7 28.6 %collective-permute-start.15 = (f32[5,8,16,128]{3,2,1,0:T(8,128)}, f32[5,8,16,128]{3,2,1,0:T(8,128)}, u32[]{:S(2)}, u32[]{:S(2)}) collective-permute-start(f32[5,8,16,128]{3,2,1,0:T(8,128)} %get-tuple-element.67), channel_id=1, source_target_pairs={{0,8},{8,16},{16,24},{24,32},{32,40},{40,48},{48,56},{56,64},{64,7... | collective-permute-start | bytes 983048 | tf_op jit(solution)/shard_map/ppermute | solution.py:476
  140.9 22.9 %collective-permute-start.13 = (f32[5,2,16,128]{3,2,1,0:T(8,128)S(1)}, f32[5,2,16,128]{3,2,1,0:T(8,128)S(1)}, u32[]{:S(2)}, u32[]{:S(2)}) collective-permute-start(f32[5,2,16,128]{3,2,1,0:T(8,128)S(1)} %get-tuple-element.65), channel_id=1, source_target_pairs={{0,1},{1,2},{2,3},{3,4},{4,5},{5,6},{6,7},{7,0},{8,9},{9,10},{10,1... | collective-permute-start | bytes 245768 | tf_op jit(solution)/shard_map/ppermute | solution.py:483
  141.0 22.8 %collective-permute-start.14 = (f32[5,2,16,128]{3,2,1,0:T(8,128)S(1)}, f32[5,2,16,128]{3,2,1,0:T(8,128)S(1)}, u32[]{:S(2)}, u32[]{:S(2)}) collective-permute-start(f32[5,2,16,128]{3,2,1,0:T(8,128)S(1)} %get-tuple-element.66), channel_id=1, source_target_pairs={{1,0},{2,1},{3,2},{4,3},{5,4},{6,5},{7,6},{0,7},{9,8},{10,9},{11,1... | collective-permute-start | bytes 245768 | tf_op jit(solution)/shard_map/ppermute | solution.py:483
  148.2 10.1 %collective-permute-start.11 = (f32[5,5,16,128]{3,2,1,0:T(8,128)S(1)}, f32[5,5,16,128]{3,2,1,0:T(8,128)S(1)}, u32[]{:S(2)}, u32[]{:S(2)}) collective-permute-start(f32[5,5,16,128]{3,2,1,0:T(8,128)S(1)} %get-tuple-element.59), channel_id=1, source_target_pairs={{0,1},{1,2},{2,3},{3,4},{4,5},{5,6},{6,7},{7,0},{8,9},{9,10},{10,1... | collective-permute-start | bytes 614408 | tf_op jit(solution)/shard_map/ppermute | solution.py:483
  148.2 11.0 %collective-permute-start.12 = (f32[5,5,16,128]{3,2,1,0:T(8,128)S(1)}, f32[5,5,16,128]{3,2,1,0:T(8,128)S(1)}, u32[]{:S(2)}, u32[]{:S(2)}) collective-permute-start(f32[5,5,16,128]{3,2,1,0:T(8,128)S(1)} %get-tuple-element.60), channel_id=1, source_target_pairs={{1,0},{2,1},{3,2},{4,3},{5,4},{6,5},{7,6},{0,7},{9,8},{10,9},{11,1... | collective-permute-start | bytes 614408 | tf_op jit(solution)/shard_map/ppermute | solution.py:483

commit v5 on v3

--- a/solution.py
+++ b/solution.py
@@ -92,18 +92,18 @@
                 )
     for copy in copies:
         copy.start()
-    for copy in copies:
-        copy.wait()
-    for state, out_ref in ((up_state, up_ref), (down_state, down_ref)):
+    for side, (state, out_ref) in enumerate(((up_state, up_ref), (down_state, down_ref))):
+        for copy in copies[side::2]:
+            copy.wait()
 
         def plane(n, carry):
-            for k in range(2):
-                x = 2 * n + k
+            for k in range(4):
+                x = 4 * n + k
                 for f, value in enumerate(slopes(mix, [state[f, x] for f in range(FIELDS)])):
                     out_ref[f, x] = value
             return carry
 
-        lax.fori_loop(0, PACKED // 2, plane, 0)
+        lax.fori_loop(0, PACKED // 4, plane, 0)
 
 
 def shares(part):

time: 161 us -> 161 us (level)
  no operation moved by 1% of the time
where the time goes in v5:
time: 161 us; the launch traced here: 160 us
  starting transfers between devices  53.1 us (33%)
  Pallas kernels  43.4 us (27%)
  waiting for transfers between devices  32.7 us (20%)
  blocking collectives  25.6 us (16%)
  local copies, waits for them, and re-layouts  2.3 us (1%)
  other arithmetic  1.84 us (1%)
    pallas_call x13, Pallas kernels, call(): pl.pallas_call(kernel, input_output_aliases=alias or {}, out_shape=out, i...  43.4 us
    all_to_all x1, blocking collectives, per_device(): change_shares = lax.all_to_all(change_share, 'tm', 0, 0)  25.6 us
    ppermute x7, starting transfers between devices, exchange(): lax.ppermute(down, 'space', backward)  24 us
    ppermute x7, waiting for transfers between devices, exchange(): lax.ppermute(up, 'space', forward)  13.3 us
    all_to_all x1, starting transfers between devices, per_device(): slope_shares = lax.all_to_all(slope_share, 'tm', 0, 0)  13.2 us
    all_to_all x1, waiting for transfers between devices, per_device(): error_share = lax.all_to_all(error_shares, 'tm', 0, 0)  9.67 us
    ppermute x2, waiting for transfers between devices, from_behind(): return lax.ppermute(array, 'tm', [(i, i + 1) for i in range(count - 1)])  9.66 us
    ppermute x2, starting transfers between devices, from_behind(): return lax.ppermute(array, 'tm', [(i, i + 1) for i in range(count - 1)])  8.87 us
  transfers between devices with their start and end apart: 18, of which 3 were waited for; matrix products, arithmetic and copies ran while one was open for 1% of the time, Pallas kernels for 22%

profile of v5, /device:TPU:1, one launch (start us, length us, event | category | flops | bytes accessed | tf_op | source)
XLA Modules:
  0.0 160.0 jit_solution(12720196858858152932)
XLA Ops:
  0.6 3.6 %shard_map.60 = (f32[5,12,16,128]{3,2,1,0:T(8,128)}, f32[5,12,16,128]{3,2,1,0:T(8,128)}) custom-call(f32[5,5]{1,0:T(8,128)} %mix_ref.25, f32[8,5,8,16,128]{4,3,2,1,0:T(8,128)} %primal_hbm.3), custom_call_target="tpu_custom_call" | custom-call | flops 6144000 | bytes 3604580 | tf_op jit(solution)/shard_map/pallas_call | solution.py:452
  4.3 2.5 %collective-permute-start.2 = (f32[5,12,16,128]{3,2,1,0:T(8,128)}, f32[5,12,16,128]{3,2,1,0:T(8,128)S(1)}, u32[]{:S(2)}, u32[]{:S(2)}) collective-permute-start(f32[5,12,16,128]{3,2,1,0:T(8,128)} %get-tuple-element.38), channel_id=1, source_target_pairs={{0,1},{1,2},{2,3},{3,4},{4,5},{5,6},{6,7},{7,0},{8,9},{9,10},{10,1... | collective-permute-start | bytes 1474568 | tf_op jit(solution)/shard_map/ppermute | solution.py:483
  6.8 2.5 %collective-permute-start.3 = (f32[5,12,16,128]{3,2,1,0:T(8,128)}, f32[5,12,16,128]{3,2,1,0:T(8,128)}, u32[]{:S(2)}, u32[]{:S(2)}) collective-permute-start(f32[5,12,16,128]{3,2,1,0:T(8,128)} %get-tuple-element.39), channel_id=1, source_target_pairs={{1,0},{2,1},{3,2},{4,3},{5,4},{6,5},{7,6},{0,7},{9,8},{10,9},{11,1... | collective-permute-start | bytes 1474568 | tf_op jit(solution)/shard_map/ppermute | solution.py:483
  9.4 6.3 %shard_map.59 = (f32[32,5,4,128]{3,2,1,0:T(4,128)}, f32[8,5,8,16,128]{4,3,2,1,0:T(8,128)S(1)}, f32[5,4,16,128]{3,2,1,0:T(8,128)S(1)}, f32[5,4,16,128]{3,2,1,0:T(...) custom-call(f32[5,5]{1,0:T(8,128)S(1)} %copy-done.1, f32[8,5,8,16,128]{4,3,2,1,0:T(8,128)} %primal_hbm.3, ...), custom_call_target="tpu_custom_call" | custom-call | flops 25600000 | bytes 9175140 | tf_op jit(solution)/shard_map/pallas_call | solution.py:452
  15.8 3.6 %collective-permute-start.1 = (f32[5,4,16,128]{3,2,1,0:T(8,128)}, f32[5,4,16,128]{3,2,1,0:T(8,128)}, u32[]{:S(2)}, u32[]{:S(2)}) collective-permute-start(f32[5,4,16,128]{3,2,1,0:T(8,128)} %get-tuple-element.36), channel_id=1, source_target_pairs={{1,0},{2,1},{3,2},{4,3},{5,4},{6,5},{7,6},{0,7},{9,8},{10,9},{11,1... | collective-permute-start | bytes 491528 | tf_op jit(solution)/shard_map/ppermute | solution.py:483
  19.4 13.3 %collective-permute-done.low_ref = f32[5,4,16,128]{3,2,1,0:T(8,128)S(1)} collective-permute-done((f32[5,4,16,128]{3,2,1,0:T(8,128)S(1)}, f32[5,4,16,128]{3,2,1,0:T(8,128)S(1)}, u32[]{:S(2)}, u32[]{:S(2)}) %collective-permute-start) | collective-permute-done | bytes 163872 | tf_op jit(solution)/shard_map/ppermute | solution.py:483
  33.3 2.9 %collective-permute-start.5 = (f32[5,4,16,128]{3,2,1,0:T(8,128)}, f32[5,4,16,128]{3,2,1,0:T(8,128)}, u32[]{:S(2)}, u32[]{:S(2)}) collective-permute-start(f32[5,4,16,128]{3,2,1,0:T(8,128)} %get-tuple-element.44), channel_id=1, source_target_pairs={{1,0},{2,1},{3,2},{4,3},{5,4},{6,5},{7,6},{0,7},{9,8},{10,9},{11,1... | collective-permute-start | bytes 491528 | tf_op jit(solution)/shard_map/ppermute | solution.py:483
  36.3 13.2 %all-to-all-start = ((f32[32,5,4,128]{3,2,1,0:T(4,128)}), f32[32,5,4,128]{3,2,1,0:T(4,128)}, u32[]{:S(2)}, u32[]{:S(2)}) async-start(f32[32,5,4,128]{3,2,1,0:T(4,128)} %get-tuple-element.46), calls=%async_computation | async-start | bytes 655360 | tf_op jit(solution)/shard_map/all_to_all | solution.py:547
  49.5 0.9 copy-done.4
  50.4 4.1 %shard_map.61 = (f32[5,8,16,128]{3,2,1,0:T(8,128)S(1)}, f32[2,5,4,16,128]{4,3,2,1,0:T(8,128)S(1)}, f32[3,5,8,16,128]{4,3,2,1,0:T(8,128)S(1)}) custom-call(f32[5,5]{1,0:T(8,128)S(1)} %copy-done.1, f32[8,5,8,16,128]{4,3,2,1,0:T(8,128)} %source_hbm.17, f32[5,8,16,128]{3,2,1,0:T(8,128)S(1)} %bitcast.8, f32[5,4,16,128]{3,2,1,0:T(8,128)S(1)} %copy-done.4, ...), custom_call_target="tpu_custom_call" | custom-call | flops 10752000 | bytes 8519780 | tf_op jit(solution)/shard_map/pallas_call | solution.py:452
  54.6 3.9 %shard_map.62 = f32[5,8,16,128]{3,2,1,0:T(8,128)} custom-call(f32[5,5]{1,0:T(8,128)S(1)} %copy-done.1, f32[3,5,8,16,128]{4,3,2,1,0:T(8,128)S(1)} %get-tuple-element.40.later_ref, f32[5,8,16,128]{3,2,1,0:T(8,128)S(1)} %get-tuple-element.41.middle_ref, f32[2,5,4,16,128]{4,3,2,1,0:T(8,128)S(1)} %get-tuple-element.42.middle_added, ...), custom_call_target="tpu_custom_call" | custom-call | flops 11776000 | bytes 5898340 | tf_op jit(solution)/shard_map/pallas_call | solution.py:452
  58.5 4.4 %collective-permute-start.6 = (f32[5,8,16,128]{3,2,1,0:T(8,128)}, f32[5,8,16,128]{3,2,1,0:T(8,128)}, u32[]{:S(2)}, u32[]{:S(2)}) collective-permute-start(f32[5,8,16,128]{3,2,1,0:T(8,128)} %shard_map.62), channel_id=1, source_target_pairs={{0,8},{8,16},{16,24},{24,32},{32,40},{40,48},{48,56},{56,64},{64,7... | collective-permute-start | bytes 983048 | tf_op jit(solution)/shard_map/ppermute | solution.py:476
  62.9 9.7 %collective-permute-done.6.ended_ref = f32[5,8,16,128]{3,2,1,0:T(8,128)} collective-permute-done((f32[5,8,16,128]{3,2,1,0:T(8,128)}, f32[5,8,16,128]{3,2,1,0:T(8,128)}, u32[]{:S(2)}, u32[]{:S(2)}) %collective-permute-start.6) | collective-permute-done | bytes 327712 | tf_op jit(solution)/shard_map/ppermute | solution.py:476
  72.6 3.0 %shard_map.63 = (f32[5,8,16,128]{3,2,1,0:T(8,128)}, f32[5,8,16,128]{3,2,1,0:T(8,128)S(1)}, f32[5,8,16,128]{3,2,1,0:T(8,128)S(1)}, f32[5,4,16,128]{3,2,1,0:T(8,128)S(1)}, f32[5,4,16,128]{3,2,1,0:T(8,128)S(1)}) custom-call(f32[5,5]{1,0:T(8,128)S(1)} %copy-done.1, s32[1]{0:T(128)} %bitcast.leads_ref, f32[8,5,8,16,128]{4,3,2,1,0:T(8,128)} %source_hbm.17, ...), custom_call_target="tpu_custom_call" | custom-call | flops 7680000 | bytes 7209064 | tf_op jit(solution)/shard_map/pallas_call | solution.py:452
  75.8 3.6 %collective-permute-start.8 = (f32[5,4,16,128]{3,2,1,0:T(8,128)S(1)}, f32[5,4,16,128]{3,2,1,0:T(8,128)S(1)}, u32[]{:S(2)}, u32[]{:S(2)}) collective-permute-start(f32[5,4,16,128]{3,2,1,0:T(8,128)S(1)} %get-tuple-element.49), channel_id=1, source_target_pairs={{1,0},{2,1},{3,2},{4,3},{5,4},{6,5},{7,6},{0,7},{9,8},{10,9},{11,1... | collective-permute-start | bytes 491528 | tf_op jit(solution)/shard_map/ppermute | solution.py:483
  79.4 1.3 shard_map.65
  80.8 3.6 %collective-permute-start.10 = (f32[5,4,16,128]{3,2,1,0:T(8,128)S(1)}, f32[5,4,16,128]{3,2,1,0:T(8,128)S(1)}, u32[]{:S(2)}, u32[]{:S(2)}) collective-permute-start(f32[5,4,16,128]{3,2,1,0:T(8,128)S(1)} %get-tuple-element.54), channel_id=1, source_target_pairs={{1,0},{2,1},{3,2},{4,3},{5,4},{6,5},{7,6},{0,7},{9,8},{10,9},{11,1... | collective-permute-start | bytes 491528 | tf_op jit(solution)/shard_map/ppermute | solution.py:483
  84.4 3.0 %shard_map.64 = (f32[5,8,16,128]{3,2,1,0:T(8,128)S(1)}, f32[2,5,4,16,128]{4,3,2,1,0:T(8,128)S(1)}) custom-call(f32[5,5]{1,0:T(8,128)S(1)} %copy-done.1, f32[8,5,8,16,128]{4,3,2,1,0:T(8,128)} %source_hbm.17, f32[5,8,16,128]{3,2,1,0:T(8,128)S(1)} %get-tuple-element.47.start_ref, f32[5,4,16,128]{3,2,1,0:T(8,128)S(1)} %collective-permute-done.7.low_ref, ...), custom_call_target="tpu_custom_call" | custom-call | flops 10752000 | bytes 7536740 | tf_op jit(solution)/shard_map/pallas_call | solution.py:452
  87.4 3.8 %shard_map.66 = (f32[5,8,16,128]{3,2,1,0:T(8,128)}, f32[32,5,4,128]{3,2,1,0:T(4,128)S(1)}) custom-call(f32[5,5]{1,0:T(8,128)S(1)} %copy-done.1, s32[1]{0:T(128)} %bitcast.leads_ref, f32[8,5,8,16,128]{4,3,2,1,0:T(8,128)} %source_hbm.17, f32[5,8,16,128]{3,2,1,0:T(8,128)S(1)} %get-tuple-element.50.middle_ref, ...), custom_call_target="tpu_custom_call" | custom-call | flops 12800000 | bytes 7864424 | tf_op jit(solution)/shard_map/pallas_call | solution.py:452
  91.2 0.7 copy-done.2
  91.9 25.6 %all_to_all.15.resid_ref = f32[32,5,4,128]{3,2,1,0:T(4,128)S(1)} all-to-all(f32[32,5,4,128]{3,2,1,0:T(4,128)} %copy-done.2), channel_id=1, replica_groups=mesh['tm'=32,'space'=8] {'tm'}, dimensions={0} | all-to-all | bytes 655360 | tf_op jit(solution)/shard_map/all_to_all | solution.py:577
  117.5 2.1 %shard_map.67 = f32[32,5,4,128]{3,2,1,0:T(4,128)} custom-call(f32[5,5]{1,0:T(8,128)S(1)} %copy-done.1, f32[32,5,4,128]{3,2,1,0:T(4,128)} %all-to-all-done.slope_ref, f32[32,5,4,128]{3,2,1,0:T(4,128)S(1)} %all_to_all.15.resid_ref), custom_call_target="tpu_custom_call" | custom-call | flops 4096000 | bytes 983140 | tf_op jit(solution)/shard_map/pallas_call | solution.py:452
  119.6 4.0 %all-to-all-start.2 = ((f32[32,5,4,128]{3,2,1,0:T(4,128)}), f32[32,5,4,128]{3,2,1,0:T(4,128)S(1)}, u32[]{:S(2)}, u32[]{:S(2)}) async-start(f32[32,5,4,128]{3,2,1,0:T(4,128)} %shard_map.67), calls=%async_computation.2 | async-start | bytes 655360 | tf_op jit(solution)/shard_map/all_to_all | solution.py:580
  123.6 4.4 %collective-permute-start.15 = (f32[5,8,16,128]{3,2,1,0:T(8,128)}, f32[5,8,16,128]{3,2,1,0:T(8,128)}, u32[]{:S(2)}, u32[]{:S(2)}) collective-permute-start(f32[5,8,16,128]{3,2,1,0:T(8,128)} %get-tuple-element.67), channel_id=1, source_target_pairs={{0,8},{8,16},{16,24},{24,32},{32,40},{40,48},{48,56},{56,64},{64,7... | collective-permute-start | bytes 983048 | tf_op jit(solution)/shard_map/ppermute | solution.py:476
  128.0 9.7 %all-to-all-done.2.share_ref = f32[32,5,4,128]{3,2,1,0:T(4,128)S(1)} async-done(((f32[32,5,4,128]{3,2,1,0:T(4,128)}), f32[32,5,4,128]{3,2,1,0:T(4,128)S(1)}, u32[]{:S(2)}, u32[]{:S(2)}) %all-to-all-start.2) | async-done | bytes 327712 | tf_op jit(solution)/shard_map/all_to_all | solution.py:580
  137.7 2.7 %shard_map.68 = (f32[5,8,16,128]{3,2,1,0:T(8,128)S(1)}, f32[5,8,16,128]{3,2,1,0:T(8,128)S(1)}, f32[5,4,16,128]{3,2,1,0:T(8,128)S(1)}, f32[5,4,16,128]{3,2,1,0:T(8,128)S(1)}) custom-call(f32[5,5]{1,0:T(8,128)S(1)} %copy-done.1, s32[1]{0:T(128)} %bitcast.leads_ref, f32[5,8,16,128]{3,2,1,0:T(8,128)} %get-tuple-element.45.relaxed_hbm, ...), custom_call_target="tpu_custom_call" | custom-call | flops 7680000 | bytes 6881384 | tf_op jit(solution)/shard_map/pallas_call | solution.py:452
  140.6 4.3 %collective-permute-start.12 = (f32[5,4,16,128]{3,2,1,0:T(8,128)S(1)}, f32[5,4,16,128]{3,2,1,0:T(8,128)S(1)}, u32[]{:S(2)}, u32[]{:S(2)}) collective-permute-start(f32[5,4,16,128]{3,2,1,0:T(8,128)S(1)} %get-tuple-element.60), channel_id=1, source_target_pairs={{1,0},{2,1},{3,2},{4,3},{5,4},{6,5},{7,6},{0,7},{9,8},{10,9},{11,1... | collective-permute-start | bytes 491528 | tf_op jit(solution)/shard_map/ppermute | solution.py:483
  144.8 2.2 %shard_map.69 = (f32[5,3,16,128]{3,2,1,0:T(8,128)S(1)}, f32[5,3,16,128]{3,2,1,0:T(8,128)S(1)}, f32[5,8,16,128]{3,2,1,0:T(8,128)S(1)}) custom-call(f32[5,5]{1,0:T(8,128)S(1)} %copy-done.1, f32[8,5,8,16,128]{4,3,2,1,0:T(8,128)} %source_hbm.17, f32[5,8,16,128]{3,2,1,0:T(8,128)S(1)} %get-tuple-element.56.middle_ref, ...), custom_call_target="tpu_custom_call" | custom-call | flops 4096000 | bytes 6144100 | tf_op jit(solution)/shard_map/pallas_call | solution.py:452
  147.2 3.6 %collective-permute-start.14 = (f32[5,3,16,128]{3,2,1,0:T(8,128)S(1)}, f32[5,3,16,128]{3,2,1,0:T(8,128)S(1)}, u32[]{:S(2)}, u32[]{:S(2)}) collective-permute-start(f32[5,3,16,128]{3,2,1,0:T(8,128)S(1)} %get-tuple-element.66), channel_id=1, source_target_pairs={{1,0},{2,1},{3,2},{4,3},{5,4},{6,5},{7,6},{0,7},{9,8},{10,9},{11,1... | collective-permute-start | bytes 368648 | tf_op jit(solution)/shard_map/ppermute | solution.py:483
  150.7 1.8 %fusion = f32[1,5,8,16,128]{4,3,2,1,0:T(8,128)} fusion(f32[5,8,16,128]{3,2,1,0:T(8,128)} %collective-permute-done.15, f32[8,5,8,16,128]{4,3,2,1,0:T(8,128)} %source_hbm.17, pred[]{:T(512)S(6)} %eq.3), kind=kLoop, calls=%fused_computation.1 | loop fusion | flops 81920 | bytes 983041 | tf_op jit(solution)/shard_map/broadcast_in_dim | solution.py:620
  152.6 4.0 %shard_map.70 = (f32[8,5,8,16,128]{4,3,2,1,0:T(8,128)}, f32[5,8,16,128]{3,2,1,0:T(8,128)S(1)}, f32[2,5,4,16,128]{4,3,2,1,0:T(8,128)S(1)}, f32[3,5,8,16,128]{4,3,2,1,0:T(8,128)S(1)}) custom-call(f32[5,5]{1,0:T(8,128)S(1)} %copy-done.1, f32[8,5,8,16,128]{4,3,2,1,0:T(8,128)} %source_hbm.17, f32[5,8,16,128]{3,2,1,0:T(8,128)S(1)} %get-tuple-element.57.next_ref, ...), custom_call_target="tpu_custom_call" | custom-call | flops 10752000 | bytes 11468900 | tf_op jit(solution)/shard_map/pallas_call | solution.py:452
  156.6 3.2 %shard_map.71 = f32[8,5,8,16,128]{4,3,2,1,0:T(8,128)} custom-call(f32[5,5]{1,0:T(8,128)S(1)} %copy-done.1, f32[8,5,8,16,128]{4,3,2,1,0:T(8,128)} %get-tuple-element.61.earlier_hbm, f32[3,5,8,16,128]{4,3,2,1,0:T(8,128)S(1)} %get-tuple-element.62.later_ref, f32[5,8,16,128]{3,2,1,0:T(8,128)S(1)} %get-tuple-element.63.middle_ref, ...), custom_call_target="tpu_custom_call", output_to_operand_aliasing={{}: (1, {})} | custom-call | flops 8704000 | bytes 10731620 | tf_op jit(solution)/shard_map/pallas_call | solution.py:452
  (29 shorter events, 1.3 us)
Async XLA Ops:
  0.6 8.7 %copy-start.1 = (f32[5,5]{1,0:T(8,128)S(1)}, f32[5,5]{1,0:T(8,128)}, u32[]{:S(2)}) copy-start(f32[5,5]{1,0:T(8,128)} %mix_ref.25) | copy-start | bytes 304
  0.6 8.7 %copy-start = (f32[1,5,8,16,128]{4,3,2,1,0:T(8,128)S(1)}, f32[1,5,8,16,128]{4,3,2,1,0:T(8,128)}, u32[]{:S(2)}) copy-start(f32[1,5,8,16,128]{4,3,2,1,0:T(8,128)} %guess_ref.3) | copy-start | bytes 983044
  4.3 45.2 %collective-permute-start.2 = (f32[5,12,16,128]{3,2,1,0:T(8,128)}, f32[5,12,16,128]{3,2,1,0:T(8,128)S(1)}, u32[]{:S(2)}, u32[]{:S(2)}) collective-permute-start(f32[5,12,16,128]{3,2,1,0:T(8,128)} %get-tuple-element.38), channel_id=1, source_target_pairs={{0,1},{1,2},{2,3},{3,4},{4,5},{5,6},{6,7},{7,0},{8,9},{9,10},{10,1... | collective-permute-start | bytes 1474568 | tf_op jit(solution)/shard_map/ppermute | solution.py:483
  6.8 42.7 %collective-permute-start.3 = (f32[5,12,16,128]{3,2,1,0:T(8,128)}, f32[5,12,16,128]{3,2,1,0:T(8,128)}, u32[]{:S(2)}, u32[]{:S(2)}) collective-permute-start(f32[5,12,16,128]{3,2,1,0:T(8,128)} %get-tuple-element.39), channel_id=1, source_target_pairs={{1,0},{2,1},{3,2},{4,3},{5,4},{6,5},{7,6},{0,7},{9,8},{10,9},{11,1... | collective-permute-start | bytes 1474568 | tf_op jit(solution)/shard_map/ppermute | solution.py:483
  15.7 17.0 %collective-permute-start = (f32[5,4,16,128]{3,2,1,0:T(8,128)S(1)}, f32[5,4,16,128]{3,2,1,0:T(8,128)S(1)}, u32[]{:S(2)}, u32[]{:S(2)}) collective-permute-start(f32[5,4,16,128]{3,2,1,0:T(8,128)S(1)} %get-tuple-element.35), channel_id=1, source_target_pairs={{0,1},{1,2},{2,3},{3,4},{4,5},{5,6},{6,7},{7,0},{8,9},{9,10},{10,1... | collective-permute-start | bytes 491528 | tf_op jit(solution)/shard_map/ppermute | solution.py:483
  15.8 33.7 %collective-permute-start.1 = (f32[5,4,16,128]{3,2,1,0:T(8,128)}, f32[5,4,16,128]{3,2,1,0:T(8,128)}, u32[]{:S(2)}, u32[]{:S(2)}) collective-permute-start(f32[5,4,16,128]{3,2,1,0:T(8,128)} %get-tuple-element.36), channel_id=1, source_target_pairs={{1,0},{2,1},{3,2},{4,3},{5,4},{6,5},{7,6},{0,7},{9,8},{10,9},{11,1... | collective-permute-start | bytes 491528 | tf_op jit(solution)/shard_map/ppermute | solution.py:483
  19.4 35.2 %collective-permute-start.4 = (f32[5,4,16,128]{3,2,1,0:T(8,128)}, f32[5,4,16,128]{3,2,1,0:T(8,128)}, u32[]{:S(2)}, u32[]{:S(2)}) collective-permute-start(f32[5,4,16,128]{3,2,1,0:T(8,128)} %get-tuple-element.43), channel_id=1, source_target_pairs={{0,1},{1,2},{2,3},{3,4},{4,5},{5,6},{6,7},{7,0},{8,9},{9,10},{10,1... | collective-permute-start | bytes 491528 | tf_op jit(solution)/shard_map/ppermute | solution.py:483
  32.7 0.7 copy-start.3
  33.3 21.2 %collective-permute-start.5 = (f32[5,4,16,128]{3,2,1,0:T(8,128)}, f32[5,4,16,128]{3,2,1,0:T(8,128)}, u32[]{:S(2)}, u32[]{:S(2)}) collective-permute-start(f32[5,4,16,128]{3,2,1,0:T(8,128)} %get-tuple-element.44), channel_id=1, source_target_pairs={{1,0},{2,1},{3,2},{4,3},{5,4},{6,5},{7,6},{0,7},{9,8},{10,9},{11,1... | collective-permute-start | bytes 491528 | tf_op jit(solution)/shard_map/ppermute | solution.py:483
  36.3 55.7 %all-to-all-start = ((f32[32,5,4,128]{3,2,1,0:T(4,128)}), f32[32,5,4,128]{3,2,1,0:T(4,128)}, u32[]{:S(2)}, u32[]{:S(2)}) async-start(f32[32,5,4,128]{3,2,1,0:T(4,128)} %get-tuple-element.46), calls=%async_computation | async-start | bytes 655360 | tf_op jit(solution)/shard_map/all_to_all | solution.py:547
  49.5 0.9 copy-start.4
  58.5 14.1 %collective-permute-start.6 = (f32[5,8,16,128]{3,2,1,0:T(8,128)}, f32[5,8,16,128]{3,2,1,0:T(8,128)}, u32[]{:S(2)}, u32[]{:S(2)}) collective-permute-start(f32[5,8,16,128]{3,2,1,0:T(8,128)} %shard_map.62), channel_id=1, source_target_pairs={{0,8},{8,16},{16,24},{24,32},{32,40},{40,48},{48,56},{56,64},{64,7... | collective-permute-start | bytes 983048 | tf_op jit(solution)/shard_map/ppermute | solution.py:476
  75.5 8.8 %collective-permute-start.7 = (f32[5,4,16,128]{3,2,1,0:T(8,128)S(1)}, f32[5,4,16,128]{3,2,1,0:T(8,128)S(1)}, u32[]{:S(2)}, u32[]{:S(2)}) collective-permute-start(f32[5,4,16,128]{3,2,1,0:T(8,128)S(1)} %get-tuple-element.48), channel_id=1, source_target_pairs={{0,1},{1,2},{2,3},{3,4},{4,5},{5,6},{6,7},{7,0},{8,9},{9,10},{10,1... | collective-permute-start | bytes 491528 | tf_op jit(solution)/shard_map/ppermute | solution.py:483
  75.8 8.6 %collective-permute-start.8 = (f32[5,4,16,128]{3,2,1,0:T(8,128)S(1)}, f32[5,4,16,128]{3,2,1,0:T(8,128)S(1)}, u32[]{:S(2)}, u32[]{:S(2)}) collective-permute-start(f32[5,4,16,128]{3,2,1,0:T(8,128)S(1)} %get-tuple-element.49), channel_id=1, source_target_pairs={{1,0},{2,1},{3,2},{4,3},{5,4},{6,5},{7,6},{0,7},{9,8},{10,9},{11,1... | collective-permute-start | bytes 491528 | tf_op jit(solution)/shard_map/ppermute | solution.py:483
  80.7 6.7 %collective-permute-start.9 = (f32[5,4,16,128]{3,2,1,0:T(8,128)S(1)}, f32[5,4,16,128]{3,2,1,0:T(8,128)S(1)}, u32[]{:S(2)}, u32[]{:S(2)}) collective-permute-start(f32[5,4,16,128]{3,2,1,0:T(8,128)S(1)} %get-tuple-element.53), channel_id=1, source_target_pairs={{0,1},{1,2},{2,3},{3,4},{4,5},{5,6},{6,7},{7,0},{8,9},{9,10},{10,1... | collective-permute-start | bytes 491528 | tf_op jit(solution)/shard_map/ppermute | solution.py:483
  80.8 6.6 %collective-permute-start.10 = (f32[5,4,16,128]{3,2,1,0:T(8,128)S(1)}, f32[5,4,16,128]{3,2,1,0:T(8,128)S(1)}, u32[]{:S(2)}, u32[]{:S(2)}) collective-permute-start(f32[5,4,16,128]{3,2,1,0:T(8,128)S(1)} %get-tuple-element.54), channel_id=1, source_target_pairs={{1,0},{2,1},{3,2},{4,3},{5,4},{6,5},{7,6},{0,7},{9,8},{10,9},{11,1... | collective-permute-start | bytes 491528 | tf_op jit(solution)/shard_map/ppermute | solution.py:483
  91.2 0.7 copy-start.2
  119.6 18.1 %all-to-all-start.2 = ((f32[32,5,4,128]{3,2,1,0:T(4,128)}), f32[32,5,4,128]{3,2,1,0:T(4,128)S(1)}, u32[]{:S(2)}, u32[]{:S(2)}) async-start(f32[32,5,4,128]{3,2,1,0:T(4,128)} %shard_map.67), calls=%async_computation.2 | async-start | bytes 655360 | tf_op jit(solution)/shard_map/all_to_all | solution.py:580
  123.6 27.1 %collective-permute-start.15 = (f32[5,8,16,128]{3,2,1,0:T(8,128)}, f32[5,8,16,128]{3,2,1,0:T(8,128)}, u32[]{:S(2)}, u32[]{:S(2)}) collective-permute-start(f32[5,8,16,128]{3,2,1,0:T(8,128)} %get-tuple-element.67), channel_id=1, source_target_pairs={{0,8},{8,16},{16,24},{24,32},{32,40},{40,48},{48,56},{56,64},{64,7... | collective-permute-start | bytes 983048 | tf_op jit(solution)/shard_map/ppermute | solution.py:476
  140.5 12.1 %collective-permute-start.11 = (f32[5,4,16,128]{3,2,1,0:T(8,128)S(1)}, f32[5,4,16,128]{3,2,1,0:T(8,128)S(1)}, u32[]{:S(2)}, u32[]{:S(2)}) collective-permute-start(f32[5,4,16,128]{3,2,1,0:T(8,128)S(1)} %get-tuple-element.59), channel_id=1, source_target_pairs={{0,1},{1,2},{2,3},{3,4},{4,5},{5,6},{6,7},{7,0},{8,9},{9,10},{10,1... | collective-permute-start | bytes 491528 | tf_op jit(solution)/shard_map/ppermute | solution.py:483
  140.6 12.0 %collective-permute-start.12 = (f32[5,4,16,128]{3,2,1,0:T(8,128)S(1)}, f32[5,4,16,128]{3,2,1,0:T(8,128)S(1)}, u32[]{:S(2)}, u32[]{:S(2)}) collective-permute-start(f32[5,4,16,128]{3,2,1,0:T(8,128)S(1)} %get-tuple-element.60), channel_id=1, source_target_pairs={{1,0},{2,1},{3,2},{4,3},{5,4},{6,5},{7,6},{0,7},{9,8},{10,9},{11,1... | collective-permute-start | bytes 491528 | tf_op jit(solution)/shard_map/ppermute | solution.py:483
  147.1 9.5 %collective-permute-start.13 = (f32[5,3,16,128]{3,2,1,0:T(8,128)S(1)}, f32[5,3,16,128]{3,2,1,0:T(8,128)S(1)}, u32[]{:S(2)}, u32[]{:S(2)}) collective-permute-start(f32[5,3,16,128]{3,2,1,0:T(8,128)S(1)} %get-tuple-element.65), channel_id=1, source_target_pairs={{0,1},{1,2},{2,3},{3,4},{4,5},{5,6},{6,7},{7,0},{8,9},{9,10},{10,1... | collective-permute-start | bytes 368648 | tf_op jit(solution)/shard_map/ppermute | solution.py:483
  147.2 9.4 %collective-permute-start.14 = (f32[5,3,16,128]{3,2,1,0:T(8,128)S(1)}, f32[5,3,16,128]{3,2,1,0:T(8,128)S(1)}, u32[]{:S(2)}, u32[]{:S(2)}) collective-permute-start(f32[5,3,16,128]{3,2,1,0:T(8,128)S(1)} %get-tuple-element.66), channel_id=1, source_target_pairs={{1,0},{2,1},{3,2},{4,3},{5,4},{6,5},{7,6},{0,7},{9,8},{10,9},{11,1... | collective-permute-start | bytes 368648 | tf_op jit(solution)/shard_map/ppermute | solution.py:483
